TPU v7x, 256 devices: a whole 4x4x8 slice. The times are simulated.
256 devices in a mesh: dp: 2 (over x_lo), ctx: 128 (over y, z, x_hi, core).
Axes of the slice: x: 4 (x_hi: 2, x_lo: 2; x = x_hi * 2 + x_lo), y: 4, z: 8, core: 2. Of those that a mesh axis runs over, the one named last changes fastest.
Arguments:
- hidden_in: bfloat16 [2, 16384, 2048], P('dp', 'ctx'), may hold values from -6 to 6
- qk_weight: bfloat16 [2048, 256], replicated, may hold values from -0.125 to 0.125
- conv_weight: float32 [3, 256], replicated, may hold values from -3 to 3
- values: bfloat16 [2, 16384, 512], P('dp', 'ctx'), may hold values from -6 to 6
- gate_in: bfloat16 [2, 16384, 512], P('dp', 'ctx'), may hold values from -6 to 6
- cotangent: bfloat16 [2, 16384, 512], P('dp', 'ctx'), may hold values from -6 to 6
Outputs:
- output: bfloat16 [2, 16384, 512], P('dp', 'ctx')
- grad_hidden: bfloat16 [2, 16384, 2048], P('dp', 'ctx')
- grad_values: bfloat16 [2, 16384, 512], P('dp', 'ctx')
- grad_gate: bfloat16 [2, 16384, 512], P('dp', 'ctx')
- grad_qk_weight: bfloat16 [2048, 256], replicated
All inputs are finite; a program needn't handle non-finite values.
Results may differ from a plain program's by a relative error of at most 0.008.
Values may be sent and summed in bfloat16 or wider, within the bound.
No kernel may reach another device: no remote copies, remote signals or barrier semaphores. Data moves between devices by JAX's collectives and lax.ppermute only.
A program may use at most 192 MiB of HBM per device.

v0:
```python
import math

import jax
import jax.numpy as jnp
import numpy as np
from jax import lax
from jax.sharding import PartitionSpec as P

H = 8
F = 16
DV = 64
KCONV = 3


def shifted(array, axis, by):
    length = lax.axis_size(axis)
    pairs = [(i, i + by) for i in range(length) if 0 <= i + by < length]
    return lax.ppermute(array, axis, pairs)


def entering(part, axis, combine, identity):
    place = lax.axis_index(axis)
    gathered = jax.tree.map(lambda a: lax.all_gather(a, axis), part)
    state = jax.tree.map(lambda a, e: jnp.zeros_like(a) + jnp.asarray(e, a.dtype), part, identity)

    def one(hop, state):
        return combine(
            state, jax.tree.map(lambda a: lax.dynamic_index_in_dim(a, hop, 0, False), gathered)
        )

    return lax.fori_loop(0, place, one, state)


def entering_2(array, axis, combine, identity):
    length, here = (lax.axis_size(axis), lax.axis_index(axis))
    everything = jax.tree.map(
        lambda part, kind: lax.all_gather(part.astype(kind), axis),
        array,
        jax.tree.map(lambda a: jnp.bfloat16 if a.dtype == jnp.float32 else a.dtype, array),
    )
    start = jax.tree.map(
        lambda part, zero: jnp.broadcast_to(jnp.asarray(zero, part.dtype), part.shape),
        array,
        identity,
    )

    def hop(k, before):
        at = length - 1 - k
        reached = at > here
        new = combine(
            before, jax.tree.map(lambda part, own: part[at].astype(own.dtype), everything, array)
        )
        return jax.tree.map(lambda a, b: jnp.where(reached, a, b), new, before)

    return lax.fori_loop(0, length, hop, start)


def pair_table(feat_width):
    table = np.zeros((feat_width * feat_width, feat_width * (feat_width + 1) // 2), np.float32)
    column = 0
    for first in range(feat_width):
        for second in range(first, feat_width):
            factor = 1.0 / math.sqrt(feat_width)
            if first == second:
                factor = factor / math.sqrt(2.0)
            table[first * feat_width + second, column] = factor
            column += 1
    return table


def taylor_map(matrix):
    feat_width = matrix.shape[-1]
    outer = (matrix[..., :, None] * matrix[..., None, :]).reshape(
        matrix.shape[:-1] + (feat_width * feat_width,)
    )
    second = jnp.dot(outer, pair_table(feat_width), precision=lax.Precision.HIGHEST)
    ones = jnp.ones(matrix.shape[:-1] + (1,), matrix.dtype)
    return jnp.concatenate([ones, matrix * feat_width ** (-0.25), second], -1)


def add_states(earlier, later):
    return jax.tree.map(jnp.add, earlier, later)


def body(hidden_in, qk_weight, conv_weight, values, gate_in, cotangent):
    highest_precision = lax.Precision.HIGHEST
    tokens = hidden_in[0]
    length = tokens.shape[0]
    half_width = qk_weight.shape[1] // 2
    projected = jnp.dot(tokens, qk_weight, preferred_element_type=jnp.float32).astype(jnp.bfloat16)
    earlier_rows = shifted(projected[length - (KCONV - 1) :], "ctx", 1)
    padded = jnp.concatenate([earlier_rows, projected], 0).astype(jnp.float32)
    mixed = conv_weight[0] * padded[KCONV - 1 : KCONV - 1 + length]
    for offset in range(1, KCONV):
        mixed = (
            mixed + conv_weight[offset] * padded[KCONV - 1 - offset : KCONV - 1 - offset + length]
        )
    queries = mixed[:, :half_width].reshape(length, H, F)
    keys_mat = mixed[:, half_width:].reshape(length, H, F)
    value_matrix = values[0].astype(jnp.float32).reshape(length, H, DV)
    query_feature_rows = taylor_map(queries)
    key_feature_rows = taylor_map(keys_mat)
    scores = jnp.einsum("thf,shf->hts", queries, keys_mat, precision=highest_precision) * F ** (
        -0.5
    )
    rows_idx = lax.broadcasted_iota(jnp.int32, (length, length), 0)
    cols_idx = lax.broadcasted_iota(jnp.int32, (length, length), 1)
    causal = (rows_idx >= cols_idx)[None]
    weights_mat = jnp.where(causal, 1.0 + scores + 0.5 * scores * scores, 0.0)
    local_numerator = jnp.einsum(
        "hts,shd->thd", weights_mat, value_matrix, precision=highest_precision
    )
    denom_local = jnp.sum(weights_mat, 2).T
    own_numerator = jnp.einsum(
        "oxa,oxn->xan", key_feature_rows, value_matrix, precision=highest_precision
    )
    norm_own = jnp.sum(key_feature_rows, 0)
    gate_f = gate_in[0].astype(jnp.float32)
    sigm = jax.nn.sigmoid(gate_f)
    gate_act = gate_f * sigm
    upstream = cotangent[0].astype(jnp.float32)
    grad_attended = (upstream * gate_act).reshape(length, H, DV)
    incoming_numerator, norm_in = entering(
        (own_numerator, norm_own),
        "ctx",
        add_states,
        (jnp.zeros_like(own_numerator), jnp.zeros_like(norm_own)),
    )
    denom = denom_local + jnp.einsum(
        "thm,hm->th", query_feature_rows, norm_in, precision=highest_precision
    )
    numerator_gradient = grad_attended / denom[..., None]
    attended = (
        local_numerator
        + jnp.einsum(
            "jfn,fna->jfa", query_feature_rows, incoming_numerator, precision=highest_precision
        )
    ) / denom[..., None]
    grad_denom = -jnp.sum(grad_attended * attended, -1) / denom
    incoming_numerator_gradient = jnp.einsum(
        "oxa,oxn->xan", query_feature_rows, numerator_gradient, precision=highest_precision
    )
    grad_norm_in = jnp.einsum(
        "thm,th->hm", query_feature_rows, grad_denom, precision=highest_precision
    )
    numerator_following, norm_following = entering_2(
        (incoming_numerator_gradient, grad_norm_in),
        "ctx",
        add_states,
        (jnp.zeros_like(incoming_numerator_gradient), jnp.zeros_like(grad_norm_in)),
    )
    attended_flat = attended.reshape(length, H * DV)
    output = (attended_flat * gate_act).astype(jnp.bfloat16)
    grad_gate = (upstream * attended_flat * sigm * (1.0 + gate_f * (1.0 - sigm))).astype(
        jnp.bfloat16
    )
    grad_weights = (
        jnp.einsum("thd,shd->hts", numerator_gradient, value_matrix, precision=highest_precision)
        + grad_denom.T[:, :, None]
    )
    grad_scores = jnp.where(causal, grad_weights * (1.0 + scores), 0.0) * F ** (-0.5)
    grad_query = jnp.einsum("hts,shf->thf", grad_scores, keys_mat, precision=highest_precision)
    grad_key = jnp.einsum("hts,thf->shf", grad_scores, queries, precision=highest_precision)
    value_gradient_rows = jnp.einsum(
        "hts,thd->shd", weights_mat, numerator_gradient, precision=highest_precision
    )
    value_gradient_rows = value_gradient_rows + jnp.einsum(
        "jfn,fna->jfa", key_feature_rows, numerator_following, precision=highest_precision
    )
    grad_qfeats = (
        jnp.einsum(
            "gpf,pnf->gpn", numerator_gradient, incoming_numerator, precision=highest_precision
        )
        + grad_denom[..., None] * norm_in[None]
    )
    grad_kfeats = (
        jnp.einsum("gpf,pnf->gpn", value_matrix, numerator_following, precision=highest_precision)
        + norm_following[None]
    )
    unused_q, pull_query = jax.vjp(taylor_map, queries)
    unused_k, pull_key = jax.vjp(taylor_map, keys_mat)
    grad_query = grad_query + pull_query(grad_qfeats)[0]
    grad_key = grad_key + pull_key(grad_kfeats)[0]
    grad_values = value_gradient_rows.reshape(length, H * DV).astype(jnp.bfloat16)
    grad_mixed = jnp.concatenate(
        [grad_query.reshape(length, half_width), grad_key.reshape(length, half_width)], 1
    )
    later_rows = shifted(grad_mixed[: KCONV - 1], "ctx", -1)
    extended = jnp.concatenate([grad_mixed, later_rows], 0)
    grad_projected = conv_weight[0] * extended[0:length]
    for offset in range(1, KCONV):
        grad_projected = grad_projected + conv_weight[offset] * extended[offset : offset + length]
    grad_projected = grad_projected.astype(jnp.bfloat16)
    grad_hidden = jnp.dot(grad_projected, qk_weight.T, preferred_element_type=jnp.float32).astype(
        jnp.bfloat16
    )
    local_term = jnp.einsum("tr,tc->rc", tokens, grad_projected, preferred_element_type=jnp.float32)
    grad_qk_weight = lax.psum(local_term, ("dp", "ctx")).astype(jnp.bfloat16)
    return (output[None], grad_hidden[None], grad_values[None], grad_gate[None], grad_qk_weight)


def solution(mesh):
    return jax.shard_map(
        body,
        mesh=mesh,
        in_specs=(
            P("dp", "ctx", None),
            P(),
            P(),
            P("dp", "ctx", None),
            P("dp", "ctx", None),
            P("dp", "ctx", None),
        ),
        out_specs=(
            P("dp", "ctx", None),
            P("dp", "ctx", None),
            P("dp", "ctx", None),
            P("dp", "ctx", None),
            P(),
        ),
        check_vma=False,
    )
```

profile of v0, /device:TPU:1, one launch (start us, length us, event | category | flops | bytes accessed | tf_op | source)
XLA Modules:
  0.0 1275.7 jit_solution(13661112365883972500)
XLA Ops:
  7.2 1.2 copy-done
  8.4 1.3 convolution_convert_fusion.2
  9.8 6.0 collective-permute-start
  16.6 1.0 copy.76
  18.0 1.6 fusion.49
  19.6 1.7 fusion.19
  21.4 1.7 copy.83
  23.1 1.7 copy.84
  26.1 1.8 fusion.22
  28.0 2.4 fusion.50
  30.4 202.8 %all-gather.1 = f32[1024,153]{1,0:T(8,128)} all-gather(f32[8,153]{1,0:T(8,128)S(1)} %fusion.18), channel_id=3, replica_groups=mesh['dp'=2,'ctx'=128] {'ctx'}, dimensions={0}, use_global_device_ids=true | all-gather | bytes 631584 | tf_op jit(solution)/shard_map/all_gather | solution.py:23
  233.2 141.7 %all-gather.7.cloned.1.call-done = f32[1024,153,64]{1,2,0:T(8,128)} async-done(((f32[8,153,64]{1,2,0:T(8,128)}), f32[1024,153,64]{1,2,0:T(8,128)}) %all-gather.7.cloned.1.call-update) | async-done | bytes 40108048 | tf_op jit(solution)/shard_map/all_gather | solution.py:23
  375.0 2.3 while.30
  375.1 1.1 constant_dynamic-slice_fusion.4
  377.3 1.8 fusion.33
  379.1 2.6 convolution_bitcast_fusion.3
  381.6 2.4 multiply_reduce_fusion.4
  384.1 3.3 convolution_convert_fusion.1
  388.2 2.0 fusion.13
  390.2 1.3 multiply_reduce_fusion.3
  391.5 1.6 fusion.5
  393.8 2.3 fusion.46
  396.0 1.1 copy.82
  397.1 472.4 %all-gather.3 = bf16[1024,153]{1,0:T(8,128)(2,1)} all-gather(bf16[8,153]{1,0:T(8,128)(2,1)S(1)} %bitcast.147), channel_id=5, replica_groups=mesh['dp'=2,'ctx'=128] {'ctx'}, dimensions={0}, use_global_device_ids=true | all-gather | bytes 315792 | tf_op jit(solution)/shard_map/all_gather | solution.py:37
  869.6 1.9 multiply_convert_fusion
  871.5 6.1 all-gather.9.cloned.1.call-done
  877.6 286.2 %while.31 = (s32[]{:T(128)}, f32[8,153,64]{2,1,0:T(8,128)S(1)}, f32[8,153]{1,0:T(8,128)S(1)}, s32[]{:T(128)}, bf16[128,8,153,64]{2,3,1,0:T(8,128)(2,1)}, /*index...) while((s32[]{:T(128)}, f32[8,153,64]{2,1,0:T(8,128)S(1)}, ...), condition=%wide.region_8.9_spmd.clone, body=%wide.region_7.8_spmd.clone.sunk | while | flops 318248 | bytes 1422465 | solution.py:55
  877.6 1.0 constant_dynamic-slice_fusion.5
  895.5 1.0 constant_dynamic-slice_fusion.5
  911.1 1.0 constant_dynamic-slice_fusion.5
  949.2 1.0 constant_dynamic-slice_fusion.5
  1002.8 1.0 constant_dynamic-slice_fusion.5
  1025.2 1.0 constant_dynamic-slice_fusion.5
  1029.7 1.0 constant_dynamic-slice_fusion.5
  1054.3 1.0 constant_dynamic-slice_fusion.5
  1056.5 1.0 constant_dynamic-slice_fusion.5
  1125.8 1.0 constant_dynamic-slice_fusion.5
  1163.8 2.3 fusion.17
  1166.2 1.3 fusion.1
  1167.5 2.0 fusion.11
  1169.9 1.8 fusion.10
  1171.8 2.2 collective-permute-start.1
  1174.0 2.2 fusion.8
  1177.0 1.2 collective-permute-done.1
  1178.3 1.5 convolution_bitcast_fusion
  1179.8 1.3 fusion
  1181.0 85.6 %all-reduce.1 = bf16[2048,256]{0,1:T(8,128)(2,1)} all-reduce(f32[2048,256]{0,1:T(8,128)S(1)} %convolution_bitcast_fusion), channel_id=1, replica_groups=mesh['dp'=2,'ctx'=128] {'dp','ctx'}, use_global_device_ids=true, to_apply=%region_11.12 | all-reduce | flops 524288 | bytes 3145728 | tf_op jit(solution)/shard_map/psum | solution.py:198
  1266.6 2.3 copy.99
  (550 shorter events, 280.7 us)
Async XLA Ops:
  7.2 1.2 copy-start
  7.2 367.8 %all-gather.7.cloned.1.call-start = ((), (), s32[]{:S(2)}) async-start(), calls=%async_computation | async-start | bytes 67633152 | tf_op jit(solution)/shard_map/all_gather | solution.py:23
  9.8 7.9 collective-permute-start
  17.6 7.2 copy-start.3
  17.9 357.1 %copy-start.4 = (f32[128,8,16]{0,2,1:T(8,128)}, f32[128,8,16]{0,2,1:T(8,128)S(1)}, u32[]{:S(2)}) copy-start(f32[128,8,16]{0,2,1:T(8,128)S(1)} %broadcast_multiply_fusion.3) | copy-start | bytes 196612
  21.3 856.3 %all-gather.9.cloned.1.call-start = ((), (), s32[]{:S(2)}) async-start(), calls=%async_computation.1 | async-start | bytes 33816576 | tf_op jit(solution)/shard_map/all_gather | solution.py:37
  24.9 350.1 %copy-start.2 = (f32[128,128]{0,1:T(8,128)}, f32[128,128]{0,1:T(8,128)S(1)}, u32[]{:S(2)}) copy-start(f32[128,128]{0,1:T(8,128)S(1)} %copy.74) | copy-start | bytes 196612
  384.1 493.5 %copy-start.1 = (f32[128,8,64]{0,2,1:T(8,128)}, f32[128,8,64]{0,2,1:T(8,128)S(1)}, u32[]{:S(2)}) copy-start(f32[128,8,64]{0,2,1:T(8,128)S(1)} %get-tuple-element.299) | copy-start | bytes 786436
  1171.8 6.4 collective-permute-start.1
Sparse Core Ops, SparseCore 0:
  21.5 353.4 all-gather.6
  387.5 489.9 all-gather.8
where the time goes:
time: 1300 us; the launch traced here: 1280 us
  blocking collectives  761 us (59%)
  local copies, waits for them, and re-layouts  163 us (13%)
  waiting for transfers between devices  149 us (11%)
  other arithmetic  139 us (11%)
  matrix products  38.5 us (3%)
  between operations  14.4 us (1%)
    all_gather x1, blocking collectives, entering_2(): lax.all_gather(part.astype(kind), axis)  472 us
    all_gather x1, blocking collectives, entering(): gathered = jax.tree.map(lambda a: lax.all_gather(a, axis), part)  203 us
    dynamic_slice x256, local copies, waits for them, and re-layouts, hop(): part[at].astype(own.dtype)  151 us
    all_gather x1, waiting for transfers between devices, entering(): gathered = jax.tree.map(lambda a: lax.all_gather(a, axis), part)  142 us
    select_n x256, other arithmetic, hop(): return jax.tree.map(lambda a, b: jnp.where(reached, a, b), new, before)  133 us
    psum x1, blocking collectives, body(): grad_qk_weight = lax.psum(local_term, ('dp', 'ctx')).astype(jnp.bfloat16)  85.6 us
  transfers between devices with their start and end apart: 4, of which 3 were waited for; matrix products, arithmetic and copies ran while one was open for 2% of the time, Pallas kernels for 0%

commit v1 on v0

v1 whole, which is shorter than its diff:
```python
import math

import jax
import jax.numpy as jnp
from jax import lax
from jax.experimental import pallas as pl
from jax.experimental.pallas import tpu as pltpu
from jax.sharding import Mesh, PartitionSpec as P

H = 8
F = 16
DV = 64
KCONV = 3
TOK = 128
ROWS = 256
FEAT = 160
SENT = FEAT + 16
WIDE = 2
f32 = jnp.float32
bf16 = jnp.bfloat16
NN = ((1,), (0,))
NT = ((1,), (1,))
TN = ((0,), (0,))


def mm(a, b, dims):
    return lax.dot_general(a, b, (dims, ((), ())), preferred_element_type=f32)


def halves(x):
    high = x.astype(bf16)
    return high, (x - high.astype(f32)).astype(bf16)


def mm3(a, b, dims):
    (ah, al), (bh, bl) = a, b
    return mm(ah, bh, dims) + (mm(ah, bl, dims) + mm(al, bh, dims))


def feature_scale(d):
    return F**-0.5 * (math.sqrt(0.5) if d == 0 else 1.0)


def up(x, d):
    return x if d == 0 else jnp.concatenate([x[d:], x[:d]], 0)


def features(x):
    rows = [x * F**-0.25]
    for d in range(F // 2):
        rows.append(x * up(x, d) * feature_scale(d))
    half = F // 2
    rows.append(x[:half] * x[half:] * feature_scale(half))
    row = lax.broadcasted_iota(jnp.int32, (8, x.shape[1]), 0)
    rows.append(jnp.where(row == 0, 1.0, 0.0))
    return jnp.concatenate(rows, 0)


def features_back(x, grads):
    total = grads[:F] * F**-0.25
    half = F // 2
    for d in range(half):
        part = grads[F * (d + 1) : F * (d + 2)] * feature_scale(d)
        total = total + part * up(x, d) + up(part * x, (F - d) % F)
    part = grads[F * (half + 1) : F * (half + 1) + half] * feature_scale(half)
    return total + jnp.concatenate([part * x[half:], part * x[:half]], 0)


def pack_state(state):
    high, low = halves(state)
    high, low = high.astype(f32), low.astype(f32)
    lane = lax.broadcasted_iota(jnp.int32, (FEAT, 2 * DV), 1)
    main = jnp.where(lane < DV, high, pltpu.roll(low, DV, 1))
    small = lane[:16]
    sums = jnp.zeros((16, 2 * DV), f32)
    for i in range(FEAT // 16):
        sums = jnp.where(small == i, high[16 * i : 16 * i + 16, DV : DV + 1], sums)
        sums = jnp.where(small == i + 16, low[16 * i : 16 * i + 16, DV : DV + 1], sums)
    return jnp.concatenate([main, sums], 0).astype(bf16)


def unpack_state(total):
    main = total[:FEAT]
    main = main + pltpu.roll(main, DV, 1)
    sums = total[FEAT:]
    sums = sums + pltpu.roll(sums, 2 * DV - 16, 1)
    column = jnp.concatenate([sums[:, i : i + 1] for i in range(FEAT // 16)], 0)
    lane = lax.broadcasted_iota(jnp.int32, (FEAT, 2 * DV), 1)
    return jnp.where(lane < DV, main, jnp.where(lane == DV, column, 0.0))


def wide_values(values):
    row = lax.broadcasted_iota(jnp.int32, (DV, values.shape[1]), 0)
    return jnp.concatenate([values, jnp.where(row == 0, 1.0, 0.0).astype(bf16)], 0)


def rows_of(ref, chunk, start, size):
    return jnp.concatenate(
        [ref[WIDE * chunk + i, start : start + size] for i in range(WIDE)], 1
    )


def pack_kernel(projected, halo, conv, values, gate, cot, out):
    now = projected[...].astype(f32)
    before = halo[...].astype(f32)
    mixed = (
        conv[0:1] * now
        + conv[1:2] * jnp.concatenate([before[1:2], now[:-1]], 0)
        + conv[2:3] * jnp.concatenate([before, now[:-2]], 0)
    )
    high, low = halves(mixed.T)
    v, g, c = values[...].T, gate[...].T, cot[...].T
    width = H * F
    for h in range(H):
        q, k = slice(F * h, F * (h + 1)), slice(width + F * h, width + F * (h + 1))
        out[h, 0:16] = high[q]
        out[h, 16:32] = high[k]
        out[h, 32:48] = low[q]
        out[h, 48:64] = low[k]
        cols = slice(DV * h, DV * (h + 1))
        out[h, 64:128] = v[cols]
        out[h, 128:192] = g[cols]
        out[h, 192:256] = c[cols]


def state_kernel(data, out):
    total = jnp.zeros((FEAT, 2 * DV), f32)
    for c in range(H // WIDE):
        key = rows_of(data, c, 16, 16).astype(f32) + rows_of(data, c, 48, 16).astype(f32)
        high, low = halves(features(key))
        v = wide_values(rows_of(data, c, 64, DV))
        total = total + (mm(high, v, NT) + mm(low, v, NT))
    out[...] = pack_state(total)


def main_kernel(place, data, states, out, gq, gk, gv, parts, sent):
    here = place[0]
    length = TOK * WIDE
    total = jnp.zeros((SENT, 2 * DV), f32)
    for b in range(states.shape[0]):
        total = total + states[b].astype(f32) * (b < here).astype(f32)
    state = unpack_state(total)
    k_at = lax.broadcasted_iota(jnp.int32, (length, length), 0)
    q_at = lax.broadcasted_iota(jnp.int32, (length, length), 1)
    causal = k_at <= q_at
    whole = jnp.zeros((FEAT, 2 * DV), f32)
    for c in range(H // WIDE):
        qh, kh = rows_of(data, c, 0, 16), rows_of(data, c, 16, 16)
        ql, kl = rows_of(data, c, 32, 16), rows_of(data, c, 48, 16)
        q, k = qh.astype(f32) + ql.astype(f32), kh.astype(f32) + kl.astype(f32)
        v = wide_values(rows_of(data, c, 64, DV))
        g = rows_of(data, c, 128, DV).astype(f32)
        cot = rows_of(data, c, 192, DV).astype(f32)
        scores = mm(
            jnp.concatenate([kh, kh, kl], 0), jnp.concatenate([qh, ql, qh], 0), TN
        ) * F**-0.5
        weights = halves(jnp.where(causal, 1.0 + scores + 0.5 * scores * scores, 0.0))
        q_feat, k_feat = halves(features(q)), halves(features(k))
        split_state = halves(state)
        numer = mm(v, weights[0], NN) + mm(v, weights[1], NN) + mm3(split_state, q_feat, TN)
        inverse = 1.0 / numer[DV : DV + 1]
        attended = numer[:DV] * inverse
        sig = jax.nn.sigmoid(g)
        act = g * sig
        result = (attended * act).astype(bf16)
        g_gate = (cot * attended * sig * (1.0 + g * (1.0 - sig))).astype(bf16)
        g_att = cot * act
        g_num = g_att * inverse
        g_den = -jnp.sum(g_att * attended, 0, keepdims=True) * inverse
        row = lax.broadcasted_iota(jnp.int32, (DV, length), 0)
        grads = halves(jnp.concatenate([g_num, jnp.where(row == 0, g_den, 0.0)], 0))
        g_weights = mm(v, grads[0], TN) + mm(v, grads[1], TN)
        g_scores = halves(jnp.where(causal, g_weights * (1.0 + scores), 0.0) * F**-0.5)
        g_query = mm3((kh, kl), g_scores, NN) + features_back(q, mm3(split_state, grads, NN))
        g_key = mm3((qh, ql), g_scores, NT)
        g_value = mm3((grads[0][:DV], grads[1][:DV]), weights, NT)
        part = mm3(q_feat, grads, NT)
        whole = whole + part
        parts[c] = part
        state = state + (mm(k_feat[0], v, NT) + mm(k_feat[1], v, NT))
        for i in range(WIDE):
            cols = slice(TOK * i, TOK * (i + 1))
            out[WIDE * c + i, 0:DV] = result[:, cols]
            out[WIDE * c + i, DV : 2 * DV] = g_gate[:, cols]
        gq[c] = g_query
        gk[c] = g_key
        gv[c] = g_value
    sent[...] = pack_state(whole)


def back_kernel(place, data, states, done, gq, gk, gv, parts, out):
    here = place[0]
    total = jnp.zeros((SENT, 2 * DV), f32)
    for b in range(states.shape[0]):
        total = total + states[b].astype(f32) * (b > here).astype(f32)
    state = unpack_state(total)
    for c in reversed(range(H // WIDE)):
        k = rows_of(data, c, 16, 16).astype(f32) + rows_of(data, c, 48, 16).astype(f32)
        v = wide_values(rows_of(data, c, 64, DV))
        k_feat = halves(features(k))
        split_state = halves(state)
        g_feat = mm(split_state[0], v, NN) + mm(split_state[1], v, NN)
        g_key = halves(gk[c] + features_back(k, g_feat))
        g_query = halves(gq[c])
        g_value = (gv[c] + mm3(split_state, k_feat, TN)[:DV]).astype(bf16)
        state = state + parts[c]
        for i in range(WIDE):
            cols = slice(TOK * i, TOK * (i + 1))
            b = WIDE * c + i
            out[b, 0 : 2 * DV] = done[b]
            out[b, 128:192] = g_value[:, cols]
            out[b, 192:208] = g_query[0][:, cols]
            out[b, 208:224] = g_key[0][:, cols]
            out[b, 224:240] = g_query[1][:, cols]
            out[b, 240:256] = g_key[1][:, cols]


def unpack_kernel(data, output, g_gate, g_value, g_mixed):
    for target, start in ((output, 0), (g_gate, 64), (g_value, 128)):
        target[...] = jnp.concatenate([data[h, start : start + DV] for h in range(H)], 0).T
    rows = [
        data[h, at : at + F].astype(f32) + data[h, at + 32 : at + 32 + F].astype(f32)
        for at in (192, 208)
        for h in range(H)
    ]
    g_mixed[...] = jnp.concatenate(rows, 0).T


def call(kernel, name, out_shape, *args, scalars=0):
    specs = [pl.BlockSpec(memory_space=pltpu.SMEM)] * scalars
    specs += [pl.BlockSpec(memory_space=pltpu.VMEM)] * (len(args) - scalars)
    outs = jax.tree.map(lambda s: pl.BlockSpec(memory_space=pltpu.VMEM), out_shape)
    return pl.pallas_call(
        kernel, name=name, out_shape=out_shape, in_specs=specs, out_specs=outs
    )(*args)


def shape(dims, kind):
    return jax.ShapeDtypeStruct(dims, kind)


def everyone(x, axis):
    count = lax.axis_size(axis)
    return lax.all_to_all(jnp.broadcast_to(x[None], (count,) + x.shape), axis, 0, 0, tiled=True)


def body(hidden_in, qk_weight, conv_weight, values, gate_in, cotangent):
    tokens = hidden_in[0]
    blocks = lax.axis_size(("s", "g"))
    chunks, width = H // WIDE, TOK * WIDE
    place = lax.axis_index("s").astype(jnp.int32).reshape(1)
    projected = jnp.dot(tokens, qk_weight, preferred_element_type=f32).astype(bf16)
    halo = lax.ppermute(
        projected[TOK - (KCONV - 1) :], ("s", "g"), [(i, i + 1) for i in range(blocks - 1)]
    )
    packed = call(
        pack_kernel,
        "pack",
        shape((H, ROWS, TOK), bf16),
        projected,
        halo,
        conv_weight,
        values[0],
        gate_in[0],
        cotangent[0],
    )
    data = lax.all_to_all(packed, "g", 0, 0, tiled=True)
    own = call(state_kernel, "state", shape((SENT, 2 * DV), bf16), data)
    done, gq, gk, gv, parts, sent = call(
        main_kernel,
        "main",
        (
            shape((H, 2 * DV, TOK), bf16),
            shape((chunks, F, width), f32),
            shape((chunks, F, width), f32),
            shape((chunks, DV, width), f32),
            shape((chunks, FEAT, 2 * DV), f32),
            shape((SENT, 2 * DV), bf16),
        ),
        place,
        data,
        everyone(own, "s"),
        scalars=1,
    )
    back = call(
        back_kernel,
        "back",
        shape((H, ROWS, TOK), bf16),
        place,
        data,
        everyone(sent, "s"),
        done,
        gq,
        gk,
        gv,
        parts,
        scalars=1,
    )
    back = lax.all_to_all(back, "g", 0, 0, tiled=True)
    output, grad_gate, grad_values, grad_mixed = call(
        unpack_kernel,
        "unpack",
        (
            shape((TOK, H * DV), bf16),
            shape((TOK, H * DV), bf16),
            shape((TOK, H * DV), bf16),
            shape((TOK, 2 * H * F), f32),
        ),
        back,
    )
    later = lax.ppermute(
        grad_mixed[: KCONV - 1], ("s", "g"), [(i + 1, i) for i in range(blocks - 1)]
    )
    extended = jnp.concatenate([grad_mixed, later], 0)
    grad_projected = conv_weight[0] * extended[:TOK]
    for j in range(1, KCONV):
        grad_projected = grad_projected + conv_weight[j] * extended[j : j + TOK]
    grad_projected = grad_projected.astype(bf16)
    grad_hidden = jnp.dot(grad_projected, qk_weight.T, preferred_element_type=f32).astype(bf16)
    local_term = jnp.einsum("tr,tc->rc", tokens, grad_projected, preferred_element_type=f32)
    grad_qk_weight = lax.psum(local_term, ("dp", "s", "g")).astype(bf16)
    return output[None], grad_hidden[None], grad_values[None], grad_gate[None], grad_qk_weight


def solution(mesh):
    pairs, blocks = mesh.devices.shape
    fine = Mesh(mesh.devices.reshape(pairs, blocks // H, H), ("dp", "s", "g"))
    split = P("dp", ("s", "g"), None)
    return jax.shard_map(
        body,
        mesh=fine,
        in_specs=(split, P(), P(), split, split, split),
        out_specs=(split, split, split, split, P()),
        check_vma=False,
    )
```

time: 1300 us -> 218 us (0.17); the launches traced: 1280 us -> 217 us
  blocking collectives: 761 us -> 127 us
  local copies, waits for them, and re-layouts: 163 us -> 9.95 us
  other arithmetic: 139 us -> 0.95 us
  waiting for transfers between devices: 149 us -> 30 us
  matrix products: 38.5 us -> 4.12 us
  starting transfers between devices: 8.28 us -> 28.8 us
  Pallas kernels: 0 us -> 15.9 us
  between operations: 14.4 us -> 0.71 us
    all_gather x2 -> x0, blocking collectives: 675 us -> none  [the longest x1 472 us: entering_2(): lax.all_gather(part.astype(kind), axis)]
    dynamic_slice x258 -> x0, local copies, waits for them, and re-layouts: 152 us -> none  [the longest x256 151 us: hop(): part[at].astype(own.dtype)]
    all_gather x2 -> x0, waiting for transfers between devices: 148 us -> none  [the longest x1 142 us: entering(): gathered = jax.tree.map(lambda a: lax.all_gather(a, axis), part)]
    select_n x256 -> x0, other arithmetic: 133 us -> none  [hop(): return jax.tree.map(lambda a, b: jnp.where(reached, a, b), new, before)]
    all_to_all x0 -> x2, blocking collectives: none -> 41.5 us  [the longest x1 25.2 us: everyone(): lax.all_to_all(jnp.broadcast_to(x[None], (count,) + x.shape), axis, 0, 0,...]
    dot_general x21 -> x3, matrix products: 38.5 us -> 4.12 us  [the longest x1 1.49 us: body(): jnp.einsum('tr,tc->rc', tokens, grad_projected, preferred_element_type=f32)]
    all_to_all x0 -> x2, waiting for transfers between devices: none -> 26.9 us  [the longest x1 17.8 us: everyone(): lax.all_to_all(jnp.broadcast_to(x[None], (count,) + x.shape), axis, 0, 0,...]
    all_to_all x0 -> x2, starting transfers between devices: none -> 19.6 us  [the longest x1 11.4 us: everyone(): lax.all_to_all(jnp.broadcast_to(x[None], (count,) + x.shape), axis, 0, 0,...]
  transfers between devices with their start and end apart: 4 -> 4, of which waited for: 3 -> 4; matrix products, arithmetic and copies ran while one was open for 2% -> 0% of each run, Pallas kernels for 0% -> 0%
where the time goes in v1:
time: 218 us; the launch traced here: 217 us
  blocking collectives  127 us (58%)
  waiting for transfers between devices  30 us (14%)
  starting transfers between devices  28.8 us (13%)
  Pallas kernels  15.9 us (7%)
  local copies, waits for them, and re-layouts  9.95 us (5%)
  matrix products  4.12 us (2%)
    psum x1, blocking collectives, body(): grad_qk_weight = lax.psum(local_term, ('dp', 's', 'g')).astype(bf16)  85.5 us
    all_to_all x1, blocking collectives, everyone(): lax.all_to_all(jnp.broadcast_to(x[None], (count,) + x.shape), axis, 0, 0,...  25.2 us
    all_to_all x1, waiting for transfers between devices, everyone(): lax.all_to_all(jnp.broadcast_to(x[None], (count,) + x.shape), axis, 0, 0,...  17.8 us
    all_to_all x1, blocking collectives, body(): data = lax.all_to_all(packed, 'g', 0, 0, tiled=True)  16.2 us
    pallas_call x5, Pallas kernels, call(): pl.pallas_call(kernel, name=name, out_shape=out_shape, in_specs=specs, ou...  15.9 us
    all_to_all x1, starting transfers between devices, everyone(): lax.all_to_all(jnp.broadcast_to(x[None], (count,) + x.shape), axis, 0, 0,...  11.4 us
    all_to_all x1, waiting for transfers between devices, body(): back = lax.all_to_all(back, 'g', 0, 0, tiled=True)  9.08 us
    all_to_all x1, starting transfers between devices, body(): back = lax.all_to_all(back, 'g', 0, 0, tiled=True)  8.23 us
  transfers between devices with their start and end apart: 4, of which 4 were waited for; matrix products, arithmetic and copies ran while one was open for 0% of the time, Pallas kernels for 0%

profile of v1, /device:TPU:1, one launch (start us, length us, event | category | flops | bytes accessed | tf_op | source)
XLA Modules:
  0.0 217.4 jit_solution(10594925575663376261)
XLA Ops:
  0.6 0.0 copy-start
  0.6 1.2 copy-done
  1.9 1.3 convolution_convert_fusion.1.projected
  3.2 0.0 copy-start.3
  3.2 6.0 %collective-permute-start = (bf16[2,256]{1,0:T(2,128)(2,1)S(1)}, bf16[2,256]{1,0:T(2,128)(2,1)S(1)}, u32[]{:S(2)}, u32[]{:S(2)}) collective-permute-start(bf16[2,256]{1,0:T(2,128)(2,1)S(1)} %slice.28), channel_id=1, source_target_pairs={{0,1},{1,2},{2,3},{3,4},{4,5},{5,6},{6,7},{7,8},{8,9},{9,10},{10,1... | collective-permute-start | bytes 3080 | tf_op jit(solution)/shard_map/ppermute | solution.py:253
  9.3 0.7 collective-permute-done.halo
  10.0 0.0 copy-start.5
  10.0 0.0 copy-done.3
  10.0 0.6 copy-done.5
  10.5 2.1 pack.1
  12.7 16.2 %all_to_all.20.data = bf16[8,256,128]{2,1,0:T(8,128)(2,1)} all-to-all(bf16[8,256,128]{2,1,0:T(8,128)(2,1)} %pack.1), channel_id=1, replica_groups=mesh['dp'=2,'s'=16,'g'=8] {'g'}, dimensions={0} | all-to-all | bytes 1048576 | tf_op jit(solution)/shard_map/all_to_all | solution.py:267
  28.9 2.1 state.1
  31.0 1.7 broadcast_in_dim.24
  32.7 11.4 %all-to-all-start.1 = ((bf16[16,176,128]{2,1,0:T(8,128)(2,1)}), bf16[16,176,128]{2,1,0:T(8,128)(2,1)S(1)}, u32[]{:S(2)}, u32[]{:S(2)}) async-start(bf16[16,176,128]{2,1,0:T(8,128)(2,1)} %broadcast_in_dim.24), calls=%async_computation.1 | async-start | bytes 1441792 | tf_op jit(solution)/shard_map/all_to_all | solution.py:244
  44.1 17.8 %all-to-all-done.1.states = bf16[16,176,128]{2,1,0:T(8,128)(2,1)S(1)} async-done(((bf16[16,176,128]{2,1,0:T(8,128)(2,1)}), bf16[16,176,128]{2,1,0:T(8,128)(2,1)S(1)}, u32[]{:S(2)}, u32[]{:S(2)}) %all-to-all-start.1) | async-done | bytes 720928 | tf_op jit(solution)/shard_map/all_to_all | solution.py:244
  62.0 0.0 copy-start.1
  62.0 0.9 copy-done.1
  62.8 6.7 %main.1 = (bf16[8,128,128]{2,1,0:T(8,128)(2,1)}, f32[4,16,256]{2,1,0:T(8,128)}, f32[4,16,256]{2,1,0:T(8,128)}, f32[4,64,256]{2,1,0:T(8,128)}, f32[4,160,128]{2,1,0:T(8,128)}, /*index=5*/bf16[176,128]{1,0:T(8,128)(2,1)}) custom-call(s32[1]{0:T(128)} %bitcast.place, bf16[8,256,128]{2,1,0:T(8,128)(2,1)} %all_to_all.20.data, bf16[16,176,128]{2,1,0:T(8,128)(2,1)} %copy-done.1), custom_call_target="tpu_custom_call" | custom-call | tf_op jit(solution)/shard_map/main/pallas_call | solution.py:233
  69.5 0.9 broadcast_in_dim.25
  70.4 25.2 %all_to_all.21.states = bf16[16,176,128]{2,1,0:T(8,128)(2,1)} all-to-all(bf16[16,176,128]{2,1,0:T(8,128)(2,1)S(1)} %broadcast_in_dim.25), channel_id=1, replica_groups=mesh['dp'=2,'s'=16,'g'=8] {'s'}, dimensions={0} | all-to-all | bytes 1441792 | tf_op jit(solution)/shard_map/all_to_all | solution.py:244
  95.6 0.0 copy-start.4
  95.6 3.1 %back.1 = bf16[8,256,128]{2,1,0:T(8,128)(2,1)} custom-call(s32[1]{0:T(128)} %bitcast.place, bf16[8,256,128]{2,1,0:T(8,128)(2,1)} %all_to_all.20.data, bf16[16,176,128]{2,1,0:T(8,128)(2,1)} %all_to_all.21.states, bf16[8,128,128]{2,1,0:T(8,128)(2,1)} %get-tuple-element.16.done, f32[4,16,256]{2,1,0:T(8,128)} %get-tuple-element.17.gq, ...), custom_call_target="tpu_custom_call" | custom-call | tf_op jit(solution)/shard_map/back/pallas_call | solution.py:233
  98.8 8.2 %all-to-all-start.3 = ((bf16[8,256,128]{2,1,0:T(8,128)(2,1)}), bf16[8,256,128]{2,1,0:T(8,128)(2,1)S(1)}, u32[]{:S(2)}, u32[]{:S(2)}) async-start(bf16[8,256,128]{2,1,0:T(8,128)(2,1)} %back.1), calls=%async_computation.3 | async-start | bytes 1048576 | tf_op jit(solution)/shard_map/all_to_all | solution.py:299
  107.0 0.0 copy-done.4
  107.0 9.1 %all-to-all-done.3.data = bf16[8,256,128]{2,1,0:T(8,128)(2,1)S(1)} async-done(((bf16[8,256,128]{2,1,0:T(8,128)(2,1)}), bf16[8,256,128]{2,1,0:T(8,128)(2,1)S(1)}, u32[]{:S(2)}, u32[]{:S(2)}) %all-to-all-start.3) | async-done | bytes 524320 | tf_op jit(solution)/shard_map/all_to_all | solution.py:299
  116.1 0.0 copy-start.2
  116.1 0.8 copy-done.2
  116.9 1.9 unpack.1
  118.8 0.7 slice.24
  119.5 3.1 %collective-permute-start.1 = (f32[2,256]{1,0:T(2,128)S(1)}, f32[2,256]{1,0:T(2,128)S(1)}, u32[]{:S(2)}, u32[]{:S(2)}) collective-permute-start(f32[2,256]{1,0:T(2,128)S(1)} %slice.24), channel_id=1, source_target_pairs={{1,0},{2,1},{3,2},{4,3},{5,4},{6,5},{7,6},{8,7},{9,8},{10,9},{11,1... | collective-permute-start | bytes 6152 | tf_op jit(solution)/shard_map/ppermute | solution.py:311
  122.6 0.9 constant_dynamic-update-slice_fusion.1
  123.5 2.3 %collective-permute-done.1 = f32[2,256]{1,0:T(2,128)S(1)} collective-permute-done((f32[2,256]{1,0:T(2,128)S(1)}, f32[2,256]{1,0:T(2,128)S(1)}, u32[]{:S(2)}, u32[]{:S(2)}) %collective-permute-start.1) | collective-permute-done | bytes 2080 | tf_op jit(solution)/shard_map/ppermute | solution.py:311
  125.9 1.0 fusion.4
  126.8 1.5 convolution_bitcast_fusion
  128.3 1.3 fusion
  129.6 85.5 %all-reduce.1 = bf16[2048,256]{0,1:T(8,128)(2,1)} all-reduce(f32[2048,256]{0,1:T(8,128)S(1)} %convolution_bitcast_fusion), channel_id=1, replica_groups=mesh['dp'=2,'s'=16,'g'=8] {'dp','s','g'}, use_global_device_ids=true, to_apply=%region_0.0 | all-reduce | flops 524288 | bytes 3145728 | tf_op jit(solution)/shard_map/psum | solution.py:321
  215.1 2.3 %copy.11 = bf16[2048,256]{1,0:T(8,128)(2,1)} copy(bf16[2048,256]{0,1:T(8,128)(2,1)} %all-reduce.1) | data formatting | bytes 2097152
  (3 shorter events, 0.0 us)
Async XLA Ops:
  0.6 1.2 copy-start
  3.2 6.8 %copy-start.3 = (bf16[128,256]{1,0:T(8,128)(2,1)}, bf16[128,256]{1,0:T(8,128)(2,1)S(1)}, u32[]{:S(2)}) copy-start(bf16[128,256]{1,0:T(8,128)(2,1)S(1)} %convolution_convert_fusion.1.projected) | copy-start | bytes 196612
  3.2 6.7 %collective-permute-start = (bf16[2,256]{1,0:T(2,128)(2,1)S(1)}, bf16[2,256]{1,0:T(2,128)(2,1)S(1)}, u32[]{:S(2)}, u32[]{:S(2)}) collective-permute-start(bf16[2,256]{1,0:T(2,128)(2,1)S(1)} %slice.28), channel_id=1, source_target_pairs={{0,1},{1,2},{2,3},{3,4},{4,5},{5,6},{6,7},{7,8},{8,9},{9,10},{10,1... | collective-permute-start | bytes 3080 | tf_op jit(solution)/shard_map/ppermute | solution.py:253
  10.0 0.6 copy-start.5
  32.7 29.3 %all-to-all-start.1 = ((bf16[16,176,128]{2,1,0:T(8,128)(2,1)}), bf16[16,176,128]{2,1,0:T(8,128)(2,1)S(1)}, u32[]{:S(2)}, u32[]{:S(2)}) async-start(bf16[16,176,128]{2,1,0:T(8,128)(2,1)} %broadcast_in_dim.24), calls=%async_computation.1 | async-start | bytes 1441792 | tf_op jit(solution)/shard_map/all_to_all | solution.py:244
  62.0 0.9 copy-start.1
  95.6 11.4 %copy-start.4 = (f32[3,256]{1,0:T(4,128)S(1)}, f32[3,256]{1,0:T(4,128)}, u32[]{:S(2)}) copy-start(f32[3,256]{1,0:T(4,128)} %conv.1) | copy-start | bytes 9220
  98.8 17.3 %all-to-all-start.3 = ((bf16[8,256,128]{2,1,0:T(8,128)(2,1)}), bf16[8,256,128]{2,1,0:T(8,128)(2,1)S(1)}, u32[]{:S(2)}, u32[]{:S(2)}) async-start(bf16[8,256,128]{2,1,0:T(8,128)(2,1)} %back.1), calls=%async_computation.3 | async-start | bytes 1048576 | tf_op jit(solution)/shard_map/all_to_all | solution.py:299
  116.1 0.8 copy-start.2
  119.5 6.4 %collective-permute-start.1 = (f32[2,256]{1,0:T(2,128)S(1)}, f32[2,256]{1,0:T(2,128)S(1)}, u32[]{:S(2)}, u32[]{:S(2)}) collective-permute-start(f32[2,256]{1,0:T(2,128)S(1)} %slice.24), channel_id=1, source_target_pairs={{1,0},{2,1},{3,2},{4,3},{5,4},{6,5},{7,6},{8,7},{9,8},{10,9},{11,1... | collective-permute-start | bytes 6152 | tf_op jit(solution)/shard_map/ppermute | solution.py:311

commit v2 on v1

--- a/solution.py
+++ b/solution.py
@@ -14,7 +14,7 @@
 TOK = 128
 ROWS = 256
 FEAT = 160
-SENT = FEAT + 16
+SENT = FEAT // 2 + 16
 WIDE = 2
 f32 = jnp.float32
 bf16 = jnp.bfloat16
@@ -67,10 +67,11 @@
 
 
 def pack_state(state):
+    half = FEAT // 2
+    lane = lax.broadcasted_iota(jnp.int32, (half, 2 * DV), 1)
+    main = jnp.where(lane < DV, state[:half], pltpu.roll(state[half:], DV, 1))
     high, low = halves(state)
     high, low = high.astype(f32), low.astype(f32)
-    lane = lax.broadcasted_iota(jnp.int32, (FEAT, 2 * DV), 1)
-    main = jnp.where(lane < DV, high, pltpu.roll(low, DV, 1))
     small = lane[:16]
     sums = jnp.zeros((16, 2 * DV), f32)
     for i in range(FEAT // 16):
@@ -80,15 +81,21 @@
 
 
 def unpack_state(total):
-    main = total[:FEAT]
-    main = main + pltpu.roll(main, DV, 1)
-    sums = total[FEAT:]
+    half = FEAT // 2
+    main = total[:half]
+    main = jnp.concatenate([main, pltpu.roll(main, DV, 1)], 0)
+    sums = total[half:]
     sums = sums + pltpu.roll(sums, 2 * DV - 16, 1)
     column = jnp.concatenate([sums[:, i : i + 1] for i in range(FEAT // 16)], 0)
     lane = lax.broadcasted_iota(jnp.int32, (FEAT, 2 * DV), 1)
     return jnp.where(lane < DV, main, jnp.where(lane == DV, column, 0.0))
 
 
+def repeat_into(out, value):
+    for i in range(out.shape[0]):
+        out[i] = value
+
+
 def wide_values(values):
     row = lax.broadcasted_iota(jnp.int32, (DV, values.shape[1]), 0)
     return jnp.concatenate([values, jnp.where(row == 0, 1.0, 0.0).astype(bf16)], 0)
@@ -98,6 +105,20 @@
     return jnp.concatenate(
         [ref[WIDE * chunk + i, start : start + size] for i in range(WIDE)], 1
     )
+
+
+def slice_kernel(tokens, states, out):
+    del states
+    cols = out.shape[2]
+    for h in range(H):
+        out[h] = tokens[:, cols * h : cols * (h + 1)]
+
+
+def sum_kernel(data, out):
+    total = data[0].astype(f32)
+    for i in range(1, data.shape[0]):
+        total = total + data[i].astype(f32)
+    repeat_into(out, total.astype(bf16))
 
 
 def pack_kernel(projected, halo, conv, values, gate, cot, out):
@@ -130,7 +151,7 @@
         high, low = halves(features(key))
         v = wide_values(rows_of(data, c, 64, DV))
         total = total + (mm(high, v, NT) + mm(low, v, NT))
-    out[...] = pack_state(total)
+    repeat_into(out, pack_state(total))
 
 
 def main_kernel(place, data, states, out, gq, gk, gv, parts, sent):
@@ -185,10 +206,10 @@
         gq[c] = g_query
         gk[c] = g_key
         gv[c] = g_value
-    sent[...] = pack_state(whole)
-
-
-def back_kernel(place, data, states, done, gq, gk, gv, parts, out):
+    repeat_into(sent, pack_state(whole))
+
+
+def back_kernel(place, data, states, done, gq, gk, gv, parts, out, mixed):
     here = place[0]
     total = jnp.zeros((SENT, 2 * DV), f32)
     for b in range(states.shape[0]):
@@ -200,38 +221,70 @@
         k_feat = halves(features(k))
         split_state = halves(state)
         g_feat = mm(split_state[0], v, NN) + mm(split_state[1], v, NN)
-        g_key = halves(gk[c] + features_back(k, g_feat))
-        g_query = halves(gq[c])
+        g_key = gk[c] + features_back(k, g_feat)
         g_value = (gv[c] + mm3(split_state, k_feat, TN)[:DV]).astype(bf16)
         state = state + parts[c]
+        cols = slice(TOK * WIDE * c, TOK * WIDE * (c + 1))
+        mixed[0:F, cols] = gq[c]
+        mixed[F : 2 * F, cols] = g_key
         for i in range(WIDE):
-            cols = slice(TOK * i, TOK * (i + 1))
             b = WIDE * c + i
             out[b, 0 : 2 * DV] = done[b]
-            out[b, 128:192] = g_value[:, cols]
-            out[b, 192:208] = g_query[0][:, cols]
-            out[b, 208:224] = g_key[0][:, cols]
-            out[b, 224:240] = g_query[1][:, cols]
-            out[b, 240:256] = g_key[1][:, cols]
-
-
-def unpack_kernel(data, output, g_gate, g_value, g_mixed):
+            out[b, 2 * DV : 3 * DV] = g_value[:, TOK * i : TOK * (i + 1)]
+
+
+def conv_back_kernel(place, mixed, later, conv, out, columns):
+    head = place[0]
+    padded = jnp.concatenate([conv[...], jnp.zeros((8 - KCONV, 2 * H * F), f32)], 0)
+    columns[...] = padded.T
+    at = pl.multiple_of(F * head, F)
+    taps = jnp.concatenate([columns[pl.ds(at, F)], columns[pl.ds(H * F + at, F)]], 0)
+    now, after = mixed[...], later[...]
+    total = (
+        taps[:, 0:1] * now
+        + taps[:, 1:2] * jnp.concatenate([now[:, 1:], after[:, 0:1]], 1)
+        + taps[:, 2:3] * jnp.concatenate([now[:, 2:], after], 1)
+    ).astype(bf16)
+    for i in range(H):
+        for b in range(H):
+            out[i, b] = total[:, TOK * b : TOK * (b + 1)]
+
+
+def weight_kernel(place, grads, tokens, out, own):
+    here = place[0]
+    total = jnp.concatenate(
+        [
+            jnp.concatenate(
+                [grads[h, b, at : at + F] for at in (0, F) for h in range(H)], 0
+            )
+            for b in range(H)
+        ],
+        1,
+    )
+    own[...] = jnp.concatenate(
+        [grads[h, here, at : at + F] for at in (0, F) for h in range(H)], 0
+    )
+    result = lax.dot_general(
+        tokens[...], total, (((0,), (1,)), ((), ())), preferred_element_type=f32
+    ).astype(bf16)
+    count, rows = out.shape[:2]
+    for i in range(count):
+        out[i] = result[rows * i : rows * (i + 1)]
+
+
+def unpack_kernel(data, output, g_gate, g_value):
     for target, start in ((output, 0), (g_gate, 64), (g_value, 128)):
         target[...] = jnp.concatenate([data[h, start : start + DV] for h in range(H)], 0).T
-    rows = [
-        data[h, at : at + F].astype(f32) + data[h, at + 32 : at + 32 + F].astype(f32)
-        for at in (192, 208)
-        for h in range(H)
-    ]
-    g_mixed[...] = jnp.concatenate(rows, 0).T
-
-
-def call(kernel, name, out_shape, *args, scalars=0):
+
+
+def call(kernel, name, out_shape, *args, scalars=0, waits=0, scratch=()):
     specs = [pl.BlockSpec(memory_space=pltpu.SMEM)] * scalars
-    specs += [pl.BlockSpec(memory_space=pltpu.VMEM)] * (len(args) - scalars)
+    specs += [pl.BlockSpec(memory_space=pltpu.VMEM)] * (len(args) - scalars - waits)
+    specs += [pl.BlockSpec(memory_space=pl.ANY)] * waits
     outs = jax.tree.map(lambda s: pl.BlockSpec(memory_space=pltpu.VMEM), out_shape)
     return pl.pallas_call(
-        kernel, name=name, out_shape=out_shape, in_specs=specs, out_specs=outs
+        kernel, name=name, out_shape=out_shape, in_specs=specs, out_specs=outs,
+        scratch_shapes=scratch,
     )(*args)
 
 
@@ -239,16 +292,23 @@
     return jax.ShapeDtypeStruct(dims, kind)
 
 
+def swap(x, axis):
+    return lax.all_to_all(x, axis, 0, 0, tiled=True)
+
+
 def everyone(x, axis):
-    count = lax.axis_size(axis)
-    return lax.all_to_all(jnp.broadcast_to(x[None], (count,) + x.shape), axis, 0, 0, tiled=True)
+    return swap(jnp.broadcast_to(x[None], (lax.axis_size(axis),) + x.shape), axis)
 
 
 def body(hidden_in, qk_weight, conv_weight, values, gate_in, cotangent):
     tokens = hidden_in[0]
-    blocks = lax.axis_size(("s", "g"))
+    supers = lax.axis_size("s")
+    blocks = supers * H
+    others = lax.axis_size(("dp", "s"))
+    model = tokens.shape[1]
     chunks, width = H // WIDE, TOK * WIDE
     place = lax.axis_index("s").astype(jnp.int32).reshape(1)
+    head = lax.axis_index("g").astype(jnp.int32).reshape(1)
     projected = jnp.dot(tokens, qk_weight, preferred_element_type=f32).astype(bf16)
     halo = lax.ppermute(
         projected[TOK - (KCONV - 1) :], ("s", "g"), [(i, i + 1) for i in range(blocks - 1)]
@@ -264,8 +324,20 @@
         gate_in[0],
         cotangent[0],
     )
-    data = lax.all_to_all(packed, "g", 0, 0, tiled=True)
-    own = call(state_kernel, "state", shape((SENT, 2 * DV), bf16), data)
+    data = swap(packed, "g")
+    own = call(state_kernel, "state", shape((supers, SENT, 2 * DV), bf16), data)
+    states = swap(own, "s")
+    columns = swap(
+        call(
+            slice_kernel,
+            "slices",
+            shape((H, TOK, model // H), bf16),
+            tokens,
+            states,
+            waits=1,
+        ),
+        "g",
+    )
     done, gq, gk, gv, parts, sent = call(
         main_kernel,
         "main",
@@ -275,20 +347,21 @@
             shape((chunks, F, width), f32),
             shape((chunks, DV, width), f32),
             shape((chunks, FEAT, 2 * DV), f32),
-            shape((SENT, 2 * DV), bf16),
+            shape((supers, SENT, 2 * DV), bf16),
         ),
         place,
         data,
-        everyone(own, "s"),
+        states,
         scalars=1,
     )
-    back = call(
+    sent, columns = lax.optimization_barrier((sent, columns))
+    back, grad_mixed = call(
         back_kernel,
         "back",
-        shape((H, ROWS, TOK), bf16),
+        (shape((H, 3 * DV, TOK), bf16), shape((2 * F, H * TOK), f32)),
         place,
         data,
-        everyone(sent, "s"),
+        swap(sent, "s"),
         done,
         gq,
         gk,
@@ -296,29 +369,43 @@
         parts,
         scalars=1,
     )
-    back = lax.all_to_all(back, "g", 0, 0, tiled=True)
-    output, grad_gate, grad_values, grad_mixed = call(
+    later = lax.ppermute(
+        grad_mixed[:, : KCONV - 1], "s", [(i + 1, i) for i in range(supers - 1)]
+    )
+    grads = call(
+        conv_back_kernel,
+        "conv_back",
+        shape((H, H, 2 * F, TOK), bf16),
+        head,
+        grad_mixed,
+        later,
+        conv_weight,
+        scalars=1,
+        scratch=(pltpu.VMEM((2 * H * F, 8), f32),),
+    )
+    partial, own_grad = call(
+        weight_kernel,
+        "weight",
+        (shape((others, model // H // others, 2 * H * F), bf16), shape((2 * H * F, TOK), bf16)),
+        head,
+        swap(grads, "g"),
+        columns.reshape(H * TOK, model // H),
+        scalars=1,
+    )
+    summed = call(
+        sum_kernel, "sum", shape(partial.shape, bf16), swap(partial, ("dp", "s"))
+    )
+    slices = swap(summed, ("dp", "s")).reshape(model // H, 2 * H * F)
+    grad_qk_weight = everyone(slices, "g").reshape(model, 2 * H * F)
+    output, grad_gate, grad_values = call(
         unpack_kernel,
         "unpack",
-        (
-            shape((TOK, H * DV), bf16),
-            shape((TOK, H * DV), bf16),
-            shape((TOK, H * DV), bf16),
-            shape((TOK, 2 * H * F), f32),
-        ),
-        back,
-    )
-    later = lax.ppermute(
-        grad_mixed[: KCONV - 1], ("s", "g"), [(i + 1, i) for i in range(blocks - 1)]
-    )
-    extended = jnp.concatenate([grad_mixed, later], 0)
-    grad_projected = conv_weight[0] * extended[:TOK]
-    for j in range(1, KCONV):
-        grad_projected = grad_projected + conv_weight[j] * extended[j : j + TOK]
-    grad_projected = grad_projected.astype(bf16)
-    grad_hidden = jnp.dot(grad_projected, qk_weight.T, preferred_element_type=f32).astype(bf16)
-    local_term = jnp.einsum("tr,tc->rc", tokens, grad_projected, preferred_element_type=f32)
-    grad_qk_weight = lax.psum(local_term, ("dp", "s", "g")).astype(bf16)
+        (shape((TOK, H * DV), bf16),) * 3,
+        swap(back, "g"),
+    )
+    grad_hidden = lax.dot_general(
+        own_grad, qk_weight, (((0,), (1,)), ((), ())), preferred_element_type=f32
+    ).astype(bf16)
     return output[None], grad_hidden[None], grad_values[None], grad_gate[None], grad_qk_weight
 
 

time: 218 us -> 190 us (0.87)
  blocking collectives: 127 us -> 107 us
  Pallas kernels: 15.9 us -> 23.6 us
  waiting for transfers between devices: 30 us -> 24 us
  local copies, waits for them, and re-layouts: 9.95 us -> 5.14 us
  starting transfers between devices: 28.8 us -> 25 us
    psum x1 -> x0, blocking collectives: 85.5 us -> none  [body(): grad_qk_weight = lax.psum(local_term, ('dp', 's', 'g')).astype(bf16)]
    all_to_all x2 -> x6, blocking collectives: 41.5 us -> 107 us  [swap(): return lax.all_to_all(x, axis, 0, 0, tiled=True)]
    all_to_all x2 -> x3, waiting for transfers between devices: 26.9 us -> 19.2 us  [swap(): return lax.all_to_all(x, axis, 0, 0, tiled=True)]
    pallas_call x5 -> x9, Pallas kernels: 15.9 us -> 23.6 us  [call(): pl.pallas_call(kernel, name=name, out_shape=out_shape, in_specs=specs, ou...]
    unnamed x14 -> x15, local copies, waits for them, and re-layouts: 6.62 us -> 3.38 us
    all_to_all x2 -> x3, starting transfers between devices: 19.6 us -> 17.7 us  [swap(): return lax.all_to_all(x, axis, 0, 0, tiled=True)]
  transfers between devices with their start and end apart: 4 -> 5, of which waited for: 4 -> 5; matrix products, arithmetic and copies ran while one was open for 0% -> 1% of each run, Pallas kernels for 0% -> 5%
where the time goes in v2:
time: 190 us; the launch traced here: 188 us
  blocking collectives  107 us (56%)
  starting transfers between devices  25 us (13%)
  waiting for transfers between devices  24 us (13%)
  Pallas kernels  23.6 us (12%)
  local copies, waits for them, and re-layouts  5.14 us (3%)
  matrix products  2.62 us (1%)
    all_to_all x6, blocking collectives, swap(): return lax.all_to_all(x, axis, 0, 0, tiled=True)  107 us
    pallas_call x9, Pallas kernels, call(): pl.pallas_call(kernel, name=name, out_shape=out_shape, in_specs=specs, ou...  23.6 us
    all_to_all x3, waiting for transfers between devices, swap(): return lax.all_to_all(x, axis, 0, 0, tiled=True)  19.2 us
    all_to_all x3, starting transfers between devices, swap(): return lax.all_to_all(x, axis, 0, 0, tiled=True)  17.7 us
    ppermute x1, starting transfers between devices, body(): lax.ppermute(projected[TOK - (KCONV - 1):], ('s', 'g'), [(i, i + 1) for i...  6.03 us
    ppermute x1, waiting for transfers between devices, body(): lax.ppermute(grad_mixed[:, :KCONV - 1], 's', [(i + 1, i) for i in range(s...  4.08 us
  transfers between devices with their start and end apart: 5, of which 5 were waited for; matrix products, arithmetic and copies ran while one was open for 1% of the time, Pallas kernels for 5%

profile of v2, /device:TPU:1, one launch (start us, length us, event | category | flops | bytes accessed | tf_op | source)
XLA Modules:
  0.0 187.9 jit_solution(14800573885376854439)
XLA Ops:
  0.6 0.0 copy-start
  0.6 1.2 copy-done
  1.9 1.3 convolution_convert_fusion.1.projected
  3.2 0.0 copy-start.3
  3.2 6.0 %collective-permute-start = (bf16[2,256]{1,0:T(2,128)(2,1)S(1)}, bf16[2,256]{1,0:T(2,128)(2,1)S(1)}, u32[]{:S(2)}, u32[]{:S(2)}) collective-permute-start(bf16[2,256]{1,0:T(2,128)(2,1)S(1)} %slice.8), channel_id=1, source_target_pairs={{0,1},{1,2},{2,3},{3,4},{4,5},{5,6},{6,7},{7,8},{8,9},{9,10},{10,1... | collective-permute-start | bytes 3080 | tf_op jit(solution)/shard_map/ppermute | solution.py:313
  9.3 0.7 collective-permute-done.halo
  10.0 0.0 copy-start.6
  10.0 0.6 copy-done.6
  10.5 0.0 copy-done.3
  10.5 2.1 %pack.1 = bf16[8,256,128]{2,1,0:T(8,128)(2,1)} custom-call(bf16[128,256]{1,0:T(8,128)(2,1)} %copy-done.3, bf16[2,256]{1,0:T(2,128)(2,1)} %copy-done.6, f32[3,256]{1,0:T(4,128)} %conv.3, bf16[128,512]{1,0:T(8,128)(2,1)} %bitcast.23, bf16[128,512]{1,0:T(8,128)(2,1)} %bitcast.24, bf16[128,512]{1,0:T(8,128)(2,1)} %bitcast.25), custom_call_target="tpu_custom_call" | custom-call | tf_op jit(solution)/shard_map/pack/pallas_call | solution.py:285
  12.7 16.2 %all_to_all.45.data = bf16[8,256,128]{2,1,0:T(8,128)(2,1)} all-to-all(bf16[8,256,128]{2,1,0:T(8,128)(2,1)} %pack.1), channel_id=1, replica_groups=mesh['dp'=2,'s'=16,'g'=8] {'g'}, dimensions={0} | all-to-all | bytes 1048576 | tf_op jit(solution)/shard_map/all_to_all | solution.py:296
  28.9 2.2 %state.1 = bf16[16,96,128]{2,1,0:T(8,128)(2,1)} custom-call(bf16[8,256,128]{2,1,0:T(8,128)(2,1)} %all_to_all.45.data), custom_call_target="tpu_custom_call" | custom-call | tf_op jit(solution)/shard_map/state/pallas_call | solution.py:285
  31.1 25.1 %all_to_all.46.states = bf16[16,96,128]{2,1,0:T(8,128)(2,1)} all-to-all(bf16[16,96,128]{2,1,0:T(8,128)(2,1)} %state.1), channel_id=1, replica_groups=mesh['dp'=2,'s'=16,'g'=8] {'s'}, dimensions={0} | all-to-all | bytes 786432 | tf_op jit(solution)/shard_map/all_to_all | solution.py:296
  56.2 1.9 slices.1
  58.1 6.0 %all-to-all-start.2 = ((bf16[8,128,256]{2,1,0:T(8,128)(2,1)}), bf16[8,128,256]{2,1,0:T(8,128)(2,1)S(1)}, u32[]{:S(2)}, u32[]{:S(2)}) async-start(bf16[8,128,256]{2,1,0:T(8,128)(2,1)} %slices.1), calls=%async_computation.2 | async-start | bytes 1048576 | tf_op jit(solution)/shard_map/all_to_all | solution.py:296
  64.1 6.7 %main.1 = (bf16[8,128,128]{2,1,0:T(8,128)(2,1)}, f32[4,16,256]{2,1,0:T(8,128)}, f32[4,16,256]{2,1,0:T(8,128)}, f32[4,64,256]{2,1,0:T(8,128)}, f32[4,160,128]{2,1,0:T(8,128)}, /*index=5*/bf16[16,96,128]{2,1,0:T(8,128)(2,1)}) custom-call(s32[1]{0:T(128)} %bitcast.place, bf16[8,256,128]{2,1,0:T(8,128)(2,1)} %all_to_all.45.data, ...), custom_call_target="tpu_custom_call" | custom-call | tf_op jit(solution)/shard_map/main/pallas_call | solution.py:285
  70.8 2.4 %all-to-all-done.2 = bf16[8,128,256]{2,1,0:T(8,128)(2,1)S(1)} async-done(((bf16[8,128,256]{2,1,0:T(8,128)(2,1)}), bf16[8,128,256]{2,1,0:T(8,128)(2,1)S(1)}, u32[]{:S(2)}, u32[]{:S(2)}) %all-to-all-start.2) | async-done | bytes 524320 | tf_op jit(solution)/shard_map/all_to_all | solution.py:296
  73.2 0.0 copy-start.1
  73.2 18.0 %all_to_all.47.states = bf16[16,96,128]{2,1,0:T(8,128)(2,1)} all-to-all(bf16[16,96,128]{2,1,0:T(8,128)(2,1)} %get-tuple-element.21), channel_id=1, replica_groups=mesh['dp'=2,'s'=16,'g'=8] {'s'}, dimensions={0} | all-to-all | bytes 786432 | tf_op jit(solution)/shard_map/all_to_all | solution.py:296
  91.2 3.0 %back.1 = (bf16[8,192,128]{2,1,0:T(8,128)(2,1)}, f32[32,1024]{1,0:T(8,128)}) custom-call(s32[1]{0:T(128)} %bitcast.place, bf16[8,256,128]{2,1,0:T(8,128)(2,1)} %all_to_all.45.data, bf16[16,96,128]{2,1,0:T(8,128)(2,1)} %all_to_all.47.states, bf16[8,128,128]{2,1,0:T(8,128)(2,1)} %get-tuple-element.22.done, f32[4,16,256]{2,1,0:T(8,128)} %get-tuple-element.23.gq, ...), custom_call_target="tpu_custom_call" | custom-call | tf_op jit(solution)/shard_map/back/pallas_call | solution.py:285
  94.2 0.0 copy-done.1
  94.2 0.7 slice.7
  94.9 1.3 collective-permute-start.1
  96.2 4.1 %collective-permute-done.1.later = f32[32,2]{1,0:T(8,128)S(1)} collective-permute-done((f32[32,2]{1,0:T(8,128)S(1)}, f32[32,2]{1,0:T(8,128)S(1)}, u32[]{:S(2)}, u32[]{:S(2)}) %collective-permute-start.1) | collective-permute-done | bytes 288 | tf_op jit(solution)/shard_map/ppermute | solution.py:372
  100.3 0.0 copy-start.5
  100.3 0.6 copy-done.5
  100.9 2.0 %conv_back.1 = bf16[8,8,32,128]{3,2,1,0:T(8,128)(2,1)} custom-call(s32[1]{0:T(128)} %bitcast.6.place, f32[32,1024]{1,0:T(8,128)} %get-tuple-element.29.mixed, f32[32,2]{1,0:T(8,128)} %copy-done.5, f32[3,256]{1,0:T(4,128)} %conv.3), custom_call_target="tpu_custom_call" | custom-call | tf_op jit(solution)/shard_map/conv_back/pallas_call | solution.py:285
  103.0 18.7 %all_to_all.48.grads = bf16[8,8,32,128]{3,2,1,0:T(8,128)(2,1)} all-to-all(bf16[8,8,32,128]{3,2,1,0:T(8,128)(2,1)} %conv_back.1), channel_id=1, replica_groups=mesh['dp'=2,'s'=16,'g'=8] {'g'}, dimensions={0} | all-to-all | bytes 1048576 | tf_op jit(solution)/shard_map/all_to_all | solution.py:296
  121.6 2.2 %weight.1 = (bf16[32,8,256]{2,1,0:T(8,128)(2,1)}, bf16[256,128]{1,0:T(8,128)(2,1)}) custom-call(s32[1]{0:T(128)} %bitcast.6.place, bf16[8,8,32,128]{3,2,1,0:T(8,128)(2,1)} %all_to_all.48.grads, bf16[1024,256]{1,0:T(8,128)(2,1)} %bitcast.21), custom_call_target="tpu_custom_call" | custom-call | tf_op jit(solution)/shard_map/weight/pallas_call | solution.py:285
  123.8 15.1 %all_to_all.49.data = bf16[32,8,256]{2,1,0:T(8,128)(2,1)} all-to-all(bf16[32,8,256]{2,1,0:T(8,128)(2,1)} %get-tuple-element.34), channel_id=1, replica_groups=mesh['dp'=2,'s'=16,'g'=8] {'dp','s'}, dimensions={0} | all-to-all | bytes 262144 | tf_op jit(solution)/shard_map/all_to_all | solution.py:296
  138.9 6.1 %all-to-all-start.4 = ((bf16[8,192,128]{2,1,0:T(8,128)(2,1)}), bf16[8,192,128]{2,1,0:T(8,128)(2,1)S(1)}, u32[]{:S(2)}, u32[]{:S(2)}) async-start(bf16[8,192,128]{2,1,0:T(8,128)(2,1)} %get-tuple-element.27), calls=%async_computation.4 | async-start | bytes 786432 | tf_op jit(solution)/shard_map/all_to_all | solution.py:296
  145.1 1.6 sum.1
  146.7 6.3 %all-to-all-done.4.data = bf16[8,192,128]{2,1,0:T(8,128)(2,1)S(1)} async-done(((bf16[8,192,128]{2,1,0:T(8,128)(2,1)}), bf16[8,192,128]{2,1,0:T(8,128)(2,1)S(1)}, u32[]{:S(2)}, u32[]{:S(2)}) %all-to-all-start.4) | async-done | bytes 393248 | tf_op jit(solution)/shard_map/all_to_all | solution.py:296
  153.0 0.0 copy-start.2
  153.0 13.8 %all_to_all.50 = bf16[32,8,256]{2,1,0:T(8,128)(2,1)S(1)} all-to-all(bf16[32,8,256]{2,1,0:T(8,128)(2,1)} %sum.1), channel_id=1, replica_groups=mesh['dp'=2,'s'=16,'g'=8] {'dp','s'}, dimensions={0} | all-to-all | bytes 262144 | tf_op jit(solution)/shard_map/all_to_all | solution.py:296
  166.8 1.0 broadcast_in_dim.24
  167.8 0.0 copy-done.2
  167.8 5.6 %all-to-all-start.8 = ((bf16[8,256,256]{2,1,0:T(8,128)(2,1)}), bf16[8,256,256]{2,1,0:T(8,128)(2,1)S(1)}, u32[]{:S(2)}, u32[]{:S(2)}) async-start(bf16[8,256,256]{2,1,0:T(8,128)(2,1)} %broadcast_in_dim.24), calls=%async_computation.8 | async-start | bytes 2097152 | tf_op jit(solution)/shard_map/all_to_all | solution.py:296
  173.4 0.0 copy-start.4
  173.4 1.9 unpack.1
  175.3 0.0 copy-done.4
  175.3 1.3 fusion
  176.5 10.4 %all-to-all-done.8 = bf16[8,256,256]{2,1,0:T(8,128)(2,1)S(1)} async-done(((bf16[8,256,256]{2,1,0:T(8,128)(2,1)}), bf16[8,256,256]{2,1,0:T(8,128)(2,1)S(1)}, u32[]{:S(2)}, u32[]{:S(2)}) %all-to-all-start.8) | async-done | bytes 1048608 | tf_op jit(solution)/shard_map/all_to_all | solution.py:296
  186.9 1.0 copy.12
  (1 shorter events, 0.0 us)
Async XLA Ops:
  0.6 1.2 copy-start
  3.2 7.3 %copy-start.3 = (bf16[128,256]{1,0:T(8,128)(2,1)}, bf16[128,256]{1,0:T(8,128)(2,1)S(1)}, u32[]{:S(2)}) copy-start(bf16[128,256]{1,0:T(8,128)(2,1)S(1)} %convolution_convert_fusion.1.projected) | copy-start | bytes 196612
  3.2 6.7 %collective-permute-start = (bf16[2,256]{1,0:T(2,128)(2,1)S(1)}, bf16[2,256]{1,0:T(2,128)(2,1)S(1)}, u32[]{:S(2)}, u32[]{:S(2)}) collective-permute-start(bf16[2,256]{1,0:T(2,128)(2,1)S(1)} %slice.8), channel_id=1, source_target_pairs={{0,1},{1,2},{2,3},{3,4},{4,5},{5,6},{6,7},{7,8},{8,9},{9,10},{10,1... | collective-permute-start | bytes 3080 | tf_op jit(solution)/shard_map/ppermute | solution.py:313
  10.0 0.6 copy-start.6
  58.1 15.1 %all-to-all-start.2 = ((bf16[8,128,256]{2,1,0:T(8,128)(2,1)}), bf16[8,128,256]{2,1,0:T(8,128)(2,1)S(1)}, u32[]{:S(2)}, u32[]{:S(2)}) async-start(bf16[8,128,256]{2,1,0:T(8,128)(2,1)} %slices.1), calls=%async_computation.2 | async-start | bytes 1048576 | tf_op jit(solution)/shard_map/all_to_all | solution.py:296
  73.2 21.0 %copy-start.1 = (bf16[8,128,256]{2,1,0:T(8,128)(2,1)}, bf16[8,128,256]{2,1,0:T(8,128)(2,1)S(1)}, u32[]{:S(2)}) copy-start(bf16[8,128,256]{2,1,0:T(8,128)(2,1)S(1)} %all-to-all-done.2) | copy-start | bytes 1572868
  94.9 5.4 %collective-permute-start.1 = (f32[32,2]{1,0:T(8,128)S(1)}, f32[32,2]{1,0:T(8,128)S(1)}, u32[]{:S(2)}, u32[]{:S(2)}) collective-permute-start(f32[32,2]{1,0:T(8,128)S(1)} %slice.7), channel_id=1, source_target_pairs={{8,0},{16,8},{24,16},{32,24},{40,32},{48,40},{56,48},{64,56},{72,6... | collective-permute-start | bytes 776 | tf_op jit(solution)/shard_map/ppermute | solution.py:372
  100.3 0.6 copy-start.5
  138.9 14.1 %all-to-all-start.4 = ((bf16[8,192,128]{2,1,0:T(8,128)(2,1)}), bf16[8,192,128]{2,1,0:T(8,128)(2,1)S(1)}, u32[]{:S(2)}, u32[]{:S(2)}) async-start(bf16[8,192,128]{2,1,0:T(8,128)(2,1)} %get-tuple-element.27), calls=%async_computation.4 | async-start | bytes 786432 | tf_op jit(solution)/shard_map/all_to_all | solution.py:296
  153.0 14.8 %copy-start.2 = (bf16[8,192,128]{2,1,0:T(8,128)(2,1)}, bf16[8,192,128]{2,1,0:T(8,128)(2,1)S(1)}, u32[]{:S(2)}) copy-start(bf16[8,192,128]{2,1,0:T(8,128)(2,1)S(1)} %all-to-all-done.4.data) | copy-start | bytes 1179652
  167.8 19.1 %all-to-all-start.8 = ((bf16[8,256,256]{2,1,0:T(8,128)(2,1)}), bf16[8,256,256]{2,1,0:T(8,128)(2,1)S(1)}, u32[]{:S(2)}, u32[]{:S(2)}) async-start(bf16[8,256,256]{2,1,0:T(8,128)(2,1)} %broadcast_in_dim.24), calls=%async_computation.8 | async-start | bytes 2097152 | tf_op jit(solution)/shard_map/all_to_all | solution.py:296
  173.4 1.9 copy-start.4

commit v3 on v2

--- a/solution.py
+++ b/solution.py
@@ -13,9 +13,12 @@
 KCONV = 3
 TOK = 128
 ROWS = 256
+PAD = 16
+HID = TOK + PAD
 FEAT = 160
 SENT = FEAT // 2 + 16
 WIDE = 2
+FIRST = 2 * F * (H + 1)
 f32 = jnp.float32
 bf16 = jnp.bfloat16
 NN = ((1,), (0,))
@@ -107,13 +110,6 @@
     )
 
 
-def slice_kernel(tokens, states, out):
-    del states
-    cols = out.shape[2]
-    for h in range(H):
-        out[h] = tokens[:, cols * h : cols * (h + 1)]
-
-
 def sum_kernel(data, out):
     total = data[0].astype(f32)
     for i in range(1, data.shape[0]):
@@ -121,9 +117,12 @@
     repeat_into(out, total.astype(bf16))
 
 
-def pack_kernel(projected, halo, conv, values, gate, cot, out):
-    now = projected[...].astype(f32)
-    before = halo[...].astype(f32)
+def pack_kernel(tokens, halo, weight, conv, values, gate, cot, out):
+    x = tokens[...]
+    edge = jnp.concatenate([halo[...], jnp.zeros((PAD - (KCONV - 1), x.shape[1]), bf16)], 0)
+    w = weight[...]
+    now = mm(x, w, NN).astype(bf16).astype(f32)
+    before = mm(edge, w, NN).astype(bf16).astype(f32)[: KCONV - 1]
     mixed = (
         conv[0:1] * now
         + conv[1:2] * jnp.concatenate([before[1:2], now[:-1]], 0)
@@ -142,6 +141,11 @@
         out[h, 64:128] = v[cols]
         out[h, 128:192] = g[cols]
         out[h, 192:256] = c[cols]
+        for i in range(x.shape[1] // H // 128):
+            at = ROWS + HID * i
+            cols = slice(x.shape[1] // H * h + 128 * i, x.shape[1] // H * h + 128 * (i + 1))
+            out[h, at : at + TOK] = x[:, cols]
+            out[h, at + TOK : at + HID] = edge[:, cols]
 
 
 def state_kernel(data, out):
@@ -209,8 +213,14 @@
     repeat_into(sent, pack_state(whole))
 
 
-def back_kernel(place, data, states, done, gq, gk, gv, parts, out, mixed):
-    here = place[0]
+def back_kernel(place, data, states, done, gq, gk, gv, parts, conv, out, columns):
+    here, head = place[0], place[1]
+    padded = jnp.concatenate([conv[...], jnp.zeros((8 - KCONV, 2 * H * F), f32)], 0)
+    columns[...] = padded.T
+    at = pl.multiple_of(F * head, F)
+    taps = jnp.concatenate([columns[pl.ds(at, F)], columns[pl.ds(H * F + at, F)]], 0)
+    after = jnp.zeros((2 * F, 2), f32)
+    length = TOK * WIDE
     total = jnp.zeros((SENT, 2 * DV), f32)
     for b in range(states.shape[0]):
         total = total + states[b].astype(f32) * (b > here).astype(f32)
@@ -224,57 +234,72 @@
         g_key = gk[c] + features_back(k, g_feat)
         g_value = (gv[c] + mm3(split_state, k_feat, TN)[:DV]).astype(bf16)
         state = state + parts[c]
-        cols = slice(TOK * WIDE * c, TOK * WIDE * (c + 1))
-        mixed[0:F, cols] = gq[c]
-        mixed[F : 2 * F, cols] = g_key
+        now = jnp.concatenate([gq[c], g_key], 0)
+        total = (
+            taps[:, 0:1] * now
+            + taps[:, 1:2] * jnp.concatenate([now[:, 1:], after[:, 0:1]], 1)
+            + taps[:, 2:3] * jnp.concatenate([now[:, 2:], after], 1)
+        ).astype(bf16)
+        after = now[:, 0:2]
         for i in range(WIDE):
+            cols = slice(TOK * i, TOK * (i + 1))
             b = WIDE * c + i
-            out[b, 0 : 2 * DV] = done[b]
-            out[b, 2 * DV : 3 * DV] = g_value[:, TOK * i : TOK * (i + 1)]
-
-
-def conv_back_kernel(place, mixed, later, conv, out, columns):
-    head = place[0]
-    padded = jnp.concatenate([conv[...], jnp.zeros((8 - KCONV, 2 * H * F), f32)], 0)
-    columns[...] = padded.T
-    at = pl.multiple_of(F * head, F)
-    taps = jnp.concatenate([columns[pl.ds(at, F)], columns[pl.ds(H * F + at, F)]], 0)
-    now, after = mixed[...], later[...]
-    total = (
-        taps[:, 0:1] * now
-        + taps[:, 1:2] * jnp.concatenate([now[:, 1:], after[:, 0:1]], 1)
-        + taps[:, 2:3] * jnp.concatenate([now[:, 2:], after], 1)
-    ).astype(bf16)
-    for i in range(H):
-        for b in range(H):
-            out[i, b] = total[:, TOK * b : TOK * (b + 1)]
-
-
-def weight_kernel(place, grads, tokens, out, own):
-    here = place[0]
-    total = jnp.concatenate(
+            out[b, FIRST : FIRST + 2 * DV] = done[b]
+            out[b, FIRST + 2 * DV : FIRST + 3 * DV] = g_value[:, cols]
+            for dest in range(H):
+                out[dest, 2 * F * b : 2 * F * (b + 1)] = total[:, cols]
+    edge = jnp.concatenate(
         [
-            jnp.concatenate(
-                [grads[h, b, at : at + F] for at in (0, F) for h in range(H)], 0
-            )
-            for b in range(H)
+            taps[:, 2:3] * after[:, 0:1],
+            taps[:, 1:2] * after[:, 0:1] + taps[:, 2:3] * after[:, 1:2],
+            jnp.zeros((2 * F, TOK - 2), f32),
         ],
         1,
-    )
-    own[...] = jnp.concatenate(
-        [grads[h, here, at : at + F] for at in (0, F) for h in range(H)], 0
-    )
-    result = lax.dot_general(
-        tokens[...], total, (((0,), (1,)), ((), ())), preferred_element_type=f32
     ).astype(bf16)
+    for dest in range(H):
+        out[dest, 2 * F * H : FIRST] = edge
+
+
+def stacked(grads, block):
+    return jnp.concatenate(
+        [
+            grads[h, pl.ds(2 * F * block + at, F)]
+            for at in (0, F)
+            for h in range(H)
+        ],
+        0,
+    )
+
+
+def weight_kernel(place, grads, data, out, own, edge):
+    blocks = [stacked(grads, b) for b in range(H + 1)]
+    own[...] = stacked(grads, place[1])
+    edge[...] = blocks[H]
+    total = jnp.concatenate(blocks[:H], 1)
     count, rows = out.shape[:2]
-    for i in range(count):
-        out[i] = result[rows * i : rows * (i + 1)]
+    parts = count * rows // 128
+    for i in range(parts):
+        at = ROWS + HID * i
+        tokens = jnp.concatenate([data[b, at : at + TOK] for b in range(H)], 0)
+        before = data[0, at + TOK : at + HID]
+        result = (
+            mm(tokens, total.T, TN) + mm(before, blocks[H].T[:PAD], TN)
+        ).astype(bf16)
+        for j in range(count // parts):
+            out[i * (count // parts) + j] = result[rows * j : rows * (j + 1)]
+
+
+def hidden_kernel(place, own, edge, weight, out):
+    last = (place[1] == H - 1).astype(f32)
+    later = pltpu.roll(edge[...].astype(f32), TOK - (KCONV - 1), 1) * last
+    grads = (own[...].astype(f32) + later).astype(bf16)
+    out[...] = mm(grads.T, weight[...], NT).astype(bf16)
 
 
 def unpack_kernel(data, output, g_gate, g_value):
-    for target, start in ((output, 0), (g_gate, 64), (g_value, 128)):
-        target[...] = jnp.concatenate([data[h, start : start + DV] for h in range(H)], 0).T
+    for i, target in enumerate((output, g_gate, g_value)):
+        at = FIRST + DV * i
+        target[...] = jnp.concatenate([data[h, at : at + DV] for h in range(H)], 0).T
 
 
 def call(kernel, name, out_shape, *args, scalars=0, waits=0, scratch=()):
@@ -307,18 +332,17 @@
     others = lax.axis_size(("dp", "s"))
     model = tokens.shape[1]
     chunks, width = H // WIDE, TOK * WIDE
-    place = lax.axis_index("s").astype(jnp.int32).reshape(1)
-    head = lax.axis_index("g").astype(jnp.int32).reshape(1)
-    projected = jnp.dot(tokens, qk_weight, preferred_element_type=f32).astype(bf16)
+    place = jnp.stack([lax.axis_index("s"), lax.axis_index("g")]).astype(jnp.int32)
     halo = lax.ppermute(
-        projected[TOK - (KCONV - 1) :], ("s", "g"), [(i, i + 1) for i in range(blocks - 1)]
+        tokens[TOK - (KCONV - 1) :], ("s", "g"), [(i, i + 1) for i in range(blocks - 1)]
     )
     packed = call(
         pack_kernel,
         "pack",
-        shape((H, ROWS, TOK), bf16),
-        projected,
+        shape((H, ROWS + HID * (model // H // 128), TOK), bf16),
+        tokens,
         halo,
+        qk_weight,
         conv_weight,
         values[0],
         gate_in[0],
@@ -326,18 +350,6 @@
     )
     data = swap(packed, "g")
     own = call(state_kernel, "state", shape((supers, SENT, 2 * DV), bf16), data)
-    states = swap(own, "s")
-    columns = swap(
-        call(
-            slice_kernel,
-            "slices",
-            shape((H, TOK, model // H), bf16),
-            tokens,
-            states,
-            waits=1,
-        ),
-        "g",
-    )
     done, gq, gk, gv, parts, sent = call(
         main_kernel,
         "main",
@@ -351,14 +363,13 @@
         ),
         place,
         data,
-        states,
+        swap(own, "s"),
         scalars=1,
     )
-    sent, columns = lax.optimization_barrier((sent, columns))
-    back, grad_mixed = call(
+    back = call(
         back_kernel,
         "back",
-        (shape((H, 3 * DV, TOK), bf16), shape((2 * F, H * TOK), f32)),
+        shape((H, FIRST + 3 * DV, TOK), bf16),
         place,
         data,
         swap(sent, "s"),
@@ -367,29 +378,22 @@
         gk,
         gv,
         parts,
-        scalars=1,
-    )
-    later = lax.ppermute(
-        grad_mixed[:, : KCONV - 1], "s", [(i + 1, i) for i in range(supers - 1)]
-    )
-    grads = call(
-        conv_back_kernel,
-        "conv_back",
-        shape((H, H, 2 * F, TOK), bf16),
-        head,
-        grad_mixed,
-        later,
         conv_weight,
         scalars=1,
         scratch=(pltpu.VMEM((2 * H * F, 8), f32),),
     )
-    partial, own_grad = call(
+    back = swap(back, "g")
+    partial, own_grad, edge = call(
         weight_kernel,
         "weight",
-        (shape((others, model // H // others, 2 * H * F), bf16), shape((2 * H * F, TOK), bf16)),
-        head,
-        swap(grads, "g"),
-        columns.reshape(H * TOK, model // H),
+        (
+            shape((others, model // H // others, 2 * H * F), bf16),
+            shape((2 * H * F, TOK), bf16),
+            shape((2 * H * F, TOK), bf16),
+        ),
+        place,
+        back,
+        data,
         scalars=1,
     )
     summed = call(
@@ -398,14 +402,19 @@
     slices = swap(summed, ("dp", "s")).reshape(model // H, 2 * H * F)
     grad_qk_weight = everyone(slices, "g").reshape(model, 2 * H * F)
     output, grad_gate, grad_values = call(
-        unpack_kernel,
-        "unpack",
-        (shape((TOK, H * DV), bf16),) * 3,
-        swap(back, "g"),
-    )
-    grad_hidden = lax.dot_general(
-        own_grad, qk_weight, (((0,), (1,)), ((), ())), preferred_element_type=f32
-    ).astype(bf16)
+        unpack_kernel, "unpack", (shape((TOK, H * DV), bf16),) * 3, back
+    )
+    later = lax.ppermute(edge, "s", [(i + 1, i) for i in range(supers - 1)])
+    grad_hidden = call(
+        hidden_kernel,
+        "hidden",
+        shape((TOK, model), bf16),
+        place,
+        own_grad,
+        later,
+        qk_weight,
+        scalars=1,
+    )
     return output[None], grad_hidden[None], grad_values[None], grad_gate[None], grad_qk_weight
 
 

time: 190 us -> 176 us (0.926)
  the two profiles are of different devices: /device:TPU:1 before, /device:TPU:32 now
where the time goes in v3:
time: 176 us; the launch traced here: 175 us
  blocking collectives  91.4 us (52%)
  waiting for transfers between devices  32.4 us (18%)
  Pallas kernels  24.8 us (14%)
  starting transfers between devices  19.9 us (11%)
  local copies, waits for them, and re-layouts  4.76 us (3%)
    all_to_all x5, blocking collectives, swap(): return lax.all_to_all(x, axis, 0, 0, tiled=True)  91.4 us
    pallas_call x8, Pallas kernels, call(): pl.pallas_call(kernel, name=name, out_shape=out_shape, in_specs=specs, ou...  24.8 us
    all_to_all x2, starting transfers between devices, swap(): return lax.all_to_all(x, axis, 0, 0, tiled=True)  16.7 us
    all_to_all x2, waiting for transfers between devices, swap(): return lax.all_to_all(x, axis, 0, 0, tiled=True)  14.3 us
    ppermute x1, waiting for transfers between devices, body(): later = lax.ppermute(edge, 's', [(i + 1, i) for i in range(supers - 1)])  12.7 us
    ppermute x1, waiting for transfers between devices, body(): lax.ppermute(tokens[TOK - (KCONV - 1):], ('s', 'g'), [(i, i + 1) for i in...  5.44 us
  transfers between devices with their start and end apart: 4, of which 3 were waited for; matrix products, arithmetic and copies ran while one was open for 0% of the time, Pallas kernels for 3%

profile of v3, /device:TPU:32, one launch (start us, length us, event | category | flops | bytes accessed | tf_op | source)
XLA Modules:
  0.0 174.6 jit_solution(10624690963713418670)
XLA Ops:
  0.6 0.8 slice_bitcast_fusion
  1.4 1.9 %collective-permute-start = (bf16[2,2048]{1,0:T(2,128)(2,1)S(1)}, bf16[2,2048]{1,0:T(2,128)(2,1)S(1)}, u32[]{:S(2)}, u32[]{:S(2)}) collective-permute-start(bf16[2,2048]{1,0:T(2,128)(2,1)S(1)} %slice_bitcast_fusion), channel_id=1, source_target_pairs={{0,1},{1,2},{2,3},{3,4},{4,5},{5,6},{6,7},{7,8},{8,9},{9,10},{10,1... | collective-permute-start | bytes 24584 | tf_op jit(solution)/shard_map/ppermute | solution.py:336
  3.3 5.4 %collective-permute-done.halo = bf16[2,2048]{1,0:T(2,128)(2,1)S(1)} collective-permute-done((bf16[2,2048]{1,0:T(2,128)(2,1)S(1)}, bf16[2,2048]{1,0:T(2,128)(2,1)S(1)}, u32[]{:S(2)}, u32[]{:S(2)}) %collective-permute-start) | collective-permute-done | bytes 8224 | tf_op jit(solution)/shard_map/ppermute | solution.py:336
  8.8 0.0 copy-start.2
  8.8 0.6 copy-done.2
  9.4 3.0 %pack.1 = bf16[8,544,128]{2,1,0:T(8,128)(2,1)} custom-call(bf16[128,2048]{1,0:T(8,128)(2,1)} %bitcast.15, bf16[2,2048]{1,0:T(2,128)(2,1)} %copy-done.2, bf16[2048,256]{1,0:T(8,128)(2,1)} %weight.5, f32[3,256]{1,0:T(4,128)} %conv.3, bf16[128,512]{1,0:T(8,128)(2,1)} %bitcast.18, bf16[128,512]{1,0:T(8,128)(2,1)} %bitcast.19, bf16[128,512]{1,0:T(8,128)(2,1)} %bitcast.20), custom_call_target="tpu_custom_call" | custom-call | tf_op jit(solution)/shard_map/pack/pallas_call | solution.py:310
  12.4 21.0 %all_to_all.35.data = bf16[8,544,128]{2,1,0:T(8,128)(2,1)} all-to-all(bf16[8,544,128]{2,1,0:T(8,128)(2,1)} %pack.1), channel_id=1, replica_groups=mesh['dp'=2,'s'=16,'g'=8] {'g'}, dimensions={0} | all-to-all | bytes 2228224 | tf_op jit(solution)/shard_map/all_to_all | solution.py:321
  33.5 2.4 %state.1 = bf16[16,96,128]{2,1,0:T(8,128)(2,1)} custom-call(bf16[8,544,128]{2,1,0:T(8,128)(2,1)} %all_to_all.35.data), custom_call_target="tpu_custom_call" | custom-call | tf_op jit(solution)/shard_map/state/pallas_call | solution.py:310
  35.9 11.8 %all-to-all-start.1 = ((bf16[16,96,128]{2,1,0:T(8,128)(2,1)}), bf16[16,96,128]{2,1,0:T(8,128)(2,1)S(1)}, u32[]{:S(2)}, u32[]{:S(2)}) async-start(bf16[16,96,128]{2,1,0:T(8,128)(2,1)} %state.1), calls=%async_computation.1 | async-start | bytes 786432 | tf_op jit(solution)/shard_map/all_to_all | solution.py:321
  47.7 0.6 pad_add_fusion.place
  48.3 14.3 %all-to-all-done.1.states = bf16[16,96,128]{2,1,0:T(8,128)(2,1)S(1)} async-done(((bf16[16,96,128]{2,1,0:T(8,128)(2,1)}), bf16[16,96,128]{2,1,0:T(8,128)(2,1)S(1)}, u32[]{:S(2)}, u32[]{:S(2)}) %all-to-all-start.1) | async-done | bytes 393248 | tf_op jit(solution)/shard_map/all_to_all | solution.py:321
  62.6 0.0 copy-start
  62.6 0.7 copy-done
  63.3 6.8 %main.1 = (bf16[8,128,128]{2,1,0:T(8,128)(2,1)}, f32[4,16,256]{2,1,0:T(8,128)}, f32[4,16,256]{2,1,0:T(8,128)}, f32[4,64,256]{2,1,0:T(8,128)}, f32[4,160,128]{2,1,0:T(8,128)}, /*index=5*/bf16[16,96,128]{2,1,0:T(8,128)(2,1)}) custom-call(s32[2]{0:T(128)} %pad_add_fusion.place, bf16[8,544,128]{2,1,0:T(8,128)(2,1)} %all_to_all.35.data, bf16[16,96,128]{2,1,0:T(8,128)(2,1)} %copy-done), custom_call_target="tpu_custom_call" | custom-call | tf_op jit(solution)/shard_map/main/pallas_call | solution.py:310
  70.2 20.0 %all_to_all.36.states = bf16[16,96,128]{2,1,0:T(8,128)(2,1)} all-to-all(bf16[16,96,128]{2,1,0:T(8,128)(2,1)} %get-tuple-element.17), channel_id=1, replica_groups=mesh['dp'=2,'s'=16,'g'=8] {'s'}, dimensions={0} | all-to-all | bytes 786432 | tf_op jit(solution)/shard_map/all_to_all | solution.py:321
  90.2 3.5 %back.1 = bf16[8,480,128]{2,1,0:T(8,128)(2,1)} custom-call(s32[2]{0:T(128)} %pad_add_fusion.place, bf16[8,544,128]{2,1,0:T(8,128)(2,1)} %all_to_all.35.data, bf16[16,96,128]{2,1,0:T(8,128)(2,1)} %all_to_all.36.states, bf16[8,128,128]{2,1,0:T(8,128)(2,1)} %get-tuple-element.18.done, f32[4,16,256]{2,1,0:T(8,128)} %get-tuple-element.19.gq, ...), custom_call_target="tpu_custom_call" | custom-call | tf_op jit(solution)/shard_map/back/pallas_call | solution.py:310
  93.7 19.9 %all_to_all.37.data.grads = bf16[8,480,128]{2,1,0:T(8,128)(2,1)} all-to-all(bf16[8,480,128]{2,1,0:T(8,128)(2,1)} %back.1), channel_id=1, replica_groups=mesh['dp'=2,'s'=16,'g'=8] {'g'}, dimensions={0} | all-to-all | bytes 1966080 | tf_op jit(solution)/shard_map/all_to_all | solution.py:321
  113.6 2.8 %weight.4 = (bf16[32,8,256]{2,1,0:T(8,128)(2,1)}, bf16[256,128]{1,0:T(8,128)(2,1)}, bf16[256,128]{1,0:T(8,128)(2,1)}) custom-call(s32[2]{0:T(128)} %pad_add_fusion.place, bf16[8,480,128]{2,1,0:T(8,128)(2,1)} %all_to_all.37.data.grads, bf16[8,544,128]{2,1,0:T(8,128)(2,1)} %all_to_all.35.data), custom_call_target="tpu_custom_call" | custom-call | tf_op jit(solution)/shard_map/weight/pallas_call | solution.py:310
  116.4 15.7 %all_to_all.38.data = bf16[32,8,256]{2,1,0:T(8,128)(2,1)} all-to-all(bf16[32,8,256]{2,1,0:T(8,128)(2,1)} %get-tuple-element.28), channel_id=1, replica_groups=mesh['dp'=2,'s'=16,'g'=8] {'dp','s'}, dimensions={0} | all-to-all | bytes 262144 | tf_op jit(solution)/shard_map/all_to_all | solution.py:321
  132.1 1.6 sum.1
  133.7 14.8 %all_to_all.39 = bf16[32,8,256]{2,1,0:T(8,128)(2,1)S(1)} all-to-all(bf16[32,8,256]{2,1,0:T(8,128)(2,1)} %sum.1), channel_id=1, replica_groups=mesh['dp'=2,'s'=16,'g'=8] {'dp','s'}, dimensions={0} | all-to-all | bytes 262144 | tf_op jit(solution)/shard_map/all_to_all | solution.py:321
  148.4 1.0 broadcast_in_dim.24
  149.5 0.0 copy-start.3
  149.5 4.9 %all-to-all-start.6 = ((bf16[8,256,256]{2,1,0:T(8,128)(2,1)}), bf16[8,256,256]{2,1,0:T(8,128)(2,1)S(1)}, u32[]{:S(2)}, u32[]{:S(2)}) async-start(bf16[8,256,256]{2,1,0:T(8,128)(2,1)} %broadcast_in_dim.24), calls=%async_computation.6 | async-start | bytes 2097152 | tf_op jit(solution)/shard_map/all_to_all | solution.py:321
  154.4 0.0 copy-done.3
  154.4 1.3 collective-permute-start.1
  155.7 2.0 %unpack.1 = (bf16[128,512]{1,0:T(8,128)(2,1)}, bf16[128,512]{1,0:T(8,128)(2,1)}, bf16[128,512]{1,0:T(8,128)(2,1)}) custom-call(bf16[8,480,128]{2,1,0:T(8,128)(2,1)} %all_to_all.37.data.grads), custom_call_target="tpu_custom_call" | custom-call | tf_op jit(solution)/shard_map/unpack/pallas_call | solution.py:310
  157.7 12.7 %collective-permute-done.1.edge = bf16[256,128]{1,0:T(8,128)(2,1)S(1)} collective-permute-done((bf16[256,128]{1,0:T(8,128)(2,1)S(1)}, bf16[256,128]{1,0:T(8,128)(2,1)S(1)}, u32[]{:S(2)}, u32[]{:S(2)}) %collective-permute-start.1) | collective-permute-done | bytes 65568 | tf_op jit(solution)/shard_map/ppermute | solution.py:407
  170.4 0.0 copy-start.1
  170.4 0.6 copy-done.1
  171.0 2.6 %hidden.1 = bf16[128,2048]{1,0:T(8,128)(2,1)} custom-call(s32[2]{0:T(128)} %pad_add_fusion.place, bf16[256,128]{1,0:T(8,128)(2,1)} %get-tuple-element.24.own, bf16[256,128]{1,0:T(8,128)(2,1)} %copy-done.1, bf16[2048,256]{1,0:T(8,128)(2,1)} %weight.5), custom_call_target="tpu_custom_call" | custom-call | tf_op jit(solution)/shard_map/hidden/pallas_call | solution.py:310
  173.6 0.0 all-to-all-done.6
  173.6 1.0 copy.12
Async XLA Ops:
  1.4 7.4 %collective-permute-start = (bf16[2,2048]{1,0:T(2,128)(2,1)S(1)}, bf16[2,2048]{1,0:T(2,128)(2,1)S(1)}, u32[]{:S(2)}, u32[]{:S(2)}) collective-permute-start(bf16[2,2048]{1,0:T(2,128)(2,1)S(1)} %slice_bitcast_fusion), channel_id=1, source_target_pairs={{0,1},{1,2},{2,3},{3,4},{4,5},{5,6},{6,7},{7,8},{8,9},{9,10},{10,1... | collective-permute-start | bytes 24584 | tf_op jit(solution)/shard_map/ppermute | solution.py:336
  8.8 0.6 copy-start.2
  35.9 26.7 %all-to-all-start.1 = ((bf16[16,96,128]{2,1,0:T(8,128)(2,1)}), bf16[16,96,128]{2,1,0:T(8,128)(2,1)S(1)}, u32[]{:S(2)}, u32[]{:S(2)}) async-start(bf16[16,96,128]{2,1,0:T(8,128)(2,1)} %state.1), calls=%async_computation.1 | async-start | bytes 786432 | tf_op jit(solution)/shard_map/all_to_all | solution.py:321
  62.6 0.7 copy-start
  149.5 4.9 %copy-start.3 = (bf16[256,128]{1,0:T(8,128)(2,1)S(1)}, bf16[256,128]{1,0:T(8,128)(2,1)}, u32[]{:S(2)}) copy-start(bf16[256,128]{1,0:T(8,128)(2,1)} %get-tuple-element.25) | copy-start | bytes 196612
  149.5 24.2 %all-to-all-start.6 = ((bf16[8,256,256]{2,1,0:T(8,128)(2,1)}), bf16[8,256,256]{2,1,0:T(8,128)(2,1)S(1)}, u32[]{:S(2)}, u32[]{:S(2)}) async-start(bf16[8,256,256]{2,1,0:T(8,128)(2,1)} %broadcast_in_dim.24), calls=%async_computation.6 | async-start | bytes 2097152 | tf_op jit(solution)/shard_map/all_to_all | solution.py:321
  154.4 16.0 %collective-permute-start.1 = (bf16[256,128]{1,0:T(8,128)(2,1)S(1)}, bf16[256,128]{1,0:T(8,128)(2,1)S(1)}, u32[]{:S(2)}, u32[]{:S(2)}) collective-permute-start(bf16[256,128]{1,0:T(8,128)(2,1)S(1)} %copy-done.3), channel_id=1, source_target_pairs={{8,0},{16,8},{24,16},{32,24},{40,32},{48,40},{56,48},{64,56},{72,6... | collective-permute-start | bytes 196616 | tf_op jit(solution)/shard_map/ppermute | solution.py:407
  170.4 0.6 copy-start.1

commit v4 on v3

--- a/solution.py
+++ b/solution.py
@@ -12,13 +12,13 @@
 DV = 64
 KCONV = 3
 TOK = 128
-ROWS = 256
-PAD = 16
-HID = TOK + PAD
+ROWS = 2 * F + 3 * DV
+AT_V, AT_G, AT_C = 2 * F, 2 * F + DV, 2 * F + 2 * DV
 FEAT = 160
 SENT = FEAT // 2 + 16
 WIDE = 2
-FIRST = 2 * F * (H + 1)
+FIRST = 2 * F * H
+SPARE = 32
 f32 = jnp.float32
 bf16 = jnp.bfloat16
 NN = ((1,), (0,))
@@ -69,7 +69,7 @@
     return total + jnp.concatenate([part * x[half:], part * x[:half]], 0)
 
 
-def pack_state(state):
+def pack_state(state, extra):
     half = FEAT // 2
     lane = lax.broadcasted_iota(jnp.int32, (half, 2 * DV), 1)
     main = jnp.where(lane < DV, state[:half], pltpu.roll(state[half:], DV, 1))
@@ -80,6 +80,8 @@
     for i in range(FEAT // 16):
         sums = jnp.where(small == i, high[16 * i : 16 * i + 16, DV : DV + 1], sums)
         sums = jnp.where(small == i + 16, low[16 * i : 16 * i + 16, DV : DV + 1], sums)
+    for i, column in enumerate(extra):
+        sums = jnp.where(small == SPARE + i, column.astype(f32), sums)
     return jnp.concatenate([main, sums], 0).astype(bf16)
 
 
@@ -110,6 +112,44 @@
     )
 
 
+def head_taps(conv, columns, head):
+    padded = jnp.concatenate([conv[...], jnp.zeros((8 - KCONV, 2 * H * F), f32)], 0)
+    columns[...] = padded.T
+    at = pl.multiple_of(F * head, F)
+    return jnp.concatenate([columns[pl.ds(at, F)], columns[pl.ds(H * F + at, F)]], 0)
+
+
+def convolve(now, before, taps):
+    return (
+        taps[:, 0:1] * now
+        + taps[:, 1:2] * jnp.concatenate([before[:, 1:2], now[:, :-1]], 1)
+        + taps[:, 2:3] * jnp.concatenate([before, now[:, :-2]], 1)
+    )
+
+
+def first_tokens(states, taps):
+    rows, lanes = F, 2 * DV
+    lane = lax.broadcasted_iota(jnp.int32, (rows, lanes), 1)
+    raw, vals = jnp.zeros((rows, lanes), f32), jnp.zeros((rows, lanes), f32)
+    for b in range(states.shape[0]):
+        tile = states[b, FEAT // 2 : SENT].astype(f32)
+        here = (lane >= 8 * b) & (lane < 8 * (b + 1))
+        raw = jnp.where(here, pltpu.roll(tile, (8 * b - SPARE) % lanes, 1), raw)
+        vals = jnp.where(here, pltpu.roll(tile, (8 * b - SPARE - 8) % lanes, 1), vals)
+    prev = jnp.where(lane < 8, 0.0, pltpu.roll(raw, 8, 1))
+    one = jnp.where(
+        lane % 4 == 0, pltpu.roll(prev, lanes - 3, 1), pltpu.roll(raw, 1, 1)
+    )
+    two = pltpu.roll(prev, lanes - 2, 1)
+    q, k = (
+        t[:, 0:1] * raw + t[:, 1:2] * one + t[:, 2:3] * two for t in (taps[:F], taps[F:])
+    )
+    v = jnp.concatenate(
+        [vals if j == 0 else pltpu.roll(vals, lanes - 2 * j, 1) for j in range(DV // F)], 0
+    )
+    return q, k, v
+
+
 def sum_kernel(data, out):
     total = data[0].astype(f32)
     for i in range(1, data.shape[0]):
@@ -117,65 +157,88 @@
     repeat_into(out, total.astype(bf16))
 
 
-def pack_kernel(tokens, halo, weight, conv, values, gate, cot, out):
+def pack_kernel(tokens, weight, values, gate, cot, out):
     x = tokens[...]
-    edge = jnp.concatenate([halo[...], jnp.zeros((PAD - (KCONV - 1), x.shape[1]), bf16)], 0)
-    w = weight[...]
-    now = mm(x, w, NN).astype(bf16).astype(f32)
-    before = mm(edge, w, NN).astype(bf16).astype(f32)[: KCONV - 1]
-    mixed = (
-        conv[0:1] * now
-        + conv[1:2] * jnp.concatenate([before[1:2], now[:-1]], 0)
-        + conv[2:3] * jnp.concatenate([before, now[:-2]], 0)
-    )
-    high, low = halves(mixed.T)
+    projected = mm(x, weight[...], NN).T.astype(bf16)
     v, g, c = values[...].T, gate[...].T, cot[...].T
     width = H * F
     for h in range(H):
-        q, k = slice(F * h, F * (h + 1)), slice(width + F * h, width + F * (h + 1))
-        out[h, 0:16] = high[q]
-        out[h, 16:32] = high[k]
-        out[h, 32:48] = low[q]
-        out[h, 48:64] = low[k]
+        out[h, 0:F] = projected[F * h : F * (h + 1)]
+        out[h, F : 2 * F] = projected[width + F * h : width + F * (h + 1)]
         cols = slice(DV * h, DV * (h + 1))
-        out[h, 64:128] = v[cols]
-        out[h, 128:192] = g[cols]
-        out[h, 192:256] = c[cols]
-        for i in range(x.shape[1] // H // 128):
-            at = ROWS + HID * i
-            cols = slice(x.shape[1] // H * h + 128 * i, x.shape[1] // H * h + 128 * (i + 1))
-            out[h, at : at + TOK] = x[:, cols]
-            out[h, at + TOK : at + HID] = edge[:, cols]
-
-
-def state_kernel(data, out):
+        out[h, AT_V : AT_V + DV] = v[cols]
+        out[h, AT_G : AT_G + DV] = g[cols]
+        out[h, AT_C : AT_C + DV] = c[cols]
+        for i in range(x.shape[1] // H // TOK):
+            at = ROWS + TOK * i
+            start = x.shape[1] // H * h + TOK * i
+            out[h, at : at + TOK] = x[:, start : start + TOK]
+
+
+def state_kernel(place, data, conv, out, columns):
+    taps = head_taps(conv, columns, place[1])[F:]
     total = jnp.zeros((FEAT, 2 * DV), f32)
+    before = jnp.zeros((F, 2), f32)
     for c in range(H // WIDE):
-        key = rows_of(data, c, 16, 16).astype(f32) + rows_of(data, c, 48, 16).astype(f32)
-        high, low = halves(features(key))
-        v = wide_values(rows_of(data, c, 64, DV))
+        raw = rows_of(data, c, F, F).astype(f32)
+        feat = features(convolve(raw, before, taps))
+        if c == 0:
+            token = lax.broadcasted_iota(jnp.int32, feat.shape, 1)
+            feat = jnp.where(token < KCONV - 1, 0.0, feat)
+        before = raw[:, -2:]
+        high, low = halves(feat)
+        v = wide_values(rows_of(data, c, AT_V, DV))
         total = total + (mm(high, v, NT) + mm(low, v, NT))
-    repeat_into(out, pack_state(total))
-
-
-def main_kernel(place, data, states, out, gq, gk, gv, parts, sent):
+    first, last = data[0, 0 : 2 * F + DV], data[H - 1, 0 : 2 * F]
+    extra = []
+    for start in (F, 0):
+        rows = slice(start, start + F)
+        extra += [first[rows, 0:1], first[rows, 1:2]]
+        extra += [last[rows, TOK - 2 : TOK - 1], last[rows, TOK - 1 : TOK]]
+    for j in range(DV // F):
+        rows = slice(2 * F + F * j, 2 * F + F * (j + 1))
+        extra += [first[rows, 0:1], first[rows, 1:2]]
+    repeat_into(out, pack_state(total, extra))
+
+
+def main_kernel(place, data, states, conv, out, gq, gk, gv, parts, keys, edges, sent, columns):
     here = place[0]
+    taps = head_taps(conv, columns, place[1])
     length = TOK * WIDE
     total = jnp.zeros((SENT, 2 * DV), f32)
     for b in range(states.shape[0]):
         total = total + states[b].astype(f32) * (b < here).astype(f32)
-    state = unpack_state(total)
+    first_q, first_k, first_v = first_tokens(states, taps)
+    lane = lax.broadcasted_iota(jnp.int32, (FEAT, 2 * DV), 1)
+    earlier = (lane % 8 < KCONV - 1) & (lane < 8 * here)
+    feat = halves(jnp.where(earlier, features(first_k), 0.0))
+    first_values = wide_values(first_v.astype(bf16))
+    state = (
+        unpack_state(total) + mm(feat[0], first_values, NT) + mm(feat[1], first_values, NT)
+    )
+    shift = 2 * DV * 2 - 8 * (here + 1)
+    edges[0:F] = pltpu.roll(first_q, shift - 4, 1)
+    edges[F : 2 * F] = pltpu.roll(first_k, shift, 1)
+    edges[2 * F :] = pltpu.roll(first_v, shift, 1)
+    tile = states[jnp.maximum(here - 1, 0), FEAT // 2 : SENT].astype(f32)
+    tile = tile * (here > 0).astype(f32)
+    before = jnp.concatenate(
+        [tile[:, SPARE + 6 : SPARE + 8], tile[:, SPARE + 2 : SPARE + 4]], 0
+    )
     k_at = lax.broadcasted_iota(jnp.int32, (length, length), 0)
     q_at = lax.broadcasted_iota(jnp.int32, (length, length), 1)
     causal = k_at <= q_at
     whole = jnp.zeros((FEAT, 2 * DV), f32)
     for c in range(H // WIDE):
-        qh, kh = rows_of(data, c, 0, 16), rows_of(data, c, 16, 16)
-        ql, kl = rows_of(data, c, 32, 16), rows_of(data, c, 48, 16)
-        q, k = qh.astype(f32) + ql.astype(f32), kh.astype(f32) + kl.astype(f32)
-        v = wide_values(rows_of(data, c, 64, DV))
-        g = rows_of(data, c, 128, DV).astype(f32)
-        cot = rows_of(data, c, 192, DV).astype(f32)
+        raw = rows_of(data, c, 0, 2 * F).astype(f32)
+        mixed = convolve(raw, before, taps)
+        before = raw[:, -2:]
+        q, k = mixed[:F], mixed[F:]
+        (qh, ql), (kh, kl) = halves(q), halves(k)
+        keys[c] = k
+        v = wide_values(rows_of(data, c, AT_V, DV))
+        g = rows_of(data, c, AT_G, DV).astype(f32)
+        cot = rows_of(data, c, AT_C, DV).astype(f32)
         scores = mm(
             jnp.concatenate([kh, kh, kl], 0), jnp.concatenate([qh, ql, qh], 0), TN
         ) * F**-0.5
@@ -193,10 +256,17 @@
         g_num = g_att * inverse
         g_den = -jnp.sum(g_att * attended, 0, keepdims=True) * inverse
         row = lax.broadcasted_iota(jnp.int32, (DV, length), 0)
-        grads = halves(jnp.concatenate([g_num, jnp.where(row == 0, g_den, 0.0)], 0))
+        wide = jnp.concatenate([g_num, jnp.where(row == 0, g_den, 0.0)], 0)
+        grads = halves(wide)
         g_weights = mm(v, grads[0], TN) + mm(v, grads[1], TN)
         g_scores = halves(jnp.where(causal, g_weights * (1.0 + scores), 0.0) * F**-0.5)
         g_query = mm3((kh, kl), g_scores, NN) + features_back(q, mm3(split_state, grads, NN))
+        if c == 0:
+            extra = [g_query[:, 0:1], g_query[:, 1:2]]
+            for j in range(DV // F + 1):
+                column = wide[F * j : F * (j + 1), 0:1]
+                high = column.astype(bf16)
+                extra += [high, column - high.astype(f32)]
         g_key = mm3((qh, ql), g_scores, NT)
         g_value = mm3((grads[0][:DV], grads[1][:DV]), weights, NT)
         part = mm3(q_feat, grads, NT)
@@ -210,24 +280,42 @@
         gq[c] = g_query
         gk[c] = g_key
         gv[c] = g_value
-    repeat_into(sent, pack_state(whole))
-
-
-def back_kernel(place, data, states, done, gq, gk, gv, parts, conv, out, columns):
-    here, head = place[0], place[1]
-    padded = jnp.concatenate([conv[...], jnp.zeros((8 - KCONV, 2 * H * F), f32)], 0)
-    columns[...] = padded.T
-    at = pl.multiple_of(F * head, F)
-    taps = jnp.concatenate([columns[pl.ds(at, F)], columns[pl.ds(H * F + at, F)]], 0)
-    after = jnp.zeros((2 * F, 2), f32)
-    length = TOK * WIDE
+    repeat_into(sent, pack_state(whole, extra))
+
+
+def back_kernel(
+    place, data, states, done, gq, gk, gv, parts, keys, edges, conv, out, columns
+):
+    here = place[0]
+    taps = head_taps(conv, columns, place[1])
+    count = states.shape[0]
     total = jnp.zeros((SENT, 2 * DV), f32)
-    for b in range(states.shape[0]):
+    for b in range(count):
         total = total + states[b].astype(f32) * (b > here).astype(f32)
     state = unpack_state(total)
+    tile = states[jnp.minimum(here + 1, count - 1), FEAT // 2 : SENT].astype(f32)
+    edge = edges[...]
+    edge_v = wide_values(edge[2 * F :].astype(bf16))
+    split_state = halves(state)
+    column = jnp.concatenate(
+        [
+            tile[:, SPARE + 2 + 2 * j : SPARE + 3 + 2 * j]
+            + tile[:, SPARE + 3 + 2 * j : SPARE + 4 + 2 * j]
+            for j in range(DV // F + 1)
+        ],
+        0,
+    )
+    pair = jnp.sum(column * edge_v[: DV + F].astype(f32), 0, keepdims=True)
+    lane = lax.broadcasted_iota(jnp.int32, (FEAT, 2 * DV), 1)
+    g_feat = mm(split_state[0], edge_v, NN) + mm(split_state[1], edge_v, NN)
+    g_feat = g_feat - jnp.where(lane == 1, features(edge[:F])[:, 0:1] * pair, 0.0)
+    after = jnp.concatenate(
+        [tile[:, SPARE : SPARE + 2], features_back(edge[F : 2 * F], g_feat)[:, 0:2]], 0
+    ) * (here + 1 < count).astype(f32)
+    length = TOK * WIDE
     for c in reversed(range(H // WIDE)):
-        k = rows_of(data, c, 16, 16).astype(f32) + rows_of(data, c, 48, 16).astype(f32)
-        v = wide_values(rows_of(data, c, 64, DV))
+        k = keys[c]
+        v = wide_values(rows_of(data, c, AT_V, DV))
         k_feat = halves(features(k))
         split_state = halves(state)
         g_feat = mm(split_state[0], v, NN) + mm(split_state[1], v, NN)
@@ -248,17 +336,6 @@
             out[b, FIRST + 2 * DV : FIRST + 3 * DV] = g_value[:, cols]
             for dest in range(H):
                 out[dest, 2 * F * b : 2 * F * (b + 1)] = total[:, cols]
-    edge = jnp.concatenate(
-        [
-            taps[:, 2:3] * after[:, 0:1],
-            taps[:, 1:2] * after[:, 0:1] + taps[:, 2:3] * after[:, 1:2],
-            jnp.zeros((2 * F, TOK - 2), f32),
-        ],
-        1,
-    ).astype(bf16)
-    for dest in range(H):
-        out[dest, 2 * F * H : FIRST] = edge
-
 
 def stacked(grads, block):
     return jnp.concatenate(
@@ -271,29 +348,21 @@
     )
 
 
-def weight_kernel(place, grads, data, out, own, edge):
-    blocks = [stacked(grads, b) for b in range(H + 1)]
+def weight_kernel(place, grads, data, out, own):
     own[...] = stacked(grads, place[1])
-    edge[...] = blocks[H]
-    total = jnp.concatenate(blocks[:H], 1)
+    total = jnp.concatenate([stacked(grads, b) for b in range(H)], 1).T
     count, rows = out.shape[:2]
-    parts = count * rows // 128
+    parts = count * rows // TOK
     for i in range(parts):
-        at = ROWS + HID * i
+        at = ROWS + TOK * i
         tokens = jnp.concatenate([data[b, at : at + TOK] for b in range(H)], 0)
-        before = data[0, at + TOK : at + HID]
-        result = (
-            mm(tokens, total.T, TN) + mm(before, blocks[H].T[:PAD], TN)
-        ).astype(bf16)
+        result = mm(tokens, total, TN).astype(bf16)
         for j in range(count // parts):
             out[i * (count // parts) + j] = result[rows * j : rows * (j + 1)]
 
 
-def hidden_kernel(place, own, edge, weight, out):
-    last = (place[1] == H - 1).astype(f32)
-    later = pltpu.roll(edge[...].astype(f32), TOK - (KCONV - 1), 1) * last
-    grads = (own[...].astype(f32) + later).astype(bf16)
-    out[...] = mm(grads.T, weight[...], NT).astype(bf16)
+def hidden_kernel(own, weight, out):
+    out[...] = mm(own[...].T, weight[...], NT).astype(bf16)
 
 
 def unpack_kernel(data, output, g_gate, g_value):
@@ -328,29 +397,33 @@
 def body(hidden_in, qk_weight, conv_weight, values, gate_in, cotangent):
     tokens = hidden_in[0]
     supers = lax.axis_size("s")
-    blocks = supers * H
     others = lax.axis_size(("dp", "s"))
     model = tokens.shape[1]
     chunks, width = H // WIDE, TOK * WIDE
     place = jnp.stack([lax.axis_index("s"), lax.axis_index("g")]).astype(jnp.int32)
-    halo = lax.ppermute(
-        tokens[TOK - (KCONV - 1) :], ("s", "g"), [(i, i + 1) for i in range(blocks - 1)]
-    )
+    taps = (pltpu.VMEM((2 * H * F, 8), f32),)
     packed = call(
         pack_kernel,
         "pack",
-        shape((H, ROWS + HID * (model // H // 128), TOK), bf16),
+        shape((H, ROWS + model // H, TOK), bf16),
         tokens,
-        halo,
         qk_weight,
-        conv_weight,
         values[0],
         gate_in[0],
         cotangent[0],
     )
     data = swap(packed, "g")
-    own = call(state_kernel, "state", shape((supers, SENT, 2 * DV), bf16), data)
-    done, gq, gk, gv, parts, sent = call(
+    own = call(
+        state_kernel,
+        "state",
+        shape((supers, SENT, 2 * DV), bf16),
+        place,
+        data,
+        conv_weight,
+        scalars=1,
+        scratch=taps,
+    )
+    done, gq, gk, gv, parts, keys, edges, sent = call(
         main_kernel,
         "main",
         (
@@ -359,12 +432,16 @@
             shape((chunks, F, width), f32),
             shape((chunks, DV, width), f32),
             shape((chunks, FEAT, 2 * DV), f32),
+            shape((chunks, F, width), f32),
+            shape((2 * F + DV, 2 * DV), f32),
             shape((supers, SENT, 2 * DV), bf16),
         ),
         place,
         data,
         swap(own, "s"),
+        conv_weight,
         scalars=1,
+        scratch=taps,
     )
     back = call(
         back_kernel,
@@ -378,17 +455,18 @@
         gk,
         gv,
         parts,
+        keys,
+        edges,
         conv_weight,
         scalars=1,
-        scratch=(pltpu.VMEM((2 * H * F, 8), f32),),
+        scratch=taps,
     )
     back = swap(back, "g")
-    partial, own_grad, edge = call(
+    partial, own_grad = call(
         weight_kernel,
         "weight",
         (
             shape((others, model // H // others, 2 * H * F), bf16),
-            shape((2 * H * F, TOK), bf16),
             shape((2 * H * F, TOK), bf16),
         ),
         place,
@@ -404,16 +482,8 @@
     output, grad_gate, grad_values = call(
         unpack_kernel, "unpack", (shape((TOK, H * DV), bf16),) * 3, back
     )
-    later = lax.ppermute(edge, "s", [(i + 1, i) for i in range(supers - 1)])
     grad_hidden = call(
-        hidden_kernel,
-        "hidden",
-        shape((TOK, model), bf16),
-        place,
-        own_grad,
-        later,
-        qk_weight,
-        scalars=1,
+        hidden_kernel, "hidden", shape((TOK, model), bf16), own_grad, qk_weight
     )
     return output[None], grad_hidden[None], grad_values[None], grad_gate[None], grad_qk_weight
 

time: 176 us -> 159 us (0.903)
  the two profiles are of different devices: /device:TPU:32 before, /device:TPU:1 now
where the time goes in v4:
time: 159 us; the launch traced here: 157 us
  blocking collectives  92.8 us (58%)
  Pallas kernels  25.3 us (16%)
  waiting for transfers between devices  21.2 us (13%)
  starting transfers between devices  13.9 us (9%)
  local copies, waits for them, and re-layouts  2.95 us (2%)
    all_to_all x5, blocking collectives, swap(): return lax.all_to_all(x, axis, 0, 0, tiled=True)  92.8 us
    pallas_call x8, Pallas kernels, call(): pl.pallas_call(kernel, name=name, out_shape=out_shape, in_specs=specs, ou...  25.3 us
    all_to_all x2, waiting for transfers between devices, swap(): return lax.all_to_all(x, axis, 0, 0, tiled=True)  21.2 us
    all_to_all x2, starting transfers between devices, swap(): return lax.all_to_all(x, axis, 0, 0, tiled=True)  13.9 us
  transfers between devices with their start and end apart: 2, of which 2 were waited for; matrix products, arithmetic and copies ran while one was open for 0% of the time, Pallas kernels for 3%

profile of v4, /device:TPU:1, one launch (start us, length us, event | category | flops | bytes accessed | tf_op | source)
XLA Modules:
  0.0 157.5 jit_solution(12510664613159533422)
XLA Ops:
  0.6 2.8 %pack.1 = bf16[8,480,128]{2,1,0:T(8,128)(2,1)} custom-call(bf16[128,2048]{1,0:T(8,128)(2,1)} %bitcast.15, bf16[2048,256]{1,0:T(8,128)(2,1)} %weight.5, bf16[128,512]{1,0:T(8,128)(2,1)} %bitcast.16, bf16[128,512]{1,0:T(8,128)(2,1)} %bitcast.17, bf16[128,512]{1,0:T(8,128)(2,1)} %bitcast.18), custom_call_target="tpu_custom_call" | custom-call | tf_op jit(solution)/shard_map/pack/pallas_call | solution.py:379
  3.4 7.1 %all-to-all-start = ((bf16[8,480,128]{2,1,0:T(8,128)(2,1)}), bf16[8,480,128]{2,1,0:T(8,128)(2,1)S(1)}, u32[]{:S(2)}, u32[]{:S(2)}) async-start(bf16[8,480,128]{2,1,0:T(8,128)(2,1)} %pack.1), calls=%async_computation | async-start | bytes 1966080 | tf_op jit(solution)/shard_map/all_to_all | solution.py:390
  10.6 0.6 pad_add_fusion.place
  11.2 12.2 %all-to-all-done.data = bf16[8,480,128]{2,1,0:T(8,128)(2,1)S(1)} async-done(((bf16[8,480,128]{2,1,0:T(8,128)(2,1)}), bf16[8,480,128]{2,1,0:T(8,128)(2,1)S(1)}, u32[]{:S(2)}, u32[]{:S(2)}) %all-to-all-start) | async-done | bytes 983072 | tf_op jit(solution)/shard_map/all_to_all | solution.py:390
  23.4 0.0 copy-start
  23.4 0.9 copy-done
  24.3 2.6 %state.1 = bf16[16,96,128]{2,1,0:T(8,128)(2,1)} custom-call(s32[2]{0:T(128)} %pad_add_fusion.place, bf16[8,480,128]{2,1,0:T(8,128)(2,1)} %copy-done, f32[3,256]{1,0:T(4,128)} %conv.5), custom_call_target="tpu_custom_call" | custom-call | tf_op jit(solution)/shard_map/state/pallas_call | solution.py:379
  27.0 23.7 %all_to_all.35.states = bf16[16,96,128]{2,1,0:T(8,128)(2,1)} all-to-all(bf16[16,96,128]{2,1,0:T(8,128)(2,1)} %state.1), channel_id=1, replica_groups=mesh['dp'=2,'s'=16,'g'=8] {'s'}, dimensions={0} | all-to-all | bytes 786432 | tf_op jit(solution)/shard_map/all_to_all | solution.py:390
  50.7 7.6 %main.1 = (bf16[8,128,128]{2,1,0:T(8,128)(2,1)}, f32[4,16,256]{2,1,0:T(8,128)}, f32[4,16,256]{2,1,0:T(8,128)}, f32[4,64,256]{2,1,0:T(8,128)}, f32[4,160,128]{2,1...) custom-call(s32[2]{0:T(128)} %pad_add_fusion.place, ...), custom_call_target="tpu_custom_call" | custom-call | tf_op jit(solution)/shard_map/main/pallas_call | solution.py:379
  58.3 16.8 %all_to_all.36.states = bf16[16,96,128]{2,1,0:T(8,128)(2,1)} all-to-all(bf16[16,96,128]{2,1,0:T(8,128)(2,1)} %get-tuple-element.18), channel_id=1, replica_groups=mesh['dp'=2,'s'=16,'g'=8] {'s'}, dimensions={0} | all-to-all | bytes 786432 | tf_op jit(solution)/shard_map/all_to_all | solution.py:390
  75.1 3.5 %back.1 = bf16[8,448,128]{2,1,0:T(8,128)(2,1)} custom-call(s32[2]{0:T(128)} %pad_add_fusion.place, bf16[8,480,128]{2,1,0:T(8,128)(2,1)} %copy-done, bf16[16,96,128]{2,1,0:T(8,128)(2,1)} %all_to_all.36.states, bf16[8,128,128]{2,1,0:T(8,128)(2,1)} %get-tuple-element.19.done, f32[4,16,256]{2,1,0:T(8,128)} %get-tuple-element.20.gq, ...), custom_call_target="tpu_custom_call" | custom-call | tf_op jit(solution)/shard_map/back/pallas_call | solution.py:379
  78.6 24.2 %all_to_all.37.data.grads = bf16[8,448,128]{2,1,0:T(8,128)(2,1)} all-to-all(bf16[8,448,128]{2,1,0:T(8,128)(2,1)} %back.1), channel_id=1, replica_groups=mesh['dp'=2,'s'=16,'g'=8] {'g'}, dimensions={0} | all-to-all | bytes 1835008 | tf_op jit(solution)/shard_map/all_to_all | solution.py:390
  102.8 2.6 %weight.4 = (bf16[32,8,256]{2,1,0:T(8,128)(2,1)}, bf16[256,128]{1,0:T(8,128)(2,1)}) custom-call(s32[2]{0:T(128)} %pad_add_fusion.place, bf16[8,448,128]{2,1,0:T(8,128)(2,1)} %all_to_all.37.data.grads, bf16[8,480,128]{2,1,0:T(8,128)(2,1)} %copy-done), custom_call_target="tpu_custom_call" | custom-call | tf_op jit(solution)/shard_map/weight/pallas_call | solution.py:379
  105.4 14.4 %all_to_all.38.data = bf16[32,8,256]{2,1,0:T(8,128)(2,1)} all-to-all(bf16[32,8,256]{2,1,0:T(8,128)(2,1)} %get-tuple-element.30), channel_id=1, replica_groups=mesh['dp'=2,'s'=16,'g'=8] {'dp','s'}, dimensions={0} | all-to-all | bytes 262144 | tf_op jit(solution)/shard_map/all_to_all | solution.py:390
  119.8 1.6 %sum.1 = bf16[32,8,256]{2,1,0:T(8,128)(2,1)} custom-call(bf16[32,8,256]{2,1,0:T(8,128)(2,1)} %all_to_all.38.data), custom_call_target="tpu_custom_call" | custom-call | tf_op jit(solution)/shard_map/sum/pallas_call | solution.py:379
  121.4 13.7 %all_to_all.39 = bf16[32,8,256]{2,1,0:T(8,128)(2,1)S(1)} all-to-all(bf16[32,8,256]{2,1,0:T(8,128)(2,1)} %sum.1), channel_id=1, replica_groups=mesh['dp'=2,'s'=16,'g'=8] {'dp','s'}, dimensions={0} | all-to-all | bytes 262144 | tf_op jit(solution)/shard_map/all_to_all | solution.py:390
  135.1 1.0 broadcast_in_dim.24
  136.2 6.8 %all-to-all-start.6 = ((bf16[8,256,256]{2,1,0:T(8,128)(2,1)}), bf16[8,256,256]{2,1,0:T(8,128)(2,1)S(1)}, u32[]{:S(2)}, u32[]{:S(2)}) async-start(bf16[8,256,256]{2,1,0:T(8,128)(2,1)} %broadcast_in_dim.24), calls=%async_computation.6 | async-start | bytes 2097152 | tf_op jit(solution)/shard_map/all_to_all | solution.py:390
  143.0 2.5 %hidden.1 = bf16[128,2048]{1,0:T(8,128)(2,1)} custom-call(bf16[256,128]{1,0:T(8,128)(2,1)} %get-tuple-element.27.own, bf16[2048,256]{1,0:T(8,128)(2,1)} %weight.5), custom_call_target="tpu_custom_call" | custom-call | tf_op jit(solution)/shard_map/hidden/pallas_call | solution.py:379
  145.5 2.0 %unpack.1 = (bf16[128,512]{1,0:T(8,128)(2,1)}, bf16[128,512]{1,0:T(8,128)(2,1)}, bf16[128,512]{1,0:T(8,128)(2,1)}) custom-call(bf16[8,448,128]{2,1,0:T(8,128)(2,1)} %all_to_all.37.data.grads), custom_call_target="tpu_custom_call" | custom-call | tf_op jit(solution)/shard_map/unpack/pallas_call | solution.py:379
  147.5 9.0 %all-to-all-done.6 = bf16[8,256,256]{2,1,0:T(8,128)(2,1)S(1)} async-done(((bf16[8,256,256]{2,1,0:T(8,128)(2,1)}), bf16[8,256,256]{2,1,0:T(8,128)(2,1)S(1)}, u32[]{:S(2)}, u32[]{:S(2)}) %all-to-all-start.6) | async-done | bytes 1048608 | tf_op jit(solution)/shard_map/all_to_all | solution.py:390
  156.5 1.0 copy.12
Async XLA Ops:
  3.4 19.9 %all-to-all-start = ((bf16[8,480,128]{2,1,0:T(8,128)(2,1)}), bf16[8,480,128]{2,1,0:T(8,128)(2,1)S(1)}, u32[]{:S(2)}, u32[]{:S(2)}) async-start(bf16[8,480,128]{2,1,0:T(8,128)(2,1)} %pack.1), calls=%async_computation | async-start | bytes 1966080 | tf_op jit(solution)/shard_map/all_to_all | solution.py:390
  23.4 0.9 copy-start
  136.2 20.3 %all-to-all-start.6 = ((bf16[8,256,256]{2,1,0:T(8,128)(2,1)}), bf16[8,256,256]{2,1,0:T(8,128)(2,1)S(1)}, u32[]{:S(2)}, u32[]{:S(2)}) async-start(bf16[8,256,256]{2,1,0:T(8,128)(2,1)} %broadcast_in_dim.24), calls=%async_computation.6 | async-start | bytes 2097152 | tf_op jit(solution)/shard_map/all_to_all | solution.py:390

commit v5 on v4

--- a/solution.py
+++ b/solution.py
@@ -11,9 +11,11 @@
 F = 16
 DV = 64
 KCONV = 3
+SUPER = ("y", "z")
+OTHER = ("dp", "y")
 TOK = 128
-ROWS = 2 * F + 3 * DV
-AT_V, AT_G, AT_C = 2 * F, 2 * F + DV, 2 * F + 2 * DV
+ROWS = 2 * F + 2 * DV
+AT_V, AT_G = 2 * F, 2 * F + DV
 FEAT = 160
 SENT = FEAT // 2 + 16
 WIDE = 2
@@ -160,15 +162,16 @@
 def pack_kernel(tokens, weight, values, gate, cot, out):
     x = tokens[...]
     projected = mm(x, weight[...], NN).T.astype(bf16)
-    v, g, c = values[...].T, gate[...].T, cot[...].T
+    g = gate[...].astype(f32)
+    v = values[...].T
+    up = (cot[...].astype(f32) * (g * jax.nn.sigmoid(g))).astype(bf16).T
     width = H * F
     for h in range(H):
         out[h, 0:F] = projected[F * h : F * (h + 1)]
         out[h, F : 2 * F] = projected[width + F * h : width + F * (h + 1)]
         cols = slice(DV * h, DV * (h + 1))
         out[h, AT_V : AT_V + DV] = v[cols]
-        out[h, AT_G : AT_G + DV] = g[cols]
-        out[h, AT_C : AT_C + DV] = c[cols]
+        out[h, AT_G : AT_G + DV] = up[cols]
         for i in range(x.shape[1] // H // TOK):
             at = ROWS + TOK * i
             start = x.shape[1] // H * h + TOK * i
@@ -237,8 +240,7 @@
         (qh, ql), (kh, kl) = halves(q), halves(k)
         keys[c] = k
         v = wide_values(rows_of(data, c, AT_V, DV))
-        g = rows_of(data, c, AT_G, DV).astype(f32)
-        cot = rows_of(data, c, AT_C, DV).astype(f32)
+        g_att = rows_of(data, c, AT_G, DV).astype(f32)
         scores = mm(
             jnp.concatenate([kh, kh, kl], 0), jnp.concatenate([qh, ql, qh], 0), TN
         ) * F**-0.5
@@ -248,11 +250,7 @@
         numer = mm(v, weights[0], NN) + mm(v, weights[1], NN) + mm3(split_state, q_feat, TN)
         inverse = 1.0 / numer[DV : DV + 1]
         attended = numer[:DV] * inverse
-        sig = jax.nn.sigmoid(g)
-        act = g * sig
-        result = (attended * act).astype(bf16)
-        g_gate = (cot * attended * sig * (1.0 + g * (1.0 - sig))).astype(bf16)
-        g_att = cot * act
+        result = attended.astype(bf16)
         g_num = g_att * inverse
         g_den = -jnp.sum(g_att * attended, 0, keepdims=True) * inverse
         row = lax.broadcasted_iota(jnp.int32, (DV, length), 0)
@@ -275,8 +273,7 @@
         state = state + (mm(k_feat[0], v, NT) + mm(k_feat[1], v, NT))
         for i in range(WIDE):
             cols = slice(TOK * i, TOK * (i + 1))
-            out[WIDE * c + i, 0:DV] = result[:, cols]
-            out[WIDE * c + i, DV : 2 * DV] = g_gate[:, cols]
+            out[WIDE * c + i] = result[:, cols]
         gq[c] = g_query
         gk[c] = g_key
         gv[c] = g_value
@@ -332,8 +329,8 @@
         for i in range(WIDE):
             cols = slice(TOK * i, TOK * (i + 1))
             b = WIDE * c + i
-            out[b, FIRST : FIRST + 2 * DV] = done[b]
-            out[b, FIRST + 2 * DV : FIRST + 3 * DV] = g_value[:, cols]
+            out[b, FIRST : FIRST + DV] = done[b]
+            out[b, FIRST + DV : FIRST + 2 * DV] = g_value[:, cols]
             for dest in range(H):
                 out[dest, 2 * F * b : 2 * F * (b + 1)] = total[:, cols]
 
@@ -365,19 +362,37 @@
     out[...] = mm(own[...].T, weight[...], NT).astype(bf16)
 
 
-def unpack_kernel(data, output, g_gate, g_value):
-    for i, target in enumerate((output, g_gate, g_value)):
-        at = FIRST + DV * i
-        target[...] = jnp.concatenate([data[h, at : at + DV] for h in range(H)], 0).T
-
-
-def call(kernel, name, out_shape, *args, scalars=0, waits=0, scratch=()):
+def unpack_kernel(data, gate, cot, output, g_gate, g_value):
+    attended, values = (
+        jnp.concatenate([data[h, at : at + DV] for h in range(H)], 0).T
+        for at in (FIRST, FIRST + DV)
+    )
+    g = gate[...].astype(f32)
+    sig = jax.nn.sigmoid(g)
+    attended = attended.astype(f32)
+    output[...] = (attended * (g * sig)).astype(bf16)
+    g_gate[...] = (
+        cot[...].astype(f32) * attended * sig * (1.0 + g * (1.0 - sig))
+    ).astype(bf16)
+    g_value[...] = values
+
+
+def near(x):
+    return pltpu.with_memory_space_constraint(x, pltpu.VMEM)
+
+
+def call(kernel, name, out_shape, *args, scalars=0, final=False, scratch=()):
     specs = [pl.BlockSpec(memory_space=pltpu.SMEM)] * scalars
-    specs += [pl.BlockSpec(memory_space=pltpu.VMEM)] * (len(args) - scalars - waits)
-    specs += [pl.BlockSpec(memory_space=pl.ANY)] * waits
+    specs += [pl.BlockSpec(memory_space=pltpu.VMEM)] * (len(args) - scalars)
     outs = jax.tree.map(lambda s: pl.BlockSpec(memory_space=pltpu.VMEM), out_shape)
+    if not final:
+        out_shape = jax.tree.map(lambda s: pltpu.VMEM(s.shape, s.dtype), out_shape)
     return pl.pallas_call(
-        kernel, name=name, out_shape=out_shape, in_specs=specs, out_specs=outs,
+        kernel,
+        name=name,
+        out_shape=out_shape,
+        in_specs=specs,
+        out_specs=outs,
         scratch_shapes=scratch,
     )(*args)
 
@@ -387,20 +402,16 @@
 
 
 def swap(x, axis):
-    return lax.all_to_all(x, axis, 0, 0, tiled=True)
-
-
-def everyone(x, axis):
-    return swap(jnp.broadcast_to(x[None], (lax.axis_size(axis),) + x.shape), axis)
+    return near(lax.all_to_all(x, axis, 0, 0, tiled=True))
 
 
 def body(hidden_in, qk_weight, conv_weight, values, gate_in, cotangent):
     tokens = hidden_in[0]
-    supers = lax.axis_size("s")
-    others = lax.axis_size(("dp", "s"))
+    supers = lax.axis_size(SUPER)
+    others = lax.axis_size(OTHER)
     model = tokens.shape[1]
     chunks, width = H // WIDE, TOK * WIDE
-    place = jnp.stack([lax.axis_index("s"), lax.axis_index("g")]).astype(jnp.int32)
+    place = jnp.stack([lax.axis_index(SUPER), lax.axis_index("g")]).astype(jnp.int32)
     taps = (pltpu.VMEM((2 * H * F, 8), f32),)
     packed = call(
         pack_kernel,
@@ -427,7 +438,7 @@
         main_kernel,
         "main",
         (
-            shape((H, 2 * DV, TOK), bf16),
+            shape((H, DV, TOK), bf16),
             shape((chunks, F, width), f32),
             shape((chunks, F, width), f32),
             shape((chunks, DV, width), f32),
@@ -438,7 +449,7 @@
         ),
         place,
         data,
-        swap(own, "s"),
+        swap(own, SUPER),
         conv_weight,
         scalars=1,
         scratch=taps,
@@ -446,17 +457,11 @@
     back = call(
         back_kernel,
         "back",
-        shape((H, FIRST + 3 * DV, TOK), bf16),
+        shape((H, FIRST + 2 * DV, TOK), bf16),
         place,
         data,
-        swap(sent, "s"),
-        done,
-        gq,
-        gk,
-        gv,
-        parts,
-        keys,
-        edges,
+        swap(sent, SUPER),
+        *(near(x) for x in (done, gq, gk, gv, parts, keys, edges)),
         conv_weight,
         scalars=1,
         scratch=taps,
@@ -474,24 +479,43 @@
         data,
         scalars=1,
     )
+    deep = model // H // others
+    some = swap(partial, OTHER)
     summed = call(
-        sum_kernel, "sum", shape(partial.shape, bf16), swap(partial, ("dp", "s"))
-    )
-    slices = swap(summed, ("dp", "s")).reshape(model // H, 2 * H * F)
-    grad_qk_weight = everyone(slices, "g").reshape(model, 2 * H * F)
+        sum_kernel, "sum_a", shape((lax.axis_size("z"), deep, 2 * H * F), bf16), some
+    )
+    summed = call(
+        sum_kernel, "sum_b", shape((H * others, deep, 2 * H * F), bf16), swap(summed, "z")
+    )
+    grad_qk_weight = lax.all_to_all(summed, ("g",) + OTHER, 0, 0, tiled=True)
+    grad_qk_weight = grad_qk_weight.reshape(model, 2 * H * F)
     output, grad_gate, grad_values = call(
-        unpack_kernel, "unpack", (shape((TOK, H * DV), bf16),) * 3, back
+        unpack_kernel,
+        "unpack",
+        (shape((TOK, H * DV), bf16),) * 3,
+        back,
+        gate_in[0],
+        cotangent[0],
+        final=True,
     )
     grad_hidden = call(
-        hidden_kernel, "hidden", shape((TOK, model), bf16), own_grad, qk_weight
+        hidden_kernel,
+        "hidden",
+        shape((TOK, model), bf16),
+        near(own_grad),
+        qk_weight,
+        final=True,
     )
     return output[None], grad_hidden[None], grad_values[None], grad_gate[None], grad_qk_weight
 
 
 def solution(mesh):
     pairs, blocks = mesh.devices.shape
-    fine = Mesh(mesh.devices.reshape(pairs, blocks // H, H), ("dp", "s", "g"))
-    split = P("dp", ("s", "g"), None)
+    y = 4 if blocks // H % 4 == 0 else 1
+    fine = Mesh(
+        mesh.devices.reshape(pairs, y, blocks // H // y, H), ("dp", "y", "z", "g")
+    )
+    split = P("dp", ("y", "z", "g"), None)
     return jax.shard_map(
         body,
         mesh=fine,

time: 159 us -> 143 us (0.90)
  blocking collectives: 92.8 us -> 78.8 us
  Pallas kernels: 25.3 us -> 18.5 us
  waiting for transfers between devices: 21.2 us -> 24.4 us
    all_to_all x5, blocking collectives: 92.8 us -> 78.8 us  [swap(): return near(lax.all_to_all(x, axis, 0, 0, tiled=True))]
    pallas_call x8 -> x9, Pallas kernels: 25.3 us -> 18.5 us  [call(): pl.pallas_call(kernel, name=name, out_shape=out_shape, in_specs=specs, ou...]
    all_to_all x2, waiting for transfers between devices: 21.2 us -> 24.4 us  [the longest x1 13.3 us: body(): grad_qk_weight = lax.all_to_all(summed, ('g',) + OTHER, 0, 0, tiled=True)]
    unnamed x3 -> x17, local copies, waits for them, and re-layouts: 1.91 us -> 4.18 us
where the time goes in v5:
time: 143 us
  blocking collectives  78.8 us (55%)
  waiting for transfers between devices  24.4 us (17%)
  Pallas kernels  18.5 us (13%)
  starting transfers between devices  15.4 us (11%)
  local copies, waits for them, and re-layouts  4.18 us (3%)
    all_to_all x5, blocking collectives, swap(): return near(lax.all_to_all(x, axis, 0, 0, tiled=True))  78.8 us
    pallas_call x9, Pallas kernels, call(): pl.pallas_call(kernel, name=name, out_shape=out_shape, in_specs=specs, ou...  18.5 us
    all_to_all x1, waiting for transfers between devices, body(): grad_qk_weight = lax.all_to_all(summed, ('g',) + OTHER, 0, 0, tiled=True)  13.3 us
    all_to_all x1, waiting for transfers between devices, swap(): return near(lax.all_to_all(x, axis, 0, 0, tiled=True))  11.1 us
    all_to_all x1, starting transfers between devices, body(): grad_qk_weight = lax.all_to_all(summed, ('g',) + OTHER, 0, 0, tiled=True)  8.22 us
    all_to_all x1, starting transfers between devices, swap(): return near(lax.all_to_all(x, axis, 0, 0, tiled=True))  7.14 us
    unnamed x17, local copies, waits for them, and re-layouts  4.18 us
  transfers between devices with their start and end apart: 2, of which 2 were waited for; matrix products, arithmetic and copies ran while one was open for 0% of the time, Pallas kernels for 3%

profile of v5, /device:TPU:1, one launch (start us, length us, event | category | flops | bytes accessed | tf_op | source)
XLA Modules:
  0.0 142.5 jit_solution(10800390696680233059)
XLA Ops:
  0.6 2.8 %pack.1 = bf16[8,416,128]{2,1,0:T(8,128)(2,1)} custom-call(bf16[128,2048]{1,0:T(8,128)(2,1)} %bitcast.13, bf16[2048,256]{1,0:T(8,128)(2,1)} %weight.5, bf16[128,512]{1,0:T(8,128)(2,1)} %bitcast.18, bf16[128,512]{1,0:T(8,128)(2,1)} %bitcast.14, bf16[128,512]{1,0:T(8,128)(2,1)} %bitcast.16), custom_call_target="tpu_custom_call" | custom-call | tf_op jit(solution)/shard_map/pack/pallas_call | solution.py:390
  3.4 7.1 %all-to-all-start = ((bf16[8,416,128]{2,1,0:T(8,128)(2,1)}), bf16[8,416,128]{2,1,0:T(8,128)(2,1)S(1)}, u32[]{:S(2)}, u32[]{:S(2)}) async-start(bf16[8,416,128]{2,1,0:T(8,128)(2,1)} %pack.1), calls=%async_computation | async-start | bytes 1703936 | tf_op jit(solution)/shard_map/all_to_all | solution.py:405
  10.5 0.6 pad_add_fusion.place
  11.1 11.1 %all-to-all-done.data = bf16[8,416,128]{2,1,0:T(8,128)(2,1)S(1)} async-done(((bf16[8,416,128]{2,1,0:T(8,128)(2,1)}), bf16[8,416,128]{2,1,0:T(8,128)(2,1)S(1)}, u32[]{:S(2)}, u32[]{:S(2)}) %all-to-all-start) | async-done | bytes 852000 | tf_op jit(solution)/shard_map/all_to_all | solution.py:405
  22.3 0.0 copy-start
  22.3 1.4 state.1
  23.6 23.3 %all_to_all.35.states = bf16[16,96,128]{2,1,0:T(8,128)(2,1)S(1)} all-to-all(bf16[16,96,128]{2,1,0:T(8,128)(2,1)S(1)} %state.1), channel_id=1, replica_groups=mesh['dp'=2,'y'=4,'z'=4,'g'=8] {'y','z'}, dimensions={0} | all-to-all | bytes 786432 | tf_op jit(solution)/shard_map/all_to_all | solution.py:405
  46.9 0.0 copy-done
  46.9 6.1 %main.1 = (bf16[8,64,128]{2,1,0:T(8,128)(2,1)S(1)}, f32[4,16,256]{2,1,0:T(8,128)S(1)}, f32[4,16,256]{2,1,0:T(8,128)S(1)}, f32[4,64,256]{2,1,0:T(8,128)S(1)}, f32...) custom-call(s32[2]{0:T(128)} %pad_add_fusion.place, ...), custom_call_target="tpu_custom_call" | custom-call | tf_op jit(solution)/shard_map/main/pallas_call | solution.py:390
  53.0 0.0 copy-start.2
  53.0 0.7 copy-done.2
  53.7 0.0 copy-start.4
  53.7 0.7 copy-done.4
  54.5 0.0 copy-start.6
  54.5 0.6 copy-done.6
  55.1 0.0 copy-start.3
  55.1 0.0 copy-start.5
  55.1 0.0 copy-start.7
  55.1 15.3 %all_to_all.36.states = bf16[16,96,128]{2,1,0:T(8,128)(2,1)S(1)} all-to-all(bf16[16,96,128]{2,1,0:T(8,128)(2,1)S(1)} %get-tuple-element.18), channel_id=1, replica_groups=mesh['dp'=2,'y'=4,'z'=4,'g'=8] {'y','z'}, dimensions={0} | all-to-all | bytes 786432 | tf_op jit(solution)/shard_map/all_to_all | solution.py:405
  70.4 0.0 copy-done.3
  70.4 0.0 copy-done.5
  70.4 0.0 copy-done.7
  70.4 0.0 copy-start.1
  70.4 1.1 copy-done.1
  71.5 1.7 %back.1 = bf16[8,384,128]{2,1,0:T(8,128)(2,1)S(1)} custom-call(s32[2]{0:T(128)} %pad_add_fusion.place, bf16[8,416,128]{2,1,0:T(8,128)(2,1)S(1)} %copy-done.1, bf16[16,96,128]{2,1,0:T(8,128)(2,1)S(1)} %all_to_all.36.states, bf16[8,64,128]{2,1,0:T(8,128)(2,1)S(1)} %get-tuple-element.19.done, f32[4,16,256]{2,1,0:T(8,128)S(1)} %get-tuple-element.20.gq, ...), custom_call_target="tpu_custom_call" | custom-call | tf_op jit(solution)/shard_map/back/pallas_call | solution.py:390
  73.2 22.1 %all_to_all.37.data.grads = bf16[8,384,128]{2,1,0:T(8,128)(2,1)S(1)} all-to-all(bf16[8,384,128]{2,1,0:T(8,128)(2,1)S(1)} %back.1), channel_id=1, replica_groups=mesh['dp'=2,'y'=4,'z'=4,'g'=8] {'g'}, dimensions={0} | all-to-all | bytes 1572864 | tf_op jit(solution)/shard_map/all_to_all | solution.py:405
  95.3 1.1 weight.4
  96.4 7.8 %all_to_all.38.data = bf16[8,32,256]{2,1,0:T(8,128)(2,1)S(1)} all-to-all(bf16[8,32,256]{2,1,0:T(8,128)(2,1)S(1)} %get-tuple-element.30), channel_id=1, replica_groups=mesh['dp'=2,'y'=4,'z'=4,'g'=8] {'dp','y'}, dimensions={0} | all-to-all | bytes 262144 | tf_op jit(solution)/shard_map/all_to_all | solution.py:405
  104.3 10.3 %all_to_all.39.data = bf16[4,32,256]{2,1,0:T(8,128)(2,1)S(1)} all-to-all(bf16[4,32,256]{2,1,0:T(8,128)(2,1)S(1)} %sum_a.1), channel_id=1, replica_groups=mesh['dp'=2,'y'=4,'z'=4,'g'=8] {'z'}, dimensions={0} | all-to-all | bytes 131072 | tf_op jit(solution)/shard_map/all_to_all | solution.py:405
  114.6 1.1 sum_b.1
  115.7 8.2 %all-to-all-start.6 = ((bf16[64,32,256]{2,1,0:T(8,128)(2,1)}), bf16[64,32,256]{2,1,0:T(8,128)(2,1)S(1)}, u32[]{:S(2)}, u32[]{:S(2)}) async-start(bf16[64,32,256]{2,1,0:T(8,128)(2,1)} %sum_b.1), calls=%async_computation.6 | async-start | bytes 2097152 | tf_op jit(solution)/shard_map/all_to_all | solution.py:490
  123.9 2.5 %hidden.1 = bf16[128,2048]{1,0:T(8,128)(2,1)} custom-call(bf16[256,128]{1,0:T(8,128)(2,1)S(1)} %get-tuple-element.27.own, bf16[2048,256]{1,0:T(8,128)(2,1)} %weight.5), custom_call_target="tpu_custom_call" | custom-call | tf_op jit(solution)/shard_map/hidden/pallas_call | solution.py:390
  126.4 1.9 %unpack.1 = (bf16[128,512]{1,0:T(8,128)(2,1)}, bf16[128,512]{1,0:T(8,128)(2,1)}, bf16[128,512]{1,0:T(8,128)(2,1)}) custom-call(bf16[8,384,128]{2,1,0:T(8,128)(2,1)S(1)} %all_to_all.37.data.grads, bf16[128,512]{1,0:T(8,128)(2,1)} %bitcast.15, bf16[128,512]{1,0:T(8,128)(2,1)} %bitcast.17), custom_call_target="tpu_custom_call" | custom-call | tf_op jit(solution)/shard_map/unpack/pallas_call | solution.py:390
  128.3 13.3 %all-to-all-done.6 = bf16[64,32,256]{2,1,0:T(8,128)(2,1)S(1)} async-done(((bf16[64,32,256]{2,1,0:T(8,128)(2,1)}), bf16[64,32,256]{2,1,0:T(8,128)(2,1)S(1)}, u32[]{:S(2)}, u32[]{:S(2)}) %all-to-all-start.6) | async-done | bytes 1048608 | tf_op jit(solution)/shard_map/all_to_all | solution.py:490
  141.6 1.0 copy.12
  (1 shorter events, 0.0 us)
Async XLA Ops:
  3.4 18.9 %all-to-all-start = ((bf16[8,416,128]{2,1,0:T(8,128)(2,1)}), bf16[8,416,128]{2,1,0:T(8,128)(2,1)S(1)}, u32[]{:S(2)}, u32[]{:S(2)}) async-start(bf16[8,416,128]{2,1,0:T(8,128)(2,1)} %pack.1), calls=%async_computation | async-start | bytes 1703936 | tf_op jit(solution)/shard_map/all_to_all | solution.py:405
  22.3 24.7 %copy-start = (bf16[8,416,128]{2,1,0:T(8,128)(2,1)}, bf16[8,416,128]{2,1,0:T(8,128)(2,1)S(1)}, u32[]{:S(2)}) copy-start(bf16[8,416,128]{2,1,0:T(8,128)(2,1)S(1)} %all-to-all-done.data) | copy-start | bytes 2555908
  53.0 0.7 copy-start.2
  53.7 0.7 copy-start.4
  54.5 0.6 copy-start.6
  55.1 15.3 %copy-start.3 = (f32[4,160,128]{2,1,0:T(8,128)S(1)}, f32[4,160,128]{2,1,0:T(8,128)}, u32[]{:S(2)}) copy-start(f32[4,160,128]{2,1,0:T(8,128)} %copy-done.2) | copy-start | bytes 983044
  55.1 15.3 %copy-start.5 = (f32[4,64,256]{2,1,0:T(8,128)S(1)}, f32[4,64,256]{2,1,0:T(8,128)}, u32[]{:S(2)}) copy-start(f32[4,64,256]{2,1,0:T(8,128)} %copy-done.4) | copy-start | bytes 786436
  55.1 15.3 %copy-start.7 = (f32[96,128]{1,0:T(8,128)S(1)}, f32[96,128]{1,0:T(8,128)}, u32[]{:S(2)}) copy-start(f32[96,128]{1,0:T(8,128)} %copy-done.6) | copy-start | bytes 147460
  70.4 1.2 copy-start.1
  115.7 25.9 %all-to-all-start.6 = ((bf16[64,32,256]{2,1,0:T(8,128)(2,1)}), bf16[64,32,256]{2,1,0:T(8,128)(2,1)S(1)}, u32[]{:S(2)}, u32[]{:S(2)}) async-start(bf16[64,32,256]{2,1,0:T(8,128)(2,1)} %sum_b.1), calls=%async_computation.6 | async-start | bytes 2097152 | tf_op jit(solution)/shard_map/all_to_all | solution.py:490

commit v6 on v5

--- a/solution.py
+++ b/solution.py
@@ -14,8 +14,9 @@
 SUPER = ("y", "z")
 OTHER = ("dp", "y")
 TOK = 128
-ROWS = 2 * F + 2 * DV
-AT_V, AT_G = 2 * F, 2 * F + DV
+HID = 256
+AT_V, AT_G, AT_P = HID, HID + DV, HID + 2 * DV
+ROWS = AT_P + 2 * F
 FEAT = 160
 SENT = FEAT // 2 + 16
 WIDE = 2
@@ -167,15 +168,14 @@
     up = (cot[...].astype(f32) * (g * jax.nn.sigmoid(g))).astype(bf16).T
     width = H * F
     for h in range(H):
-        out[h, 0:F] = projected[F * h : F * (h + 1)]
-        out[h, F : 2 * F] = projected[width + F * h : width + F * (h + 1)]
+        out[h, AT_P : AT_P + F] = projected[F * h : F * (h + 1)]
+        out[h, AT_P + F : ROWS] = projected[width + F * h : width + F * (h + 1)]
         cols = slice(DV * h, DV * (h + 1))
         out[h, AT_V : AT_V + DV] = v[cols]
         out[h, AT_G : AT_G + DV] = up[cols]
         for i in range(x.shape[1] // H // TOK):
-            at = ROWS + TOK * i
             start = x.shape[1] // H * h + TOK * i
-            out[h, at : at + TOK] = x[:, start : start + TOK]
+            out[h, TOK * i : TOK * (i + 1)] = x[:, start : start + TOK]
 
 
 def state_kernel(place, data, conv, out, columns):
@@ -183,7 +183,7 @@
     total = jnp.zeros((FEAT, 2 * DV), f32)
     before = jnp.zeros((F, 2), f32)
     for c in range(H // WIDE):
-        raw = rows_of(data, c, F, F).astype(f32)
+        raw = rows_of(data, c, AT_P + F, F).astype(f32)
         feat = features(convolve(raw, before, taps))
         if c == 0:
             token = lax.broadcasted_iota(jnp.int32, feat.shape, 1)
@@ -192,15 +192,16 @@
         high, low = halves(feat)
         v = wide_values(rows_of(data, c, AT_V, DV))
         total = total + (mm(high, v, NT) + mm(low, v, NT))
-    first, last = data[0, 0 : 2 * F + DV], data[H - 1, 0 : 2 * F]
+    first, last = data[0, AT_P:ROWS], data[H - 1, AT_P:ROWS]
+    begin = data[0, AT_V : AT_V + DV]
     extra = []
     for start in (F, 0):
         rows = slice(start, start + F)
         extra += [first[rows, 0:1], first[rows, 1:2]]
         extra += [last[rows, TOK - 2 : TOK - 1], last[rows, TOK - 1 : TOK]]
     for j in range(DV // F):
-        rows = slice(2 * F + F * j, 2 * F + F * (j + 1))
-        extra += [first[rows, 0:1], first[rows, 1:2]]
+        rows = slice(F * j, F * (j + 1))
+        extra += [begin[rows, 0:1], begin[rows, 1:2]]
     repeat_into(out, pack_state(total, extra))
 
 
@@ -233,21 +234,21 @@
     causal = k_at <= q_at
     whole = jnp.zeros((FEAT, 2 * DV), f32)
     for c in range(H // WIDE):
-        raw = rows_of(data, c, 0, 2 * F).astype(f32)
+        raw = rows_of(data, c, AT_P, 2 * F).astype(f32)
         mixed = convolve(raw, before, taps)
         before = raw[:, -2:]
         q, k = mixed[:F], mixed[F:]
-        (qh, ql), (kh, kl) = halves(q), halves(k)
+        (qh, ql), (kh, kl) = halves(q * F**-0.5), halves(k)
         keys[c] = k
         v = wide_values(rows_of(data, c, AT_V, DV))
         g_att = rows_of(data, c, AT_G, DV).astype(f32)
-        scores = mm(
+        near_one = 1.0 + mm(
             jnp.concatenate([kh, kh, kl], 0), jnp.concatenate([qh, ql, qh], 0), TN
-        ) * F**-0.5
-        weights = halves(jnp.where(causal, 1.0 + scores + 0.5 * scores * scores, 0.0))
+        )
+        weights = jnp.where(causal, 0.5 + 0.5 * near_one * near_one, 0.0).astype(bf16)
         q_feat, k_feat = halves(features(q)), halves(features(k))
         split_state = halves(state)
-        numer = mm(v, weights[0], NN) + mm(v, weights[1], NN) + mm3(split_state, q_feat, TN)
+        numer = mm(v, weights, NN) + mm3(split_state, q_feat, TN)
         inverse = 1.0 / numer[DV : DV + 1]
         attended = numer[:DV] * inverse
         result = attended.astype(bf16)
@@ -257,16 +258,17 @@
         wide = jnp.concatenate([g_num, jnp.where(row == 0, g_den, 0.0)], 0)
         grads = halves(wide)
         g_weights = mm(v, grads[0], TN) + mm(v, grads[1], TN)
-        g_scores = halves(jnp.where(causal, g_weights * (1.0 + scores), 0.0) * F**-0.5)
-        g_query = mm3((kh, kl), g_scores, NN) + features_back(q, mm3(split_state, grads, NN))
+        g_scores = jnp.where(causal, g_weights * near_one, 0.0).astype(bf16)
+        g_local = (mm(kh, g_scores, NN) + mm(kl, g_scores, NN)) * F**-0.5
+        g_query = g_local + features_back(q, mm3(split_state, grads, NN))
         if c == 0:
             extra = [g_query[:, 0:1], g_query[:, 1:2]]
             for j in range(DV // F + 1):
                 column = wide[F * j : F * (j + 1), 0:1]
                 high = column.astype(bf16)
                 extra += [high, column - high.astype(f32)]
-        g_key = mm3((qh, ql), g_scores, NT)
-        g_value = mm3((grads[0][:DV], grads[1][:DV]), weights, NT)
+        g_key = mm(qh, g_scores, NT) + mm(ql, g_scores, NT)
+        g_value = mm(grads[0][:DV], weights, NT) + mm(grads[1][:DV], weights, NT)
         part = mm3(q_feat, grads, NT)
         whole = whole + part
         parts[c] = part
@@ -281,8 +283,10 @@
 
 
 def back_kernel(
-    place, data, states, done, gq, gk, gv, parts, keys, edges, conv, out, columns
+    place, states, done, gq, gk, gv, parts, keys, edges, conv, far, out, columns, data, sem
 ):
+    fetch = pltpu.make_async_copy(far.at[:, AT_V : AT_V + DV], data, sem)
+    fetch.start()
     here = place[0]
     taps = head_taps(conv, columns, place[1])
     count = states.shape[0]
@@ -309,10 +313,10 @@
     after = jnp.concatenate(
         [tile[:, SPARE : SPARE + 2], features_back(edge[F : 2 * F], g_feat)[:, 0:2]], 0
     ) * (here + 1 < count).astype(f32)
-    length = TOK * WIDE
+    fetch.wait()
     for c in reversed(range(H // WIDE)):
         k = keys[c]
-        v = wide_values(rows_of(data, c, AT_V, DV))
+        v = wide_values(rows_of(data, c, 0, DV))
         k_feat = halves(features(k))
         split_state = halves(state)
         g_feat = mm(split_state[0], v, NN) + mm(split_state[1], v, NN)
@@ -345,13 +349,16 @@
     )
 
 
-def weight_kernel(place, grads, data, out, own):
+def weight_kernel(place, grads, far, out, own, data, sem):
+    fetch = pltpu.make_async_copy(far.at[:, 0:HID], data, sem)
+    fetch.start()
     own[...] = stacked(grads, place[1])
     total = jnp.concatenate([stacked(grads, b) for b in range(H)], 1).T
     count, rows = out.shape[:2]
     parts = count * rows // TOK
+    fetch.wait()
     for i in range(parts):
-        at = ROWS + TOK * i
+        at = TOK * i
         tokens = jnp.concatenate([data[b, at : at + TOK] for b in range(H)], 0)
         result = mm(tokens, total, TN).astype(bf16)
         for j in range(count // parts):
@@ -381,11 +388,13 @@
     return pltpu.with_memory_space_constraint(x, pltpu.VMEM)
 
 
-def call(kernel, name, out_shape, *args, scalars=0, final=False, scratch=()):
+def call(kernel, name, out_shape, *args, scalars=0, lazy=0, far=False, scratch=()):
+    whole = pl.BlockSpec(memory_space=pltpu.VMEM)
     specs = [pl.BlockSpec(memory_space=pltpu.SMEM)] * scalars
-    specs += [pl.BlockSpec(memory_space=pltpu.VMEM)] * (len(args) - scalars)
-    outs = jax.tree.map(lambda s: pl.BlockSpec(memory_space=pltpu.VMEM), out_shape)
-    if not final:
+    specs += [whole] * (len(args) - scalars - lazy)
+    specs += [pl.BlockSpec(memory_space=pl.ANY)] * lazy
+    outs = jax.tree.map(lambda s: whole, out_shape)
+    if not far:
         out_shape = jax.tree.map(lambda s: pltpu.VMEM(s.shape, s.dtype), out_shape)
     return pl.pallas_call(
         kernel,
@@ -395,6 +404,10 @@
         out_specs=outs,
         scratch_shapes=scratch,
     )(*args)
+
+
+def window(size):
+    return pltpu.VMEM((H, size, TOK), bf16), pltpu.SemaphoreType.DMA(())
 
 
 def shape(dims, kind):
@@ -416,20 +429,20 @@
     packed = call(
         pack_kernel,
         "pack",
-        shape((H, ROWS + model // H, TOK), bf16),
+        shape((H, ROWS, TOK), bf16),
         tokens,
         qk_weight,
         values[0],
         gate_in[0],
         cotangent[0],
     )
-    data = swap(packed, "g")
+    data = lax.all_to_all(packed, "g", 0, 0, tiled=True)
     own = call(
         state_kernel,
         "state",
         shape((supers, SENT, 2 * DV), bf16),
         place,
-        data,
+        near(data),
         conv_weight,
         scalars=1,
         scratch=taps,
@@ -448,10 +461,11 @@
             shape((supers, SENT, 2 * DV), bf16),
         ),
         place,
-        data,
+        near(data),
         swap(own, SUPER),
         conv_weight,
         scalars=1,
+        far=True,
         scratch=taps,
     )
     back = call(
@@ -459,12 +473,19 @@
         "back",
         shape((H, FIRST + 2 * DV, TOK), bf16),
         place,
+        swap(sent, SUPER),
+        done,
+        gq,
+        gk,
+        gv,
+        parts,
+        keys,
+        edges,
+        conv_weight,
         data,
-        swap(sent, SUPER),
-        *(near(x) for x in (done, gq, gk, gv, parts, keys, edges)),
-        conv_weight,
         scalars=1,
-        scratch=taps,
+        lazy=1,
+        scratch=taps + window(DV),
     )
     back = swap(back, "g")
     partial, own_grad = call(
@@ -478,6 +499,8 @@
         back,
         data,
         scalars=1,
+        lazy=1,
+        scratch=window(HID),
     )
     deep = model // H // others
     some = swap(partial, OTHER)
@@ -496,7 +519,7 @@
         back,
         gate_in[0],
         cotangent[0],
-        final=True,
+        far=True,
     )
     grad_hidden = call(
         hidden_kernel,
@@ -504,7 +527,7 @@
         shape((TOK, model), bf16),
         near(own_grad),
         qk_weight,
-        final=True,
+        far=True,
     )
     return output[None], grad_hidden[None], grad_values[None], grad_gate[None], grad_qk_weight
 

time: 143 us -> 142 us (level)
  local copies, waits for them, and re-layouts: 4.18 us -> 0.97 us
  Pallas kernels: 18.5 us -> 21.1 us
    unnamed x17 -> x3, local copies, waits for them, and re-layouts: 4.18 us -> 0.97 us
    pallas_call x9, Pallas kernels: 18.5 us -> 21.1 us  [call(): pl.pallas_call(kernel, name=name, out_shape=out_shape, in_specs=specs, ou...]
where the time goes in v6:
time: 142 us; the launch traced here: 141 us
  blocking collectives  78.9 us (56%)
  waiting for transfers between devices  24.4 us (17%)
  Pallas kernels  21.1 us (15%)
  starting transfers between devices  14.6 us (10%)
    all_to_all x5, blocking collectives, swap(): return near(lax.all_to_all(x, axis, 0, 0, tiled=True))  78.9 us
    pallas_call x9, Pallas kernels, call(): pl.pallas_call(kernel, name=name, out_shape=out_shape, in_specs=specs, ou...  21.1 us
    all_to_all x1, waiting for transfers between devices, body(): grad_qk_weight = lax.all_to_all(summed, ('g',) + OTHER, 0, 0, tiled=True)  13.3 us
    all_to_all x1, waiting for transfers between devices, body(): data = lax.all_to_all(packed, 'g', 0, 0, tiled=True)  11.1 us
    all_to_all x1, starting transfers between devices, body(): grad_qk_weight = lax.all_to_all(summed, ('g',) + OTHER, 0, 0, tiled=True)  7.45 us
    all_to_all x1, starting transfers between devices, body(): data = lax.all_to_all(packed, 'g', 0, 0, tiled=True)  7.14 us
  transfers between devices with their start and end apart: 2, of which 2 were waited for; matrix products, arithmetic and copies ran while one was open for 0% of the time, Pallas kernels for 3%

profile of v6, /device:TPU:1, one launch (start us, length us, event | category | flops | bytes accessed | tf_op | source)
XLA Modules:
  0.0 141.3 jit_solution(488434628135539393)
XLA Ops:
  0.6 2.8 %pack.1 = bf16[8,416,128]{2,1,0:T(8,128)(2,1)} custom-call(bf16[128,2048]{1,0:T(8,128)(2,1)} %bitcast.13, bf16[2048,256]{1,0:T(8,128)(2,1)} %weight.5, bf16[128,512]{1,0:T(8,128)(2,1)} %bitcast.18, bf16[128,512]{1,0:T(8,128)(2,1)} %bitcast.14, bf16[128,512]{1,0:T(8,128)(2,1)} %bitcast.16), custom_call_target="tpu_custom_call" | custom-call | tf_op jit(solution)/shard_map/pack/pallas_call | solution.py:399
  3.4 7.1 %all-to-all-start = ((bf16[8,416,128]{2,1,0:T(8,128)(2,1)}), bf16[8,416,128]{2,1,0:T(8,128)(2,1)S(1)}, u32[]{:S(2)}, u32[]{:S(2)}) async-start(bf16[8,416,128]{2,1,0:T(8,128)(2,1)} %pack.1), calls=%async_computation | async-start | bytes 1703936 | tf_op jit(solution)/shard_map/all_to_all | solution.py:439
  10.5 0.6 pad_add_fusion.place
  11.2 11.1 %all-to-all-done.data.far = bf16[8,416,128]{2,1,0:T(8,128)(2,1)S(1)} async-done(((bf16[8,416,128]{2,1,0:T(8,128)(2,1)}), bf16[8,416,128]{2,1,0:T(8,128)(2,1)S(1)}, u32[]{:S(2)}, u32[]{:S(2)}) %all-to-all-start) | async-done | bytes 852000 | tf_op jit(solution)/shard_map/all_to_all | solution.py:439
  22.3 0.0 copy-start
  22.3 1.4 state.1
  23.6 23.3 %all_to_all.35.states = bf16[16,96,128]{2,1,0:T(8,128)(2,1)S(1)} all-to-all(bf16[16,96,128]{2,1,0:T(8,128)(2,1)S(1)} %state.1), channel_id=1, replica_groups=mesh['dp'=2,'y'=4,'z'=4,'g'=8] {'y','z'}, dimensions={0} | all-to-all | bytes 786432 | tf_op jit(solution)/shard_map/all_to_all | solution.py:418
  46.9 0.0 copy-done
  46.9 6.2 %main.1 = (bf16[8,64,128]{2,1,0:T(8,128)(2,1)}, f32[4,16,256]{2,1,0:T(8,128)}, f32[4,16,256]{2,1,0:T(8,128)}, f32[4,64,256]{2,1,0:T(8,128)}, f32[4,160,128]{2,1,...) custom-call(s32[2]{0:T(128)} %pad_add_fusion.place, ...), custom_call_target="tpu_custom_call" | custom-call | tf_op jit(solution)/shard_map/main/pallas_call | solution.py:399
  53.2 16.0 %all_to_all.36.states = bf16[16,96,128]{2,1,0:T(8,128)(2,1)S(1)} all-to-all(bf16[16,96,128]{2,1,0:T(8,128)(2,1)} %get-tuple-element.18), channel_id=1, replica_groups=mesh['dp'=2,'y'=4,'z'=4,'g'=8] {'y','z'}, dimensions={0} | all-to-all | bytes 786432 | tf_op jit(solution)/shard_map/all_to_all | solution.py:418
  69.2 3.1 %back.1 = bf16[8,384,128]{2,1,0:T(8,128)(2,1)S(1)} custom-call(s32[2]{0:T(128)} %pad_add_fusion.place, bf16[16,96,128]{2,1,0:T(8,128)(2,1)S(1)} %all_to_all.36.states, bf16[8,64,128]{2,1,0:T(8,128)(2,1)} %get-tuple-element.19.done, f32[4,16,256]{2,1,0:T(8,128)} %get-tuple-element.20.gq, f32[4,16,256]{2,1,0:T(8,128)} %get-tuple-element.21.gk, ...), custom_call_target="tpu_custom_call" | custom-call | tf_op jit(solution)/shard_map/back/pallas_call | solution.py:399
  72.2 22.2 %all_to_all.37.data.grads = bf16[8,384,128]{2,1,0:T(8,128)(2,1)S(1)} all-to-all(bf16[8,384,128]{2,1,0:T(8,128)(2,1)S(1)} %back.1), channel_id=1, replica_groups=mesh['dp'=2,'y'=4,'z'=4,'g'=8] {'g'}, dimensions={0} | all-to-all | bytes 1572864 | tf_op jit(solution)/shard_map/all_to_all | solution.py:418
  94.4 2.2 %weight.4 = (bf16[8,32,256]{2,1,0:T(8,128)(2,1)S(1)}, bf16[256,128]{1,0:T(8,128)(2,1)S(1)}) custom-call(s32[2]{0:T(128)} %pad_add_fusion.place, bf16[8,384,128]{2,1,0:T(8,128)(2,1)S(1)} %all_to_all.37.data.grads, bf16[8,416,128]{2,1,0:T(8,128)(2,1)} %copy-done), custom_call_target="tpu_custom_call" | custom-call | tf_op jit(solution)/shard_map/weight/pallas_call | solution.py:399
  96.7 7.8 %all_to_all.38.data = bf16[8,32,256]{2,1,0:T(8,128)(2,1)S(1)} all-to-all(bf16[8,32,256]{2,1,0:T(8,128)(2,1)S(1)} %get-tuple-element.30), channel_id=1, replica_groups=mesh['dp'=2,'y'=4,'z'=4,'g'=8] {'dp','y'}, dimensions={0} | all-to-all | bytes 262144 | tf_op jit(solution)/shard_map/all_to_all | solution.py:418
  104.5 9.6 %all_to_all.39.data = bf16[4,32,256]{2,1,0:T(8,128)(2,1)S(1)} all-to-all(bf16[4,32,256]{2,1,0:T(8,128)(2,1)S(1)} %sum_a.1), channel_id=1, replica_groups=mesh['dp'=2,'y'=4,'z'=4,'g'=8] {'z'}, dimensions={0} | all-to-all | bytes 131072 | tf_op jit(solution)/shard_map/all_to_all | solution.py:418
  114.1 1.1 sum_b.1
  115.2 7.4 %all-to-all-start.6 = ((bf16[64,32,256]{2,1,0:T(8,128)(2,1)}), bf16[64,32,256]{2,1,0:T(8,128)(2,1)S(1)}, u32[]{:S(2)}, u32[]{:S(2)}) async-start(bf16[64,32,256]{2,1,0:T(8,128)(2,1)} %sum_b.1), calls=%async_computation.6 | async-start | bytes 2097152 | tf_op jit(solution)/shard_map/all_to_all | solution.py:513
  122.7 2.5 %hidden.1 = bf16[128,2048]{1,0:T(8,128)(2,1)} custom-call(bf16[256,128]{1,0:T(8,128)(2,1)S(1)} %get-tuple-element.27.own, bf16[2048,256]{1,0:T(8,128)(2,1)} %weight.5), custom_call_target="tpu_custom_call" | custom-call | tf_op jit(solution)/shard_map/hidden/pallas_call | solution.py:399
  125.1 1.9 %unpack.1 = (bf16[128,512]{1,0:T(8,128)(2,1)}, bf16[128,512]{1,0:T(8,128)(2,1)}, bf16[128,512]{1,0:T(8,128)(2,1)}) custom-call(bf16[8,384,128]{2,1,0:T(8,128)(2,1)S(1)} %all_to_all.37.data.grads, bf16[128,512]{1,0:T(8,128)(2,1)} %bitcast.15, bf16[128,512]{1,0:T(8,128)(2,1)} %bitcast.17), custom_call_target="tpu_custom_call" | custom-call | tf_op jit(solution)/shard_map/unpack/pallas_call | solution.py:399
  127.0 13.3 %all-to-all-done.6 = bf16[64,32,256]{2,1,0:T(8,128)(2,1)S(1)} async-done(((bf16[64,32,256]{2,1,0:T(8,128)(2,1)}), bf16[64,32,256]{2,1,0:T(8,128)(2,1)S(1)}, u32[]{:S(2)}, u32[]{:S(2)}) %all-to-all-start.6) | async-done | bytes 1048608 | tf_op jit(solution)/shard_map/all_to_all | solution.py:513
  140.3 1.0 copy.12
  (1 shorter events, 0.0 us)
Async XLA Ops:
  3.4 18.9 %all-to-all-start = ((bf16[8,416,128]{2,1,0:T(8,128)(2,1)}), bf16[8,416,128]{2,1,0:T(8,128)(2,1)S(1)}, u32[]{:S(2)}, u32[]{:S(2)}) async-start(bf16[8,416,128]{2,1,0:T(8,128)(2,1)} %pack.1), calls=%async_computation | async-start | bytes 1703936 | tf_op jit(solution)/shard_map/all_to_all | solution.py:439
  22.3 24.7 %copy-start = (bf16[8,416,128]{2,1,0:T(8,128)(2,1)}, bf16[8,416,128]{2,1,0:T(8,128)(2,1)S(1)}, u32[]{:S(2)}) copy-start(bf16[8,416,128]{2,1,0:T(8,128)(2,1)S(1)} %all-to-all-done.data.far) | copy-start | bytes 2555908
  115.2 25.1 %all-to-all-start.6 = ((bf16[64,32,256]{2,1,0:T(8,128)(2,1)}), bf16[64,32,256]{2,1,0:T(8,128)(2,1)S(1)}, u32[]{:S(2)}, u32[]{:S(2)}) async-start(bf16[64,32,256]{2,1,0:T(8,128)(2,1)} %sum_b.1), calls=%async_computation.6 | async-start | bytes 2097152 | tf_op jit(solution)/shard_map/all_to_all | solution.py:513

commit v7 on v6

--- a/solution.py
+++ b/solution.py
@@ -13,6 +13,7 @@
 KCONV = 3
 SUPER = ("y", "z")
 OTHER = ("dp", "y")
+GROUP = ("h", "core")
 TOK = 128
 HID = 256
 AT_V, AT_G, AT_P = HID, HID + DV, HID + 2 * DV
@@ -365,6 +366,20 @@
             out[i * (count // parts) + j] = result[rows * j : rows * (j + 1)]
 
 
+def join_kernel(place, mine, theirs, out, sems):
+    core = place[1] % 2
+    copies = []
+    for h in range(H // 2):
+        for i, (part, at) in enumerate(((mine, core), (theirs, 1 - core))):
+            copies.append(
+                pltpu.make_async_copy(part.at[h], out.at[2 * h + at], sems.at[2 * h + i])
+            )
+    for copy in copies:
+        copy.start()
+    for copy in copies:
+        copy.wait()
+
+
 def hidden_kernel(own, weight, out):
     out[...] = mm(own[...].T, weight[...], NT).astype(bf16)
 
@@ -388,12 +403,12 @@
     return pltpu.with_memory_space_constraint(x, pltpu.VMEM)
 
 
-def call(kernel, name, out_shape, *args, scalars=0, lazy=0, far=False, scratch=()):
+def call(kernel, name, out_shape, *args, scalars=0, lazy=0, far=False, results=pltpu.VMEM, scratch=()):
     whole = pl.BlockSpec(memory_space=pltpu.VMEM)
     specs = [pl.BlockSpec(memory_space=pltpu.SMEM)] * scalars
     specs += [whole] * (len(args) - scalars - lazy)
     specs += [pl.BlockSpec(memory_space=pl.ANY)] * lazy
-    outs = jax.tree.map(lambda s: whole, out_shape)
+    outs = jax.tree.map(lambda s: pl.BlockSpec(memory_space=results), out_shape)
     if not far:
         out_shape = jax.tree.map(lambda s: pltpu.VMEM(s.shape, s.dtype), out_shape)
     return pl.pallas_call(
@@ -424,7 +439,7 @@
     others = lax.axis_size(OTHER)
     model = tokens.shape[1]
     chunks, width = H // WIDE, TOK * WIDE
-    place = jnp.stack([lax.axis_index(SUPER), lax.axis_index("g")]).astype(jnp.int32)
+    place = jnp.stack([lax.axis_index(SUPER), lax.axis_index(GROUP)]).astype(jnp.int32)
     taps = (pltpu.VMEM((2 * H * F, 8), f32),)
     packed = call(
         pack_kernel,
@@ -436,7 +451,7 @@
         gate_in[0],
         cotangent[0],
     )
-    data = lax.all_to_all(packed, "g", 0, 0, tiled=True)
+    data = lax.all_to_all(packed, GROUP, 0, 0, tiled=True)
     own = call(
         state_kernel,
         "state",
@@ -487,7 +502,7 @@
         lazy=1,
         scratch=taps + window(DV),
     )
-    back = swap(back, "g")
+    back = swap(back, GROUP)
     partial, own_grad = call(
         weight_kernel,
         "weight",
@@ -508,10 +523,10 @@
         sum_kernel, "sum_a", shape((lax.axis_size("z"), deep, 2 * H * F), bf16), some
     )
     summed = call(
-        sum_kernel, "sum_b", shape((H * others, deep, 2 * H * F), bf16), swap(summed, "z")
-    )
-    grad_qk_weight = lax.all_to_all(summed, ("g",) + OTHER, 0, 0, tiled=True)
-    grad_qk_weight = grad_qk_weight.reshape(model, 2 * H * F)
+        sum_kernel, "sum_b", shape((H // 2 * others, deep, 2 * H * F), bf16), swap(summed, "z")
+    )
+    mine = lax.all_to_all(summed, ("h",) + OTHER, 0, 0, tiled=True)
+    mine = mine.reshape(H // 2, model // H, 2 * H * F)
     output, grad_gate, grad_values = call(
         unpack_kernel,
         "unpack",
@@ -529,6 +544,21 @@
         qk_weight,
         far=True,
     )
+    mine, output, grad_hidden = lax.optimization_barrier((mine, output, grad_hidden))
+    theirs = lax.ppermute(mine, "core", [(0, 1), (1, 0)])
+    grad_qk_weight = call(
+        join_kernel,
+        "join",
+        shape((H, model // H, 2 * H * F), bf16),
+        place,
+        near(mine),
+        near(theirs),
+        scalars=1,
+        lazy=2,
+        far=True,
+        results=pl.ANY,
+        scratch=(pltpu.SemaphoreType.DMA((H,)),),
+    ).reshape(model, 2 * H * F)
     return output[None], grad_hidden[None], grad_values[None], grad_gate[None], grad_qk_weight
 
 
@@ -536,9 +566,10 @@
     pairs, blocks = mesh.devices.shape
     y = 4 if blocks // H % 4 == 0 else 1
     fine = Mesh(
-        mesh.devices.reshape(pairs, y, blocks // H // y, H), ("dp", "y", "z", "g")
-    )
-    split = P("dp", ("y", "z", "g"), None)
+        mesh.devices.reshape(pairs, y, blocks // H // y, H // 2, 2),
+        ("dp", "y", "z", "h", "core"),
+    )
+    split = P("dp", SUPER + GROUP, None)
     return jax.shard_map(
         body,
         mesh=fine,

time: 142 us -> 136 us (0.958)
  waiting for transfers between devices: 24.4 us -> 17.3 us
  Pallas kernels: 21.1 us -> 22.6 us
    all_to_all x2, waiting for transfers between devices: 24.4 us -> 15.7 us  [the longest x1 11.1 us: body(): data = lax.all_to_all(packed, GROUP, 0, 0, tiled=True)]
    ppermute x0 -> x1, starting transfers between devices: none -> 4.51 us  [body(): theirs = lax.ppermute(mine, 'core', [(0, 1), (1, 0)])]
    all_to_all x2, starting transfers between devices: 14.6 us -> 11 us  [the longest x1 7.14 us: body(): data = lax.all_to_all(packed, GROUP, 0, 0, tiled=True)]
    ppermute x0 -> x1, waiting for transfers between devices: none -> 1.54 us  [body(): theirs = lax.ppermute(mine, 'core', [(0, 1), (1, 0)])]
    pallas_call x9 -> x10, Pallas kernels: 21.1 us -> 22.6 us  [call(): pl.pallas_call(kernel, name=name, out_shape=out_shape, in_specs=specs, ou...]
  transfers between devices with their start and end apart: 2 -> 3, of which waited for: 2 -> 3; matrix products, arithmetic and copies ran while one was open for 0% -> 0% of each run, Pallas kernels for 3% -> 3%
where the time goes in v7:
time: 136 us
  blocking collectives  78.9 us (58%)
  Pallas kernels  22.6 us (17%)
  waiting for transfers between devices  17.3 us (13%)
  starting transfers between devices  15.5 us (11%)
    all_to_all x5, blocking collectives, swap(): return near(lax.all_to_all(x, axis, 0, 0, tiled=True))  78.9 us
    pallas_call x10, Pallas kernels, call(): pl.pallas_call(kernel, name=name, out_shape=out_shape, in_specs=specs, ou...  22.6 us
    all_to_all x1, waiting for transfers between devices, body(): data = lax.all_to_all(packed, GROUP, 0, 0, tiled=True)  11.1 us
    all_to_all x1, starting transfers between devices, body(): data = lax.all_to_all(packed, GROUP, 0, 0, tiled=True)  7.14 us
    all_to_all x1, waiting for transfers between devices, body(): mine = lax.all_to_all(summed, ('h',) + OTHER, 0, 0, tiled=True)  4.62 us
    ppermute x1, starting transfers between devices, body(): theirs = lax.ppermute(mine, 'core', [(0, 1), (1, 0)])  4.51 us
    all_to_all x1, starting transfers between devices, body(): mine = lax.all_to_all(summed, ('h',) + OTHER, 0, 0, tiled=True)  3.89 us
  transfers between devices with their start and end apart: 3, of which 3 were waited for; matrix products, arithmetic and copies ran while one was open for 0% of the time, Pallas kernels for 3%

profile of v7, /device:TPU:1, one launch (start us, length us, event | category | flops | bytes accessed | tf_op | source)
XLA Modules:
  0.0 135.6 jit_solution(12516284340915667645)
XLA Ops:
  0.6 2.8 %pack.1 = bf16[8,416,128]{2,1,0:T(8,128)(2,1)} custom-call(bf16[128,2048]{1,0:T(8,128)(2,1)} %bitcast.16, bf16[2048,256]{1,0:T(8,128)(2,1)} %weight.5, bf16[128,512]{1,0:T(8,128)(2,1)} %bitcast.21, bf16[128,512]{1,0:T(8,128)(2,1)} %bitcast.17, bf16[128,512]{1,0:T(8,128)(2,1)} %bitcast.19), custom_call_target="tpu_custom_call" | custom-call | tf_op jit(solution)/shard_map/pack/pallas_call | solution.py:414
  3.4 7.1 %all-to-all-start = ((bf16[8,416,128]{2,1,0:T(8,128)(2,1)}), bf16[8,416,128]{2,1,0:T(8,128)(2,1)S(1)}, u32[]{:S(2)}, u32[]{:S(2)}) async-start(bf16[8,416,128]{2,1,0:T(8,128)(2,1)} %pack.1), calls=%async_computation | async-start | bytes 1703936 | tf_op jit(solution)/shard_map/all_to_all | solution.py:454
  10.5 0.6 pad_add_fusion.place
  11.1 11.1 %all-to-all-done.data.far = bf16[8,416,128]{2,1,0:T(8,128)(2,1)S(1)} async-done(((bf16[8,416,128]{2,1,0:T(8,128)(2,1)}), bf16[8,416,128]{2,1,0:T(8,128)(2,1)S(1)}, u32[]{:S(2)}, u32[]{:S(2)}) %all-to-all-start) | async-done | bytes 852000 | tf_op jit(solution)/shard_map/all_to_all | solution.py:454
  22.3 0.0 copy-start
  22.3 1.4 %state.1 = bf16[16,96,128]{2,1,0:T(8,128)(2,1)S(1)} custom-call(s32[2]{0:T(128)} %pad_add_fusion.place, bf16[8,416,128]{2,1,0:T(8,128)(2,1)S(1)} %all-to-all-done.data.far, f32[3,256]{1,0:T(4,128)} %conv.5), custom_call_target="tpu_custom_call" | custom-call | tf_op jit(solution)/shard_map/state/pallas_call | solution.py:414
  23.6 23.3 %all_to_all.35.states = bf16[16,96,128]{2,1,0:T(8,128)(2,1)S(1)} all-to-all(bf16[16,96,128]{2,1,0:T(8,128)(2,1)S(1)} %state.1), channel_id=1, replica_groups=mesh['dp'=2,'y'=4,'z'=4,'h'=4,'core'=2] {'y','z'}, dimensions={0} | all-to-all | bytes 786432 | tf_op jit(solution)/shard_map/all_to_all | solution.py:433
  46.9 0.0 copy-done
  46.9 6.2 %main.1 = (bf16[8,64,128]{2,1,0:T(8,128)(2,1)}, f32[4,16,256]{2,1,0:T(8,128)}, f32[4,16,256]{2,1,0:T(8,128)}, f32[4,64,256]{2,1,0:T(8,128)}, f32[4,160,128]{2,1,...) custom-call(s32[2]{0:T(128)} %pad_add_fusion.place, ...), custom_call_target="tpu_custom_call" | custom-call | tf_op jit(solution)/shard_map/main/pallas_call | solution.py:414
  53.2 16.0 %all_to_all.36.states = bf16[16,96,128]{2,1,0:T(8,128)(2,1)S(1)} all-to-all(bf16[16,96,128]{2,1,0:T(8,128)(2,1)} %get-tuple-element.21), channel_id=1, replica_groups=mesh['dp'=2,'y'=4,'z'=4,'h'=4,'core'=2] {'y','z'}, dimensions={0} | all-to-all | bytes 786432 | tf_op jit(solution)/shard_map/all_to_all | solution.py:433
  69.2 3.1 %back.1 = bf16[8,384,128]{2,1,0:T(8,128)(2,1)S(1)} custom-call(s32[2]{0:T(128)} %pad_add_fusion.place, bf16[16,96,128]{2,1,0:T(8,128)(2,1)S(1)} %all_to_all.36.states, bf16[8,64,128]{2,1,0:T(8,128)(2,1)} %get-tuple-element.22.done, f32[4,16,256]{2,1,0:T(8,128)} %get-tuple-element.23.gq, f32[4,16,256]{2,1,0:T(8,128)} %get-tuple-element.24.gk, ...), custom_call_target="tpu_custom_call" | custom-call | tf_op jit(solution)/shard_map/back/pallas_call | solution.py:414
  72.2 22.2 %all_to_all.37.grads.data = bf16[8,384,128]{2,1,0:T(8,128)(2,1)S(1)} all-to-all(bf16[8,384,128]{2,1,0:T(8,128)(2,1)S(1)} %back.1), channel_id=1, replica_groups=mesh['dp'=2,'y'=4,'z'=4,'h'=4,'core'=2] {'h','core'}, dimensions={0} | all-to-all | bytes 1572864 | tf_op jit(solution)/shard_map/all_to_all | solution.py:433
  94.4 2.2 %weight.4 = (bf16[8,32,256]{2,1,0:T(8,128)(2,1)S(1)}, bf16[256,128]{1,0:T(8,128)(2,1)S(1)}) custom-call(s32[2]{0:T(128)} %pad_add_fusion.place, bf16[8,384,128]{2,1,0:T(8,128)(2,1)S(1)} %all_to_all.37.grads.data, bf16[8,416,128]{2,1,0:T(8,128)(2,1)} %copy-done), custom_call_target="tpu_custom_call" | custom-call | tf_op jit(solution)/shard_map/weight/pallas_call | solution.py:414
  96.7 7.8 %all_to_all.38.data = bf16[8,32,256]{2,1,0:T(8,128)(2,1)S(1)} all-to-all(bf16[8,32,256]{2,1,0:T(8,128)(2,1)S(1)} %get-tuple-element.29), channel_id=1, replica_groups=mesh['dp'=2,'y'=4,'z'=4,'h'=4,'core'=2] {'dp','y'}, dimensions={0} | all-to-all | bytes 262144 | tf_op jit(solution)/shard_map/all_to_all | solution.py:433
  104.5 9.6 %all_to_all.39.data = bf16[4,32,256]{2,1,0:T(8,128)(2,1)S(1)} all-to-all(bf16[4,32,256]{2,1,0:T(8,128)(2,1)S(1)} %sum_a.1), channel_id=1, replica_groups=mesh['dp'=2,'y'=4,'z'=4,'h'=4,'core'=2] {'z'}, dimensions={0} | all-to-all | bytes 131072 | tf_op jit(solution)/shard_map/all_to_all | solution.py:433
  114.1 0.9 sum_b.1
  115.0 3.9 %all-to-all-start.6 = ((bf16[32,32,256]{2,1,0:T(8,128)(2,1)}), bf16[32,32,256]{2,1,0:T(8,128)(2,1)S(1)}, u32[]{:S(2)}, u32[]{:S(2)}) async-start(bf16[32,32,256]{2,1,0:T(8,128)(2,1)} %sum_b.1), calls=%async_computation.6 | async-start | bytes 1048576 | tf_op jit(solution)/shard_map/all_to_all | solution.py:528
  118.9 2.5 %hidden.1 = bf16[128,2048]{1,0:T(8,128)(2,1)} custom-call(bf16[256,128]{1,0:T(8,128)(2,1)S(1)} %get-tuple-element.31.own, bf16[2048,256]{1,0:T(8,128)(2,1)} %weight.5), custom_call_target="tpu_custom_call" | custom-call | tf_op jit(solution)/shard_map/hidden/pallas_call | solution.py:414
  121.4 1.9 %unpack.1 = (bf16[128,512]{1,0:T(8,128)(2,1)}, bf16[128,512]{1,0:T(8,128)(2,1)}, bf16[128,512]{1,0:T(8,128)(2,1)}) custom-call(bf16[8,384,128]{2,1,0:T(8,128)(2,1)S(1)} %all_to_all.37.grads.data, bf16[128,512]{1,0:T(8,128)(2,1)} %bitcast.18, bf16[128,512]{1,0:T(8,128)(2,1)} %bitcast.20), custom_call_target="tpu_custom_call" | custom-call | tf_op jit(solution)/shard_map/unpack/pallas_call | solution.py:414
  123.2 4.6 %all-to-all-done.6 = bf16[32,32,256]{2,1,0:T(8,128)(2,1)S(1)} async-done(((bf16[32,32,256]{2,1,0:T(8,128)(2,1)}), bf16[32,32,256]{2,1,0:T(8,128)(2,1)S(1)}, u32[]{:S(2)}, u32[]{:S(2)}) %all-to-all-start.6) | async-done | bytes 524320 | tf_op jit(solution)/shard_map/all_to_all | solution.py:528
  127.8 4.5 %collective-permute-start = (bf16[4,256,256]{2,1,0:T(8,128)(2,1)S(1)}, bf16[4,256,256]{2,1,0:T(8,128)(2,1)S(1)}, u32[]{:S(2)}, u32[]{:S(2)}) collective-permute-start(bf16[4,256,256]{2,1,0:T(8,128)(2,1)S(1)} %bitcast.12), channel_id=1, source_target_pairs={{0,1},{1,0},{2,3},{3,2},{4,5},{5,4},{6,7},{7,6},{8,9},{9,8},{10,11... | collective-permute-start | bytes 1572872 | tf_op jit(solution)/shard_map/ppermute | solution.py:548
  132.4 1.5 %collective-permute-done.theirs = bf16[4,256,256]{2,1,0:T(8,128)(2,1)S(1)} collective-permute-done((bf16[4,256,256]{2,1,0:T(8,128)(2,1)S(1)}, bf16[4,256,256]{2,1,0:T(8,128)(2,1)S(1)}, u32[]{:S(2)}, u32[]{:S(2)}) %collective-permute-start) | collective-permute-done | bytes 524320 | tf_op jit(solution)/shard_map/ppermute | solution.py:548
  133.9 1.7 %join.1 = bf16[8,256,256]{2,1,0:T(8,128)(2,1)} custom-call(s32[2]{0:T(128)} %pad_add_fusion.place, bf16[4,256,256]{2,1,0:T(8,128)(2,1)S(1)} %bitcast.13, bf16[4,256,256]{2,1,0:T(8,128)(2,1)S(1)} %collective-permute-done.theirs), custom_call_target="tpu_custom_call" | custom-call | tf_op jit(solution)/shard_map/join/pallas_call | solution.py:414
  (1 shorter events, 0.0 us)
Async XLA Ops:
  3.4 18.9 %all-to-all-start = ((bf16[8,416,128]{2,1,0:T(8,128)(2,1)}), bf16[8,416,128]{2,1,0:T(8,128)(2,1)S(1)}, u32[]{:S(2)}, u32[]{:S(2)}) async-start(bf16[8,416,128]{2,1,0:T(8,128)(2,1)} %pack.1), calls=%async_computation | async-start | bytes 1703936 | tf_op jit(solution)/shard_map/all_to_all | solution.py:454
  22.3 24.7 %copy-start = (bf16[8,416,128]{2,1,0:T(8,128)(2,1)}, bf16[8,416,128]{2,1,0:T(8,128)(2,1)S(1)}, u32[]{:S(2)}) copy-start(bf16[8,416,128]{2,1,0:T(8,128)(2,1)S(1)} %all-to-all-done.data.far) | copy-start | bytes 2555908
  115.0 12.9 %all-to-all-start.6 = ((bf16[32,32,256]{2,1,0:T(8,128)(2,1)}), bf16[32,32,256]{2,1,0:T(8,128)(2,1)S(1)}, u32[]{:S(2)}, u32[]{:S(2)}) async-start(bf16[32,32,256]{2,1,0:T(8,128)(2,1)} %sum_b.1), calls=%async_computation.6 | async-start | bytes 1048576 | tf_op jit(solution)/shard_map/all_to_all | solution.py:528
  127.8 6.0 %collective-permute-start = (bf16[4,256,256]{2,1,0:T(8,128)(2,1)S(1)}, bf16[4,256,256]{2,1,0:T(8,128)(2,1)S(1)}, u32[]{:S(2)}, u32[]{:S(2)}) collective-permute-start(bf16[4,256,256]{2,1,0:T(8,128)(2,1)S(1)} %bitcast.12), channel_id=1, source_target_pairs={{0,1},{1,0},{2,3},{3,2},{4,5},{5,4},{6,7},{7,6},{8,9},{9,8},{10,11... | collective-permute-start | bytes 1572872 | tf_op jit(solution)/shard_map/ppermute | solution.py:548

commit v8 on v7

--- a/solution.py
+++ b/solution.py
@@ -37,11 +37,6 @@
 def halves(x):
     high = x.astype(bf16)
     return high, (x - high.astype(f32)).astype(bf16)
-
-
-def mm3(a, b, dims):
-    (ah, al), (bh, bl) = a, b
-    return mm(ah, bh, dims) + (mm(ah, bl, dims) + mm(al, bh, dims))
 
 
 def feature_scale(d):
@@ -206,7 +201,7 @@
     repeat_into(out, pack_state(total, extra))
 
 
-def main_kernel(place, data, states, conv, out, gq, gk, gv, parts, keys, edges, sent, columns):
+def main_kernel(place, data, states, conv, out, saved, parts, edges, sent, columns):
     here = place[0]
     taps = head_taps(conv, columns, place[1])
     length = TOK * WIDE
@@ -240,16 +235,16 @@
         before = raw[:, -2:]
         q, k = mixed[:F], mixed[F:]
         (qh, ql), (kh, kl) = halves(q * F**-0.5), halves(k)
-        keys[c] = k
+        saved[c, 2 * F : 3 * F] = k
         v = wide_values(rows_of(data, c, AT_V, DV))
         g_att = rows_of(data, c, AT_G, DV).astype(f32)
         near_one = 1.0 + mm(
             jnp.concatenate([kh, kh, kl], 0), jnp.concatenate([qh, ql, qh], 0), TN
         )
         weights = jnp.where(causal, 0.5 + 0.5 * near_one * near_one, 0.0).astype(bf16)
-        q_feat, k_feat = halves(features(q)), halves(features(k))
-        split_state = halves(state)
-        numer = mm(v, weights, NN) + mm3(split_state, q_feat, TN)
+        q_feat, k_feat = features(q).astype(bf16), features(k).astype(bf16)
+        held = state.astype(bf16)
+        numer = mm(v, weights, NN) + mm(held, q_feat, TN)
         inverse = 1.0 / numer[DV : DV + 1]
         attended = numer[:DV] * inverse
         result = attended.astype(bf16)
@@ -261,7 +256,7 @@
         g_weights = mm(v, grads[0], TN) + mm(v, grads[1], TN)
         g_scores = jnp.where(causal, g_weights * near_one, 0.0).astype(bf16)
         g_local = (mm(kh, g_scores, NN) + mm(kl, g_scores, NN)) * F**-0.5
-        g_query = g_local + features_back(q, mm3(split_state, grads, NN))
+        g_query = g_local + features_back(q, mm(held, grads[0], NN))
         if c == 0:
             extra = [g_query[:, 0:1], g_query[:, 1:2]]
             for j in range(DV // F + 1):
@@ -270,21 +265,21 @@
                 extra += [high, column - high.astype(f32)]
         g_key = mm(qh, g_scores, NT) + mm(ql, g_scores, NT)
         g_value = mm(grads[0][:DV], weights, NT) + mm(grads[1][:DV], weights, NT)
-        part = mm3(q_feat, grads, NT)
+        part = mm(q_feat, grads[0], NT)
         whole = whole + part
-        parts[c] = part
-        state = state + (mm(k_feat[0], v, NT) + mm(k_feat[1], v, NT))
+        parts[c] = part.astype(bf16)
+        state = state + mm(k_feat, v, NT)
         for i in range(WIDE):
             cols = slice(TOK * i, TOK * (i + 1))
             out[WIDE * c + i] = result[:, cols]
-        gq[c] = g_query
-        gk[c] = g_key
-        gv[c] = g_value
+        saved[c, 0:F] = g_query
+        saved[c, F : 2 * F] = g_key
+        saved[c, 3 * F :] = g_value
     repeat_into(sent, pack_state(whole, extra))
 
 
 def back_kernel(
-    place, states, done, gq, gk, gv, parts, keys, edges, conv, far, out, columns, data, sem
+    place, states, done, saved, parts, edges, conv, far, out, columns, data, sem
 ):
     fetch = pltpu.make_async_copy(far.at[:, AT_V : AT_V + DV], data, sem)
     fetch.start()
@@ -316,15 +311,14 @@
     ) * (here + 1 < count).astype(f32)
     fetch.wait()
     for c in reversed(range(H // WIDE)):
-        k = keys[c]
+        k = saved[c, 2 * F : 3 * F]
         v = wide_values(rows_of(data, c, 0, DV))
-        k_feat = halves(features(k))
-        split_state = halves(state)
-        g_feat = mm(split_state[0], v, NN) + mm(split_state[1], v, NN)
-        g_key = gk[c] + features_back(k, g_feat)
-        g_value = (gv[c] + mm3(split_state, k_feat, TN)[:DV]).astype(bf16)
-        state = state + parts[c]
-        now = jnp.concatenate([gq[c], g_key], 0)
+        k_feat = features(k).astype(bf16)
+        held = state.astype(bf16)
+        g_key = saved[c, F : 2 * F] + features_back(k, mm(held, v, NN))
+        g_value = (saved[c, 3 * F :] + mm(held, k_feat, TN)[:DV]).astype(bf16)
+        state = state + parts[c].astype(f32)
+        now = jnp.concatenate([saved[c, 0:F], g_key], 0)
         total = (
             taps[:, 0:1] * now
             + taps[:, 1:2] * jnp.concatenate([now[:, 1:], after[:, 0:1]], 1)
@@ -462,18 +456,15 @@
         scalars=1,
         scratch=taps,
     )
-    done, gq, gk, gv, parts, keys, edges, sent = call(
+    done, saved, parts, edges, sent = call(
         main_kernel,
         "main",
         (
             shape((H, DV, TOK), bf16),
-            shape((chunks, F, width), f32),
-            shape((chunks, F, width), f32),
-            shape((chunks, DV, width), f32),
-            shape((chunks, FEAT, 2 * DV), f32),
-            shape((chunks, F, width), f32),
+            shape((chunks, 3 * F + DV, width), f32),
+            shape((chunks, FEAT, 2 * DV), bf16),
             shape((2 * F + DV, 2 * DV), f32),
-            shape((supers, SENT, 2 * DV), bf16),
+            pltpu.VMEM((supers, SENT, 2 * DV), bf16),
         ),
         place,
         near(data),
@@ -490,11 +481,8 @@
         place,
         swap(sent, SUPER),
         done,
-        gq,
-        gk,
-        gv,
+        saved,
         parts,
-        keys,
         edges,
         conv_weight,
         data,

time: 136 us -> 136 us (level)
  no operation moved by 1% of the time
where the time goes in v8:
time: 136 us; the launch traced here: 135 us
  blocking collectives  78.7 us (58%)
  Pallas kernels  21.6 us (16%)
  waiting for transfers between devices  17.2 us (13%)
  starting transfers between devices  16.3 us (12%)
    all_to_all x5, blocking collectives, swap(): return near(lax.all_to_all(x, axis, 0, 0, tiled=True))  78.7 us
    pallas_call x10, Pallas kernels, call(): pl.pallas_call(kernel, name=name, out_shape=out_shape, in_specs=specs, ou...  21.6 us
    all_to_all x1, waiting for transfers between devices, body(): data = lax.all_to_all(packed, GROUP, 0, 0, tiled=True)  11.1 us
    all_to_all x1, starting transfers between devices, body(): data = lax.all_to_all(packed, GROUP, 0, 0, tiled=True)  7.14 us
    ppermute x1, starting transfers between devices, body(): theirs = lax.ppermute(mine, 'core', [(0, 1), (1, 0)])  5.14 us
    all_to_all x1, waiting for transfers between devices, body(): mine = lax.all_to_all(summed, ('h',) + OTHER, 0, 0, tiled=True)  4.59 us
    all_to_all x1, starting transfers between devices, body(): mine = lax.all_to_all(summed, ('h',) + OTHER, 0, 0, tiled=True)  4.05 us
  transfers between devices with their start and end apart: 3, of which 3 were waited for; matrix products, arithmetic and copies ran while one was open for 0% of the time, Pallas kernels for 3%

profile of v8, /device:TPU:1, one launch (start us, length us, event | category | flops | bytes accessed | tf_op | source)
XLA Modules:
  0.0 135.1 jit_solution(3939588793058199452)
XLA Ops:
  0.6 2.8 %pack.1 = bf16[8,416,128]{2,1,0:T(8,128)(2,1)} custom-call(bf16[128,2048]{1,0:T(8,128)(2,1)} %bitcast.16, bf16[2048,256]{1,0:T(8,128)(2,1)} %weight.5, bf16[128,512]{1,0:T(8,128)(2,1)} %bitcast.21, bf16[128,512]{1,0:T(8,128)(2,1)} %bitcast.17, bf16[128,512]{1,0:T(8,128)(2,1)} %bitcast.19), custom_call_target="tpu_custom_call" | custom-call | tf_op jit(solution)/shard_map/pack/pallas_call | solution.py:408
  3.4 7.1 %all-to-all-start = ((bf16[8,416,128]{2,1,0:T(8,128)(2,1)}), bf16[8,416,128]{2,1,0:T(8,128)(2,1)S(1)}, u32[]{:S(2)}, u32[]{:S(2)}) async-start(bf16[8,416,128]{2,1,0:T(8,128)(2,1)} %pack.1), calls=%async_computation | async-start | bytes 1703936 | tf_op jit(solution)/shard_map/all_to_all | solution.py:448
  10.5 0.7 pad_add_fusion.place
  11.2 11.1 %all-to-all-done.data.far = bf16[8,416,128]{2,1,0:T(8,128)(2,1)S(1)} async-done(((bf16[8,416,128]{2,1,0:T(8,128)(2,1)}), bf16[8,416,128]{2,1,0:T(8,128)(2,1)S(1)}, u32[]{:S(2)}, u32[]{:S(2)}) %all-to-all-start) | async-done | bytes 852000 | tf_op jit(solution)/shard_map/all_to_all | solution.py:448
  22.3 0.0 copy-start
  22.3 1.4 %state.1 = bf16[16,96,128]{2,1,0:T(8,128)(2,1)S(1)} custom-call(s32[2]{0:T(128)} %pad_add_fusion.place, bf16[8,416,128]{2,1,0:T(8,128)(2,1)S(1)} %all-to-all-done.data.far, f32[3,256]{1,0:T(4,128)} %conv.5), custom_call_target="tpu_custom_call" | custom-call | tf_op jit(solution)/shard_map/state/pallas_call | solution.py:408
  23.6 23.3 %all_to_all.35.states = bf16[16,96,128]{2,1,0:T(8,128)(2,1)S(1)} all-to-all(bf16[16,96,128]{2,1,0:T(8,128)(2,1)S(1)} %state.1), channel_id=1, replica_groups=mesh['dp'=2,'y'=4,'z'=4,'h'=4,'core'=2] {'y','z'}, dimensions={0} | all-to-all | bytes 786432 | tf_op jit(solution)/shard_map/all_to_all | solution.py:427
  46.9 0.0 copy-done
  46.9 5.6 %main.1 = (bf16[8,64,128]{2,1,0:T(8,128)(2,1)}, f32[4,112,256]{2,1,0:T(8,128)}, bf16[4,160,128]{2,1,0:T(8,128)(2,1)}, f32[96,128]{1,0:T(8,128)}, bf16[16,96,128]{2,1,0:T(8,128)(2,1)S(1)}) custom-call(s32[2]{0:T(128)} %pad_add_fusion.place, bf16[8,416,128]{2,1,0:T(8,128)(2,1)S(1)} %all-to-all-done.data.far, bf16[16,96,128]{2,1,0:T(8,128)(2,1)S(1)} %all_to_all.35.states, ...), custom_call_target="tpu_custom_call" | custom-call | tf_op jit(solution)/shard_map/main/pallas_call | solution.py:408
  52.5 15.2 %all_to_all.36.states = bf16[16,96,128]{2,1,0:T(8,128)(2,1)S(1)} all-to-all(bf16[16,96,128]{2,1,0:T(8,128)(2,1)S(1)} %get-tuple-element.18), channel_id=1, replica_groups=mesh['dp'=2,'y'=4,'z'=4,'h'=4,'core'=2] {'y','z'}, dimensions={0} | all-to-all | bytes 786432 | tf_op jit(solution)/shard_map/all_to_all | solution.py:427
  67.7 2.7 %back.1 = bf16[8,384,128]{2,1,0:T(8,128)(2,1)S(1)} custom-call(s32[2]{0:T(128)} %pad_add_fusion.place, bf16[16,96,128]{2,1,0:T(8,128)(2,1)S(1)} %all_to_all.36.states, bf16[8,64,128]{2,1,0:T(8,128)(2,1)} %get-tuple-element.19.done, f32[4,112,256]{2,1,0:T(8,128)} %get-tuple-element.20.saved, bf16[4,160,128]{2,1,0:T(8,128)(2,1)} %get-tuple-element.21.parts, ...), custom_call_target="tpu_custom_call" | custom-call | tf_op jit(solution)/shard_map/back/pallas_call | solution.py:408
  70.4 22.1 %all_to_all.37.grads.data = bf16[8,384,128]{2,1,0:T(8,128)(2,1)S(1)} all-to-all(bf16[8,384,128]{2,1,0:T(8,128)(2,1)S(1)} %back.1), channel_id=1, replica_groups=mesh['dp'=2,'y'=4,'z'=4,'h'=4,'core'=2] {'h','core'}, dimensions={0} | all-to-all | bytes 1572864 | tf_op jit(solution)/shard_map/all_to_all | solution.py:427
  92.5 2.2 %weight.4 = (bf16[8,32,256]{2,1,0:T(8,128)(2,1)S(1)}, bf16[256,128]{1,0:T(8,128)(2,1)S(1)}) custom-call(s32[2]{0:T(128)} %pad_add_fusion.place, bf16[8,384,128]{2,1,0:T(8,128)(2,1)S(1)} %all_to_all.37.grads.data, bf16[8,416,128]{2,1,0:T(8,128)(2,1)} %copy-done), custom_call_target="tpu_custom_call" | custom-call | tf_op jit(solution)/shard_map/weight/pallas_call | solution.py:408
  94.7 7.8 %all_to_all.38.data = bf16[8,32,256]{2,1,0:T(8,128)(2,1)S(1)} all-to-all(bf16[8,32,256]{2,1,0:T(8,128)(2,1)S(1)} %get-tuple-element.23), channel_id=1, replica_groups=mesh['dp'=2,'y'=4,'z'=4,'h'=4,'core'=2] {'dp','y'}, dimensions={0} | all-to-all | bytes 262144 | tf_op jit(solution)/shard_map/all_to_all | solution.py:427
  102.6 10.3 %all_to_all.39.data = bf16[4,32,256]{2,1,0:T(8,128)(2,1)S(1)} all-to-all(bf16[4,32,256]{2,1,0:T(8,128)(2,1)S(1)} %sum_a.1), channel_id=1, replica_groups=mesh['dp'=2,'y'=4,'z'=4,'h'=4,'core'=2] {'z'}, dimensions={0} | all-to-all | bytes 131072 | tf_op jit(solution)/shard_map/all_to_all | solution.py:427
  112.9 0.9 sum_b.1
  113.7 4.1 %all-to-all-start.6 = ((bf16[32,32,256]{2,1,0:T(8,128)(2,1)}), bf16[32,32,256]{2,1,0:T(8,128)(2,1)S(1)}, u32[]{:S(2)}, u32[]{:S(2)}) async-start(bf16[32,32,256]{2,1,0:T(8,128)(2,1)} %sum_b.1), calls=%async_computation.6 | async-start | bytes 1048576 | tf_op jit(solution)/shard_map/all_to_all | solution.py:516
  117.8 2.5 %hidden.1 = bf16[128,2048]{1,0:T(8,128)(2,1)} custom-call(bf16[256,128]{1,0:T(8,128)(2,1)S(1)} %get-tuple-element.25.own, bf16[2048,256]{1,0:T(8,128)(2,1)} %weight.5), custom_call_target="tpu_custom_call" | custom-call | tf_op jit(solution)/shard_map/hidden/pallas_call | solution.py:408
  120.3 1.9 %unpack.1 = (bf16[128,512]{1,0:T(8,128)(2,1)}, bf16[128,512]{1,0:T(8,128)(2,1)}, bf16[128,512]{1,0:T(8,128)(2,1)}) custom-call(bf16[8,384,128]{2,1,0:T(8,128)(2,1)S(1)} %all_to_all.37.grads.data, bf16[128,512]{1,0:T(8,128)(2,1)} %bitcast.18, bf16[128,512]{1,0:T(8,128)(2,1)} %bitcast.20), custom_call_target="tpu_custom_call" | custom-call | tf_op jit(solution)/shard_map/unpack/pallas_call | solution.py:408
  122.2 4.6 %all-to-all-done.6 = bf16[32,32,256]{2,1,0:T(8,128)(2,1)S(1)} async-done(((bf16[32,32,256]{2,1,0:T(8,128)(2,1)}), bf16[32,32,256]{2,1,0:T(8,128)(2,1)S(1)}, u32[]{:S(2)}, u32[]{:S(2)}) %all-to-all-start.6) | async-done | bytes 524320 | tf_op jit(solution)/shard_map/all_to_all | solution.py:516
  126.8 5.1 %collective-permute-start = (bf16[4,256,256]{2,1,0:T(8,128)(2,1)S(1)}, bf16[4,256,256]{2,1,0:T(8,128)(2,1)S(1)}, u32[]{:S(2)}, u32[]{:S(2)}) collective-permute-start(bf16[4,256,256]{2,1,0:T(8,128)(2,1)S(1)} %bitcast.12), channel_id=1, source_target_pairs={{0,1},{1,0},{2,3},{3,2},{4,5},{5,4},{6,7},{7,6},{8,9},{9,8},{10,11... | collective-permute-start | bytes 1572872 | tf_op jit(solution)/shard_map/ppermute | solution.py:536
  131.9 1.5 %collective-permute-done.theirs = bf16[4,256,256]{2,1,0:T(8,128)(2,1)S(1)} collective-permute-done((bf16[4,256,256]{2,1,0:T(8,128)(2,1)S(1)}, bf16[4,256,256]{2,1,0:T(8,128)(2,1)S(1)}, u32[]{:S(2)}, u32[]{:S(2)}) %collective-permute-start) | collective-permute-done | bytes 524320 | tf_op jit(solution)/shard_map/ppermute | solution.py:536
  133.4 1.7 %join.1 = bf16[8,256,256]{2,1,0:T(8,128)(2,1)} custom-call(s32[2]{0:T(128)} %pad_add_fusion.place, bf16[4,256,256]{2,1,0:T(8,128)(2,1)S(1)} %bitcast.13, bf16[4,256,256]{2,1,0:T(8,128)(2,1)S(1)} %collective-permute-done.theirs), custom_call_target="tpu_custom_call" | custom-call | tf_op jit(solution)/shard_map/join/pallas_call | solution.py:408
  (1 shorter events, 0.0 us)
Async XLA Ops:
  3.4 18.9 %all-to-all-start = ((bf16[8,416,128]{2,1,0:T(8,128)(2,1)}), bf16[8,416,128]{2,1,0:T(8,128)(2,1)S(1)}, u32[]{:S(2)}, u32[]{:S(2)}) async-start(bf16[8,416,128]{2,1,0:T(8,128)(2,1)} %pack.1), calls=%async_computation | async-start | bytes 1703936 | tf_op jit(solution)/shard_map/all_to_all | solution.py:448
  22.3 24.7 %copy-start = (bf16[8,416,128]{2,1,0:T(8,128)(2,1)}, bf16[8,416,128]{2,1,0:T(8,128)(2,1)S(1)}, u32[]{:S(2)}) copy-start(bf16[8,416,128]{2,1,0:T(8,128)(2,1)S(1)} %all-to-all-done.data.far) | copy-start | bytes 2555908
  113.7 13.0 %all-to-all-start.6 = ((bf16[32,32,256]{2,1,0:T(8,128)(2,1)}), bf16[32,32,256]{2,1,0:T(8,128)(2,1)S(1)}, u32[]{:S(2)}, u32[]{:S(2)}) async-start(bf16[32,32,256]{2,1,0:T(8,128)(2,1)} %sum_b.1), calls=%async_computation.6 | async-start | bytes 1048576 | tf_op jit(solution)/shard_map/all_to_all | solution.py:516
  126.8 6.7 %collective-permute-start = (bf16[4,256,256]{2,1,0:T(8,128)(2,1)S(1)}, bf16[4,256,256]{2,1,0:T(8,128)(2,1)S(1)}, u32[]{:S(2)}, u32[]{:S(2)}) collective-permute-start(bf16[4,256,256]{2,1,0:T(8,128)(2,1)S(1)} %bitcast.12), channel_id=1, source_target_pairs={{0,1},{1,0},{2,3},{3,2},{4,5},{5,4},{6,7},{7,6},{8,9},{9,8},{10,11... | collective-permute-start | bytes 1572872 | tf_op jit(solution)/shard_map/ppermute | solution.py:536

commit v9 on v8

--- a/solution.py
+++ b/solution.py
@@ -1,3 +1,4 @@
+import functools
 import math
 
 import jax
@@ -156,19 +157,41 @@
     repeat_into(out, total.astype(bf16))
 
 
-def pack_kernel(tokens, weight, values, gate, cot, out):
-    x = tokens[...]
-    projected = mm(x, weight[...], NN).T.astype(bf16)
+def fetch(sources, targets, sems):
+    copies = [
+        pltpu.make_async_copy(source, target, sems.at[i])
+        for i, (source, target) in enumerate(zip(sources, targets))
+    ]
+    for copy in copies:
+        copy.start()
+    return copies
+
+
+def pack_kernel(*refs):
+    out, gate, cot, values, weight, tokens, sems = refs[5:]
+    far_tokens, far_weight, far_values, far_gate, far_cot = refs[:5]
+    copies = fetch(
+        (far_gate, far_cot, far_values, far_weight, far_tokens),
+        (gate, cot, values, weight, tokens),
+        sems,
+    )
+    for copy in copies[:3]:
+        copy.wait()
     g = gate[...].astype(f32)
     v = values[...].T
     up = (cot[...].astype(f32) * (g * jax.nn.sigmoid(g))).astype(bf16).T
+    for h in range(H):
+        cols = slice(DV * h, DV * (h + 1))
+        out[h, AT_V : AT_V + DV] = v[cols]
+        out[h, AT_G : AT_G + DV] = up[cols]
+    for copy in copies[3:]:
+        copy.wait()
+    x = tokens[...]
+    projected = mm(x, weight[...], NN).T.astype(bf16)
     width = H * F
     for h in range(H):
         out[h, AT_P : AT_P + F] = projected[F * h : F * (h + 1)]
         out[h, AT_P + F : ROWS] = projected[width + F * h : width + F * (h + 1)]
-        cols = slice(DV * h, DV * (h + 1))
-        out[h, AT_V : AT_V + DV] = v[cols]
-        out[h, AT_G : AT_G + DV] = up[cols]
         for i in range(x.shape[1] // H // TOK):
             start = x.shape[1] // H * h + TOK * i
             out[h, TOK * i : TOK * (i + 1)] = x[:, start : start + TOK]
@@ -201,8 +224,12 @@
     repeat_into(out, pack_state(total, extra))
 
 
-def main_kernel(place, data, states, conv, out, saved, parts, edges, sent, columns):
+def main_kernel(
+    place, data, states, conv, far_out, far_saved, far_parts, far_edges, sent,
+    columns, out, saved, parts, edges, sems,
+):
     here = place[0]
+    copies = []
     taps = head_taps(conv, columns, place[1])
     length = TOK * WIDE
     total = jnp.zeros((SENT, 2 * DV), f32)
@@ -220,6 +247,7 @@
     edges[0:F] = pltpu.roll(first_q, shift - 4, 1)
     edges[F : 2 * F] = pltpu.roll(first_k, shift, 1)
     edges[2 * F :] = pltpu.roll(first_v, shift, 1)
+    copies += fetch((edges,), (far_edges,), sems.at[pl.ds(0, 1)])
     tile = states[jnp.maximum(here - 1, 0), FEAT // 2 : SENT].astype(f32)
     tile = tile * (here > 0).astype(f32)
     before = jnp.concatenate(
@@ -275,14 +303,26 @@
         saved[c, 0:F] = g_query
         saved[c, F : 2 * F] = g_key
         saved[c, 3 * F :] = g_value
+        some = slice(WIDE * c, WIDE * (c + 1))
+        copies += fetch(
+            (out.at[some], saved.at[c], parts.at[c]),
+            (far_out.at[some], far_saved.at[c], far_parts.at[c]),
+            sems.at[pl.ds(1 + 3 * c, 3)],
+        )
     repeat_into(sent, pack_state(whole, extra))
+    for copy in copies:
+        copy.wait()
 
 
 def back_kernel(
-    place, states, done, saved, parts, edges, conv, far, out, columns, data, sem
+    place, states, conv, far_done, far_saved, far_parts, far_edges, far, out,
+    columns, edges, data, done, saved, parts, sems,
 ):
-    fetch = pltpu.make_async_copy(far.at[:, AT_V : AT_V + DV], data, sem)
-    fetch.start()
+    copies = fetch(
+        (far_edges, far.at[:, AT_V : AT_V + DV], far_saved, far_parts, far_done),
+        (edges, data, saved, parts, done),
+        sems,
+    )
     here = place[0]
     taps = head_taps(conv, columns, place[1])
     count = states.shape[0]
@@ -291,6 +331,7 @@
         total = total + states[b].astype(f32) * (b > here).astype(f32)
     state = unpack_state(total)
     tile = states[jnp.minimum(here + 1, count - 1), FEAT // 2 : SENT].astype(f32)
+    copies[0].wait()
     edge = edges[...]
     edge_v = wide_values(edge[2 * F :].astype(bf16))
     split_state = halves(state)
@@ -309,7 +350,8 @@
     after = jnp.concatenate(
         [tile[:, SPARE : SPARE + 2], features_back(edge[F : 2 * F], g_feat)[:, 0:2]], 0
     ) * (here + 1 < count).astype(f32)
-    fetch.wait()
+    for copy in copies[1:]:
+        copy.wait()
     for c in reversed(range(H // WIDE)):
         k = saved[c, 2 * F : 3 * F]
         v = wide_values(rows_of(data, c, 0, DV))
@@ -345,13 +387,13 @@
 
 
 def weight_kernel(place, grads, far, out, own, data, sem):
-    fetch = pltpu.make_async_copy(far.at[:, 0:HID], data, sem)
-    fetch.start()
+    copy = pltpu.make_async_copy(far.at[:, 0:HID], data, sem)
+    copy.start()
     own[...] = stacked(grads, place[1])
     total = jnp.concatenate([stacked(grads, b) for b in range(H)], 1).T
     count, rows = out.shape[:2]
     parts = count * rows // TOK
-    fetch.wait()
+    copy.wait()
     for i in range(parts):
         at = TOK * i
         tokens = jnp.concatenate([data[b, at : at + TOK] for b in range(H)], 0)
@@ -360,16 +402,14 @@
             out[i * (count // parts) + j] = result[rows * j : rows * (j + 1)]
 
 
-def join_kernel(place, mine, theirs, out, sems):
-    core = place[1] % 2
-    copies = []
-    for h in range(H // 2):
-        for i, (part, at) in enumerate(((mine, core), (theirs, 1 - core))):
-            copies.append(
-                pltpu.make_async_copy(part.at[h], out.at[2 * h + at], sems.at[2 * h + i])
-            )
-    for copy in copies:
-        copy.start()
+def join_kernel(place, part, *refs, flip):
+    out, sems = refs[-2:]
+    at = (place[1] + flip) % 2
+    copies = fetch(
+        [part.at[h] for h in range(H // 2)],
+        [out.at[2 * h + at] for h in range(H // 2)],
+        sems,
+    )
     for copy in copies:
         copy.wait()
 
@@ -397,12 +437,15 @@
     return pltpu.with_memory_space_constraint(x, pltpu.VMEM)
 
 
-def call(kernel, name, out_shape, *args, scalars=0, lazy=0, far=False, results=pltpu.VMEM, scratch=()):
+def call(kernel, name, out_shape, *args, scalars=0, lazy=0, far=False, results=pltpu.VMEM, scratch=(), alias={}):
     whole = pl.BlockSpec(memory_space=pltpu.VMEM)
     specs = [pl.BlockSpec(memory_space=pltpu.SMEM)] * scalars
     specs += [whole] * (len(args) - scalars - lazy)
     specs += [pl.BlockSpec(memory_space=pl.ANY)] * lazy
-    outs = jax.tree.map(lambda s: pl.BlockSpec(memory_space=results), out_shape)
+    if isinstance(results, tuple):
+        outs = tuple(pl.BlockSpec(memory_space=r) for r in results)
+    else:
+        outs = jax.tree.map(lambda s: pl.BlockSpec(memory_space=results), out_shape)
     if not far:
         out_shape = jax.tree.map(lambda s: pltpu.VMEM(s.shape, s.dtype), out_shape)
     return pl.pallas_call(
@@ -412,6 +455,7 @@
         in_specs=specs,
         out_specs=outs,
         scratch_shapes=scratch,
+        input_output_aliases=alias,
     )(*args)
 
 
@@ -444,6 +488,13 @@
         values[0],
         gate_in[0],
         cotangent[0],
+        lazy=5,
+        scratch=(
+            *(pltpu.VMEM((TOK, H * DV), bf16),) * 3,
+            pltpu.VMEM(qk_weight.shape, bf16),
+            pltpu.VMEM(tokens.shape, bf16),
+            pltpu.SemaphoreType.DMA((5,)),
+        ),
     )
     data = lax.all_to_all(packed, GROUP, 0, 0, tiled=True)
     own = call(
@@ -472,7 +523,15 @@
         conv_weight,
         scalars=1,
         far=True,
-        scratch=taps,
+        results=(pl.ANY,) * 4 + (pltpu.VMEM,),
+        scratch=taps
+        + (
+            pltpu.VMEM((H, DV, TOK), bf16),
+            pltpu.VMEM((chunks, 3 * F + DV, width), f32),
+            pltpu.VMEM((chunks, FEAT, 2 * DV), bf16),
+            pltpu.VMEM((2 * F + DV, 2 * DV), f32),
+            pltpu.SemaphoreType.DMA((1 + 3 * chunks,)),
+        ),
     )
     back = call(
         back_kernel,
@@ -480,15 +539,23 @@
         shape((H, FIRST + 2 * DV, TOK), bf16),
         place,
         swap(sent, SUPER),
+        conv_weight,
         done,
         saved,
         parts,
         edges,
-        conv_weight,
         data,
         scalars=1,
-        lazy=1,
-        scratch=taps + window(DV),
+        lazy=5,
+        scratch=taps
+        + (
+            pltpu.VMEM((2 * F + DV, 2 * DV), f32),
+            pltpu.VMEM((H, DV, TOK), bf16),
+            pltpu.VMEM((H, DV, TOK), bf16),
+            pltpu.VMEM((chunks, 3 * F + DV, width), f32),
+            pltpu.VMEM((chunks, FEAT, 2 * DV), bf16),
+            pltpu.SemaphoreType.DMA((5,)),
+        ),
     )
     back = swap(back, GROUP)
     partial, own_grad = call(
@@ -534,19 +601,25 @@
     )
     mine, output, grad_hidden = lax.optimization_barrier((mine, output, grad_hidden))
     theirs = lax.ppermute(mine, "core", [(0, 1), (1, 0)])
-    grad_qk_weight = call(
-        join_kernel,
-        "join",
-        shape((H, model // H, 2 * H * F), bf16),
-        place,
-        near(mine),
-        near(theirs),
-        scalars=1,
-        lazy=2,
-        far=True,
-        results=pl.ANY,
-        scratch=(pltpu.SemaphoreType.DMA((H,)),),
-    ).reshape(model, 2 * H * F)
+    joined = ()
+    for flip, part in enumerate((mine, theirs)):
+        joined = (
+            call(
+                functools.partial(join_kernel, flip=flip),
+                f"join_{flip}",
+                shape((H, model // H, 2 * H * F), bf16),
+                place,
+                near(part),
+                *joined,
+                scalars=1,
+                lazy=1 + flip,
+                far=True,
+                results=pl.ANY,
+                scratch=(pltpu.SemaphoreType.DMA((H // 2,)),),
+                alias={2: 0} if flip else {},
+            ),
+        )
+    grad_qk_weight = joined[0].reshape(model, 2 * H * F)
     return output[None], grad_hidden[None], grad_values[None], grad_gate[None], grad_qk_weight
 
 

time: 136 us -> 136 us (level)
  waiting for transfers between devices: 17.2 us -> 15.7 us
    ppermute x1, waiting for transfers between devices: 1.54 us -> 0.04 us  [body(): theirs = lax.ppermute(mine, 'core', [(0, 1), (1, 0)])]
    pallas_call x10 -> x11, Pallas kernels: 21.6 us -> 22.7 us  [call(): pl.pallas_call(kernel, name=name, out_shape=out_shape, in_specs=specs, ou...]
  transfers between devices with their start and end apart: 3 -> 3, of which waited for: 3 -> 2; matrix products, arithmetic and copies ran while one was open for 0% -> 0% of each run, Pallas kernels for 3% -> 4%
where the time goes in v9:
time: 136 us; the launch traced here: 135 us
  blocking collectives  78.7 us (58%)
  Pallas kernels  22.7 us (17%)
  starting transfers between devices  16.3 us (12%)
  waiting for transfers between devices  15.7 us (12%)
    all_to_all x5, blocking collectives, swap(): return near(lax.all_to_all(x, axis, 0, 0, tiled=True))  78.7 us
    pallas_call x11, Pallas kernels, call(): pl.pallas_call(kernel, name=name, out_shape=out_shape, in_specs=specs, ou...  22.7 us
    all_to_all x1, waiting for transfers between devices, body(): data = lax.all_to_all(packed, GROUP, 0, 0, tiled=True)  11.1 us
    all_to_all x1, starting transfers between devices, body(): data = lax.all_to_all(packed, GROUP, 0, 0, tiled=True)  7.15 us
    ppermute x1, starting transfers between devices, body(): theirs = lax.ppermute(mine, 'core', [(0, 1), (1, 0)])  5.14 us
    all_to_all x1, waiting for transfers between devices, body(): mine = lax.all_to_all(summed, ('h',) + OTHER, 0, 0, tiled=True)  4.59 us
    all_to_all x1, starting transfers between devices, body(): mine = lax.all_to_all(summed, ('h',) + OTHER, 0, 0, tiled=True)  4.05 us
  transfers between devices with their start and end apart: 3, of which 2 were waited for; matrix products, arithmetic and copies ran while one was open for 0% of the time, Pallas kernels for 4%

profile of v9, /device:TPU:1, one launch (start us, length us, event | category | flops | bytes accessed | tf_op | source)
XLA Modules:
  0.0 134.8 jit_solution(17481625416290589001)
XLA Ops:
  0.6 2.9 %pack.1 = bf16[8,416,128]{2,1,0:T(8,128)(2,1)} custom-call(bf16[128,2048]{1,0:T(8,128)(2,1)} %bitcast.16, bf16[2048,256]{1,0:T(8,128)(2,1)} %weight.3, bf16[128,512]{1,0:T(8,128)(2,1)} %bitcast.21, bf16[128,512]{1,0:T(8,128)(2,1)} %bitcast.17, bf16[128,512]{1,0:T(8,128)(2,1)} %bitcast.19), custom_call_target="tpu_custom_call" | custom-call | tf_op jit(solution)/shard_map/pack/pallas_call | solution.py:451
  3.5 7.2 %all-to-all-start = ((bf16[8,416,128]{2,1,0:T(8,128)(2,1)}), bf16[8,416,128]{2,1,0:T(8,128)(2,1)S(1)}, u32[]{:S(2)}, u32[]{:S(2)}) async-start(bf16[8,416,128]{2,1,0:T(8,128)(2,1)} %pack.1), calls=%async_computation | async-start | bytes 1703936 | tf_op jit(solution)/shard_map/all_to_all | solution.py:499
  10.7 0.7 pad_add_fusion.place
  11.3 11.1 %all-to-all-done.data.far = bf16[8,416,128]{2,1,0:T(8,128)(2,1)S(1)} async-done(((bf16[8,416,128]{2,1,0:T(8,128)(2,1)}), bf16[8,416,128]{2,1,0:T(8,128)(2,1)S(1)}, u32[]{:S(2)}, u32[]{:S(2)}) %all-to-all-start) | async-done | bytes 852000 | tf_op jit(solution)/shard_map/all_to_all | solution.py:499
  22.4 0.0 copy-start
  22.4 1.4 %state.1 = bf16[16,96,128]{2,1,0:T(8,128)(2,1)S(1)} custom-call(s32[2]{0:T(128)} %pad_add_fusion.place, bf16[8,416,128]{2,1,0:T(8,128)(2,1)S(1)} %all-to-all-done.data.far, f32[3,256]{1,0:T(4,128)} %conv.5), custom_call_target="tpu_custom_call" | custom-call | tf_op jit(solution)/shard_map/state/pallas_call | solution.py:451
  23.8 23.3 %all_to_all.35.states = bf16[16,96,128]{2,1,0:T(8,128)(2,1)S(1)} all-to-all(bf16[16,96,128]{2,1,0:T(8,128)(2,1)S(1)} %state.1), channel_id=1, replica_groups=mesh['dp'=2,'y'=4,'z'=4,'h'=4,'core'=2] {'y','z'}, dimensions={0} | all-to-all | bytes 786432 | tf_op jit(solution)/shard_map/all_to_all | solution.py:471
  47.1 0.0 copy-done
  47.1 5.6 %main.1 = (bf16[8,64,128]{2,1,0:T(8,128)(2,1)}, f32[4,112,256]{2,1,0:T(8,128)}, bf16[4,160,128]{2,1,0:T(8,128)(2,1)}, f32[96,128]{1,0:T(8,128)}, bf16[16,96,128]{2,1,0:T(8,128)(2,1)S(1)}) custom-call(s32[2]{0:T(128)} %pad_add_fusion.place, bf16[8,416,128]{2,1,0:T(8,128)(2,1)S(1)} %all-to-all-done.data.far, bf16[16,96,128]{2,1,0:T(8,128)(2,1)S(1)} %all_to_all.35.states, ...), custom_call_target="tpu_custom_call" | custom-call | tf_op jit(solution)/shard_map/main/pallas_call | solution.py:451
  52.7 15.1 %all_to_all.36.states = bf16[16,96,128]{2,1,0:T(8,128)(2,1)S(1)} all-to-all(bf16[16,96,128]{2,1,0:T(8,128)(2,1)S(1)} %get-tuple-element.18), channel_id=1, replica_groups=mesh['dp'=2,'y'=4,'z'=4,'h'=4,'core'=2] {'y','z'}, dimensions={0} | all-to-all | bytes 786432 | tf_op jit(solution)/shard_map/all_to_all | solution.py:471
  67.8 2.5 %back.1 = bf16[8,384,128]{2,1,0:T(8,128)(2,1)S(1)} custom-call(s32[2]{0:T(128)} %pad_add_fusion.place, bf16[16,96,128]{2,1,0:T(8,128)(2,1)S(1)} %all_to_all.36.states, f32[3,256]{1,0:T(4,128)} %conv.5, bf16[8,64,128]{2,1,0:T(8,128)(2,1)} %get-tuple-element.19.far_done, f32[4,112,256]{2,1,0:T(8,128)} %get-tuple-element.20.far_saved, ...), custom_call_target="tpu_custom_call" | custom-call | tf_op jit(solution)/shard_map/back/pallas_call | solution.py:451
  70.3 22.1 %all_to_all.37.grads.data = bf16[8,384,128]{2,1,0:T(8,128)(2,1)S(1)} all-to-all(bf16[8,384,128]{2,1,0:T(8,128)(2,1)S(1)} %back.1), channel_id=1, replica_groups=mesh['dp'=2,'y'=4,'z'=4,'h'=4,'core'=2] {'h','core'}, dimensions={0} | all-to-all | bytes 1572864 | tf_op jit(solution)/shard_map/all_to_all | solution.py:471
  92.4 2.2 %weight.2 = (bf16[8,32,256]{2,1,0:T(8,128)(2,1)S(1)}, bf16[256,128]{1,0:T(8,128)(2,1)S(1)}) custom-call(s32[2]{0:T(128)} %pad_add_fusion.place, bf16[8,384,128]{2,1,0:T(8,128)(2,1)S(1)} %all_to_all.37.grads.data, bf16[8,416,128]{2,1,0:T(8,128)(2,1)} %copy-done), custom_call_target="tpu_custom_call" | custom-call | tf_op jit(solution)/shard_map/weight/pallas_call | solution.py:451
  94.6 7.8 %all_to_all.38.data = bf16[8,32,256]{2,1,0:T(8,128)(2,1)S(1)} all-to-all(bf16[8,32,256]{2,1,0:T(8,128)(2,1)S(1)} %get-tuple-element.23), channel_id=1, replica_groups=mesh['dp'=2,'y'=4,'z'=4,'h'=4,'core'=2] {'dp','y'}, dimensions={0} | all-to-all | bytes 262144 | tf_op jit(solution)/shard_map/all_to_all | solution.py:471
  102.4 10.3 %all_to_all.39.data = bf16[4,32,256]{2,1,0:T(8,128)(2,1)S(1)} all-to-all(bf16[4,32,256]{2,1,0:T(8,128)(2,1)S(1)} %sum_a.1), channel_id=1, replica_groups=mesh['dp'=2,'y'=4,'z'=4,'h'=4,'core'=2] {'z'}, dimensions={0} | all-to-all | bytes 131072 | tf_op jit(solution)/shard_map/all_to_all | solution.py:471
  112.8 0.9 sum_b.1
  113.6 4.0 %all-to-all-start.6 = ((bf16[32,32,256]{2,1,0:T(8,128)(2,1)}), bf16[32,32,256]{2,1,0:T(8,128)(2,1)S(1)}, u32[]{:S(2)}, u32[]{:S(2)}) async-start(bf16[32,32,256]{2,1,0:T(8,128)(2,1)} %sum_b.1), calls=%async_computation.6 | async-start | bytes 1048576 | tf_op jit(solution)/shard_map/all_to_all | solution.py:583
  117.7 2.5 %hidden.1 = bf16[128,2048]{1,0:T(8,128)(2,1)} custom-call(bf16[256,128]{1,0:T(8,128)(2,1)S(1)} %get-tuple-element.25.own, bf16[2048,256]{1,0:T(8,128)(2,1)} %weight.3), custom_call_target="tpu_custom_call" | custom-call | tf_op jit(solution)/shard_map/hidden/pallas_call | solution.py:451
  120.2 1.9 %unpack.1 = (bf16[128,512]{1,0:T(8,128)(2,1)}, bf16[128,512]{1,0:T(8,128)(2,1)}, bf16[128,512]{1,0:T(8,128)(2,1)}) custom-call(bf16[8,384,128]{2,1,0:T(8,128)(2,1)S(1)} %all_to_all.37.grads.data, bf16[128,512]{1,0:T(8,128)(2,1)} %bitcast.18, bf16[128,512]{1,0:T(8,128)(2,1)} %bitcast.20), custom_call_target="tpu_custom_call" | custom-call | tf_op jit(solution)/shard_map/unpack/pallas_call | solution.py:451
  122.0 4.6 %all-to-all-done.6 = bf16[32,32,256]{2,1,0:T(8,128)(2,1)S(1)} async-done(((bf16[32,32,256]{2,1,0:T(8,128)(2,1)}), bf16[32,32,256]{2,1,0:T(8,128)(2,1)S(1)}, u32[]{:S(2)}, u32[]{:S(2)}) %all-to-all-start.6) | async-done | bytes 524320 | tf_op jit(solution)/shard_map/all_to_all | solution.py:583
  126.6 5.1 %collective-permute-start = (bf16[4,256,256]{2,1,0:T(8,128)(2,1)S(1)}, bf16[4,256,256]{2,1,0:T(8,128)(2,1)S(1)}, u32[]{:S(2)}, u32[]{:S(2)}) collective-permute-start(bf16[4,256,256]{2,1,0:T(8,128)(2,1)S(1)} %bitcast.12), channel_id=1, source_target_pairs={{0,1},{1,0},{2,3},{3,2},{4,5},{5,4},{6,7},{7,6},{8,9},{9,8},{10,11... | collective-permute-start | bytes 1572872 | tf_op jit(solution)/shard_map/ppermute | solution.py:603
  131.8 1.5 %join_0.1.refs_0_ = bf16[8,256,256]{2,1,0:T(8,128)(2,1)} custom-call(s32[2]{0:T(128)} %pad_add_fusion.place, bf16[4,256,256]{2,1,0:T(8,128)(2,1)S(1)} %bitcast.13), custom_call_target="tpu_custom_call" | custom-call | tf_op jit(solution)/shard_map/join_0/pallas_call | solution.py:451
  133.3 0.0 collective-permute-done.part
  133.3 1.5 %join_1.1 = bf16[8,256,256]{2,1,0:T(8,128)(2,1)} custom-call(s32[2]{0:T(128)} %pad_add_fusion.place, bf16[4,256,256]{2,1,0:T(8,128)(2,1)S(1)} %collective-permute-done.part, bf16[8,256,256]{2,1,0:T(8,128)(2,1)} %join_0.1.refs_0_), custom_call_target="tpu_custom_call", output_to_operand_aliasing={{}: (2, {})} | custom-call | tf_op jit(solution)/shard_map/join_1/pallas_call | solution.py:451
  (1 shorter events, 0.0 us)
Async XLA Ops:
  3.5 18.9 %all-to-all-start = ((bf16[8,416,128]{2,1,0:T(8,128)(2,1)}), bf16[8,416,128]{2,1,0:T(8,128)(2,1)S(1)}, u32[]{:S(2)}, u32[]{:S(2)}) async-start(bf16[8,416,128]{2,1,0:T(8,128)(2,1)} %pack.1), calls=%async_computation | async-start | bytes 1703936 | tf_op jit(solution)/shard_map/all_to_all | solution.py:499
  22.4 24.7 %copy-start = (bf16[8,416,128]{2,1,0:T(8,128)(2,1)}, bf16[8,416,128]{2,1,0:T(8,128)(2,1)S(1)}, u32[]{:S(2)}) copy-start(bf16[8,416,128]{2,1,0:T(8,128)(2,1)S(1)} %all-to-all-done.data.far) | copy-start | bytes 2555908
  113.6 13.0 %all-to-all-start.6 = ((bf16[32,32,256]{2,1,0:T(8,128)(2,1)}), bf16[32,32,256]{2,1,0:T(8,128)(2,1)S(1)}, u32[]{:S(2)}, u32[]{:S(2)}) async-start(bf16[32,32,256]{2,1,0:T(8,128)(2,1)} %sum_b.1), calls=%async_computation.6 | async-start | bytes 1048576 | tf_op jit(solution)/shard_map/all_to_all | solution.py:583
  126.6 6.7 %collective-permute-start = (bf16[4,256,256]{2,1,0:T(8,128)(2,1)S(1)}, bf16[4,256,256]{2,1,0:T(8,128)(2,1)S(1)}, u32[]{:S(2)}, u32[]{:S(2)}) collective-permute-start(bf16[4,256,256]{2,1,0:T(8,128)(2,1)S(1)} %bitcast.12), channel_id=1, source_target_pairs={{0,1},{1,0},{2,3},{3,2},{4,5},{5,4},{6,7},{7,6},{8,9},{9,8},{10,11... | collective-permute-start | bytes 1572872 | tf_op jit(solution)/shard_map/ppermute | solution.py:603

commit v10 on v9

--- a/solution.py
+++ b/solution.py
@@ -170,9 +170,16 @@
 def pack_kernel(*refs):
     out, gate, cot, values, weight, tokens, sems = refs[5:]
     far_tokens, far_weight, far_values, far_gate, far_cot = refs[:5]
+    w_rows, t_rows = (
+        [pl.ds(n // 4 * i, n // 4) for i in range(4)] for n in (weight.shape[0], TOK)
+    )
     copies = fetch(
-        (far_gate, far_cot, far_values, far_weight, far_tokens),
-        (gate, cot, values, weight, tokens),
+        [far_gate, far_cot, far_values]
+        + [far_weight.at[r] for r in w_rows]
+        + [far_tokens.at[r] for r in t_rows],
+        [gate, cot, values]
+        + [weight.at[r] for r in w_rows]
+        + [tokens.at[r] for r in t_rows],
         sems,
     )
     for copy in copies[:3]:
@@ -387,13 +394,15 @@
 
 
 def weight_kernel(place, grads, far, out, own, data, sem):
-    copy = pltpu.make_async_copy(far.at[:, 0:HID], data, sem)
-    copy.start()
+    copies = fetch(
+        [far.at[b, 0:HID] for b in range(H)], [data.at[b] for b in range(H)], sem
+    )
     own[...] = stacked(grads, place[1])
     total = jnp.concatenate([stacked(grads, b) for b in range(H)], 1).T
     count, rows = out.shape[:2]
     parts = count * rows // TOK
-    copy.wait()
+    for copy in copies:
+        copy.wait()
     for i in range(parts):
         at = TOK * i
         tokens = jnp.concatenate([data[b, at : at + TOK] for b in range(H)], 0)
@@ -405,9 +414,11 @@
 def join_kernel(place, part, *refs, flip):
     out, sems = refs[-2:]
     at = (place[1] + flip) % 2
+    size = part.shape[1] // 4
+    pieces = [(h, pl.ds(size * i, size)) for h in range(H // 2) for i in range(4)]
     copies = fetch(
-        [part.at[h] for h in range(H // 2)],
-        [out.at[2 * h + at] for h in range(H // 2)],
+        [part.at[h, r] for h, r in pieces],
+        [out.at[2 * h + at, r] for h, r in pieces],
         sems,
     )
     for copy in copies:
@@ -460,7 +471,7 @@
 
 
 def window(size):
-    return pltpu.VMEM((H, size, TOK), bf16), pltpu.SemaphoreType.DMA(())
+    return pltpu.VMEM((H, size, TOK), bf16), pltpu.SemaphoreType.DMA((H,))
 
 
 def shape(dims, kind):
@@ -493,7 +504,7 @@
             *(pltpu.VMEM((TOK, H * DV), bf16),) * 3,
             pltpu.VMEM(qk_weight.shape, bf16),
             pltpu.VMEM(tokens.shape, bf16),
-            pltpu.SemaphoreType.DMA((5,)),
+            pltpu.SemaphoreType.DMA((11,)),
         ),
     )
     data = lax.all_to_all(packed, GROUP, 0, 0, tiled=True)
@@ -615,7 +626,7 @@
                 lazy=1 + flip,
                 far=True,
                 results=pl.ANY,
-                scratch=(pltpu.SemaphoreType.DMA((H // 2,)),),
+                scratch=(pltpu.SemaphoreType.DMA((2 * H,)),),
                 alias={2: 0} if flip else {},
             ),
         )

time: 136 us -> 136 us (level)
  no operation moved by 1% of the time
where the time goes in v10:
time: 136 us; the launch traced here: 135 us
  blocking collectives  78.7 us (58%)
  Pallas kernels  23 us (17%)
  starting transfers between devices  16.3 us (12%)
  waiting for transfers between devices  15.7 us (12%)
    all_to_all x5, blocking collectives, swap(): return near(lax.all_to_all(x, axis, 0, 0, tiled=True))  78.7 us
    pallas_call x11, Pallas kernels, call(): pl.pallas_call(kernel, name=name, out_shape=out_shape, in_specs=specs, ou...  23 us
    all_to_all x1, waiting for transfers between devices, body(): data = lax.all_to_all(packed, GROUP, 0, 0, tiled=True)  11.1 us
    all_to_all x1, starting transfers between devices, body(): data = lax.all_to_all(packed, GROUP, 0, 0, tiled=True)  7.15 us
    ppermute x1, starting transfers between devices, body(): theirs = lax.ppermute(mine, 'core', [(0, 1), (1, 0)])  5.14 us
    all_to_all x1, waiting for transfers between devices, body(): mine = lax.all_to_all(summed, ('h',) + OTHER, 0, 0, tiled=True)  4.59 us
    all_to_all x1, starting transfers between devices, body(): mine = lax.all_to_all(summed, ('h',) + OTHER, 0, 0, tiled=True)  4.05 us
  transfers between devices with their start and end apart: 3, of which 2 were waited for; matrix products, arithmetic and copies ran while one was open for 0% of the time, Pallas kernels for 4%

profile of v10, /device:TPU:1, one launch (start us, length us, event | category | flops | bytes accessed | tf_op | source)
XLA Modules:
  0.0 135.1 jit_solution(16451300293956667362)
XLA Ops:
  0.6 2.9 %pack.1 = bf16[8,416,128]{2,1,0:T(8,128)(2,1)} custom-call(bf16[128,2048]{1,0:T(8,128)(2,1)} %bitcast.16, bf16[2048,256]{1,0:T(8,128)(2,1)} %weight.3, bf16[128,512]{1,0:T(8,128)(2,1)} %bitcast.21, bf16[128,512]{1,0:T(8,128)(2,1)} %bitcast.17, bf16[128,512]{1,0:T(8,128)(2,1)} %bitcast.19), custom_call_target="tpu_custom_call" | custom-call | tf_op jit(solution)/shard_map/pack/pallas_call | solution.py:462
  3.6 7.2 %all-to-all-start = ((bf16[8,416,128]{2,1,0:T(8,128)(2,1)}), bf16[8,416,128]{2,1,0:T(8,128)(2,1)S(1)}, u32[]{:S(2)}, u32[]{:S(2)}) async-start(bf16[8,416,128]{2,1,0:T(8,128)(2,1)} %pack.1), calls=%async_computation | async-start | bytes 1703936 | tf_op jit(solution)/shard_map/all_to_all | solution.py:510
  10.7 0.7 pad_add_fusion.place
  11.4 11.1 %all-to-all-done.data.far = bf16[8,416,128]{2,1,0:T(8,128)(2,1)S(1)} async-done(((bf16[8,416,128]{2,1,0:T(8,128)(2,1)}), bf16[8,416,128]{2,1,0:T(8,128)(2,1)S(1)}, u32[]{:S(2)}, u32[]{:S(2)}) %all-to-all-start) | async-done | bytes 852000 | tf_op jit(solution)/shard_map/all_to_all | solution.py:510
  22.4 0.0 copy-start
  22.4 1.4 %state.1 = bf16[16,96,128]{2,1,0:T(8,128)(2,1)S(1)} custom-call(s32[2]{0:T(128)} %pad_add_fusion.place, bf16[8,416,128]{2,1,0:T(8,128)(2,1)S(1)} %all-to-all-done.data.far, f32[3,256]{1,0:T(4,128)} %conv.5), custom_call_target="tpu_custom_call" | custom-call | tf_op jit(solution)/shard_map/state/pallas_call | solution.py:462
  23.8 23.3 %all_to_all.35.states = bf16[16,96,128]{2,1,0:T(8,128)(2,1)S(1)} all-to-all(bf16[16,96,128]{2,1,0:T(8,128)(2,1)S(1)} %state.1), channel_id=1, replica_groups=mesh['dp'=2,'y'=4,'z'=4,'h'=4,'core'=2] {'y','z'}, dimensions={0} | all-to-all | bytes 786432 | tf_op jit(solution)/shard_map/all_to_all | solution.py:482
  47.1 0.0 copy-done
  47.1 5.6 %main.1 = (bf16[8,64,128]{2,1,0:T(8,128)(2,1)}, f32[4,112,256]{2,1,0:T(8,128)}, bf16[4,160,128]{2,1,0:T(8,128)(2,1)}, f32[96,128]{1,0:T(8,128)}, bf16[16,96,128]{2,1,0:T(8,128)(2,1)S(1)}) custom-call(s32[2]{0:T(128)} %pad_add_fusion.place, bf16[8,416,128]{2,1,0:T(8,128)(2,1)S(1)} %all-to-all-done.data.far, bf16[16,96,128]{2,1,0:T(8,128)(2,1)S(1)} %all_to_all.35.states, ...), custom_call_target="tpu_custom_call" | custom-call | tf_op jit(solution)/shard_map/main/pallas_call | solution.py:462
  52.7 15.2 %all_to_all.36.states = bf16[16,96,128]{2,1,0:T(8,128)(2,1)S(1)} all-to-all(bf16[16,96,128]{2,1,0:T(8,128)(2,1)S(1)} %get-tuple-element.18), channel_id=1, replica_groups=mesh['dp'=2,'y'=4,'z'=4,'h'=4,'core'=2] {'y','z'}, dimensions={0} | all-to-all | bytes 786432 | tf_op jit(solution)/shard_map/all_to_all | solution.py:482
  67.8 2.5 %back.1 = bf16[8,384,128]{2,1,0:T(8,128)(2,1)S(1)} custom-call(s32[2]{0:T(128)} %pad_add_fusion.place, bf16[16,96,128]{2,1,0:T(8,128)(2,1)S(1)} %all_to_all.36.states, f32[3,256]{1,0:T(4,128)} %conv.5, bf16[8,64,128]{2,1,0:T(8,128)(2,1)} %get-tuple-element.19.far_done, f32[4,112,256]{2,1,0:T(8,128)} %get-tuple-element.20.far_saved, ...), custom_call_target="tpu_custom_call" | custom-call | tf_op jit(solution)/shard_map/back/pallas_call | solution.py:462
  70.3 22.1 %all_to_all.37.grads.data = bf16[8,384,128]{2,1,0:T(8,128)(2,1)S(1)} all-to-all(bf16[8,384,128]{2,1,0:T(8,128)(2,1)S(1)} %back.1), channel_id=1, replica_groups=mesh['dp'=2,'y'=4,'z'=4,'h'=4,'core'=2] {'h','core'}, dimensions={0} | all-to-all | bytes 1572864 | tf_op jit(solution)/shard_map/all_to_all | solution.py:482
  92.4 2.3 %weight.2 = (bf16[8,32,256]{2,1,0:T(8,128)(2,1)S(1)}, bf16[256,128]{1,0:T(8,128)(2,1)S(1)}) custom-call(s32[2]{0:T(128)} %pad_add_fusion.place, bf16[8,384,128]{2,1,0:T(8,128)(2,1)S(1)} %all_to_all.37.grads.data, bf16[8,416,128]{2,1,0:T(8,128)(2,1)} %copy-done), custom_call_target="tpu_custom_call" | custom-call | tf_op jit(solution)/shard_map/weight/pallas_call | solution.py:462
  94.7 7.8 %all_to_all.38.data = bf16[8,32,256]{2,1,0:T(8,128)(2,1)S(1)} all-to-all(bf16[8,32,256]{2,1,0:T(8,128)(2,1)S(1)} %get-tuple-element.23), channel_id=1, replica_groups=mesh['dp'=2,'y'=4,'z'=4,'h'=4,'core'=2] {'dp','y'}, dimensions={0} | all-to-all | bytes 262144 | tf_op jit(solution)/shard_map/all_to_all | solution.py:482
  102.6 10.3 %all_to_all.39.data = bf16[4,32,256]{2,1,0:T(8,128)(2,1)S(1)} all-to-all(bf16[4,32,256]{2,1,0:T(8,128)(2,1)S(1)} %sum_a.1), channel_id=1, replica_groups=mesh['dp'=2,'y'=4,'z'=4,'h'=4,'core'=2] {'z'}, dimensions={0} | all-to-all | bytes 131072 | tf_op jit(solution)/shard_map/all_to_all | solution.py:482
  112.9 0.9 sum_b.1
  113.7 4.1 %all-to-all-start.6 = ((bf16[32,32,256]{2,1,0:T(8,128)(2,1)}), bf16[32,32,256]{2,1,0:T(8,128)(2,1)S(1)}, u32[]{:S(2)}, u32[]{:S(2)}) async-start(bf16[32,32,256]{2,1,0:T(8,128)(2,1)} %sum_b.1), calls=%async_computation.6 | async-start | bytes 1048576 | tf_op jit(solution)/shard_map/all_to_all | solution.py:594
  117.8 2.5 %hidden.1 = bf16[128,2048]{1,0:T(8,128)(2,1)} custom-call(bf16[256,128]{1,0:T(8,128)(2,1)S(1)} %get-tuple-element.25.own, bf16[2048,256]{1,0:T(8,128)(2,1)} %weight.3), custom_call_target="tpu_custom_call" | custom-call | tf_op jit(solution)/shard_map/hidden/pallas_call | solution.py:462
  120.3 1.9 %unpack.1 = (bf16[128,512]{1,0:T(8,128)(2,1)}, bf16[128,512]{1,0:T(8,128)(2,1)}, bf16[128,512]{1,0:T(8,128)(2,1)}) custom-call(bf16[8,384,128]{2,1,0:T(8,128)(2,1)S(1)} %all_to_all.37.grads.data, bf16[128,512]{1,0:T(8,128)(2,1)} %bitcast.18, bf16[128,512]{1,0:T(8,128)(2,1)} %bitcast.20), custom_call_target="tpu_custom_call" | custom-call | tf_op jit(solution)/shard_map/unpack/pallas_call | solution.py:462
  122.2 4.6 %all-to-all-done.6 = bf16[32,32,256]{2,1,0:T(8,128)(2,1)S(1)} async-done(((bf16[32,32,256]{2,1,0:T(8,128)(2,1)}), bf16[32,32,256]{2,1,0:T(8,128)(2,1)S(1)}, u32[]{:S(2)}, u32[]{:S(2)}) %all-to-all-start.6) | async-done | bytes 524320 | tf_op jit(solution)/shard_map/all_to_all | solution.py:594
  126.8 5.1 %collective-permute-start = (bf16[4,256,256]{2,1,0:T(8,128)(2,1)S(1)}, bf16[4,256,256]{2,1,0:T(8,128)(2,1)S(1)}, u32[]{:S(2)}, u32[]{:S(2)}) collective-permute-start(bf16[4,256,256]{2,1,0:T(8,128)(2,1)S(1)} %bitcast.12), channel_id=1, source_target_pairs={{0,1},{1,0},{2,3},{3,2},{4,5},{5,4},{6,7},{7,6},{8,9},{9,8},{10,11... | collective-permute-start | bytes 1572872 | tf_op jit(solution)/shard_map/ppermute | solution.py:614
  131.9 1.6 %join_0.1.refs_0_ = bf16[8,256,256]{2,1,0:T(8,128)(2,1)} custom-call(s32[2]{0:T(128)} %pad_add_fusion.place, bf16[4,256,256]{2,1,0:T(8,128)(2,1)S(1)} %bitcast.13), custom_call_target="tpu_custom_call" | custom-call | tf_op jit(solution)/shard_map/join_0/pallas_call | solution.py:462
  133.5 0.0 collective-permute-done.part
  133.5 1.6 %join_1.1 = bf16[8,256,256]{2,1,0:T(8,128)(2,1)} custom-call(s32[2]{0:T(128)} %pad_add_fusion.place, bf16[4,256,256]{2,1,0:T(8,128)(2,1)S(1)} %collective-permute-done.part, bf16[8,256,256]{2,1,0:T(8,128)(2,1)} %join_0.1.refs_0_), custom_call_target="tpu_custom_call", output_to_operand_aliasing={{}: (2, {})} | custom-call | tf_op jit(solution)/shard_map/join_1/pallas_call | solution.py:462
  (1 shorter events, 0.0 us)
Async XLA Ops:
  3.6 18.9 %all-to-all-start = ((bf16[8,416,128]{2,1,0:T(8,128)(2,1)}), bf16[8,416,128]{2,1,0:T(8,128)(2,1)S(1)}, u32[]{:S(2)}, u32[]{:S(2)}) async-start(bf16[8,416,128]{2,1,0:T(8,128)(2,1)} %pack.1), calls=%async_computation | async-start | bytes 1703936 | tf_op jit(solution)/shard_map/all_to_all | solution.py:510
  22.4 24.7 %copy-start = (bf16[8,416,128]{2,1,0:T(8,128)(2,1)}, bf16[8,416,128]{2,1,0:T(8,128)(2,1)S(1)}, u32[]{:S(2)}) copy-start(bf16[8,416,128]{2,1,0:T(8,128)(2,1)S(1)} %all-to-all-done.data.far) | copy-start | bytes 2555908
  113.7 13.0 %all-to-all-start.6 = ((bf16[32,32,256]{2,1,0:T(8,128)(2,1)}), bf16[32,32,256]{2,1,0:T(8,128)(2,1)S(1)}, u32[]{:S(2)}, u32[]{:S(2)}) async-start(bf16[32,32,256]{2,1,0:T(8,128)(2,1)} %sum_b.1), calls=%async_computation.6 | async-start | bytes 1048576 | tf_op jit(solution)/shard_map/all_to_all | solution.py:594
  126.8 6.7 %collective-permute-start = (bf16[4,256,256]{2,1,0:T(8,128)(2,1)S(1)}, bf16[4,256,256]{2,1,0:T(8,128)(2,1)S(1)}, u32[]{:S(2)}, u32[]{:S(2)}) collective-permute-start(bf16[4,256,256]{2,1,0:T(8,128)(2,1)S(1)} %bitcast.12), channel_id=1, source_target_pairs={{0,1},{1,0},{2,3},{3,2},{4,5},{5,4},{6,7},{7,6},{8,9},{9,8},{10,11... | collective-permute-start | bytes 1572872 | tf_op jit(solution)/shard_map/ppermute | solution.py:614

commit v11 on v9

--- a/solution.py
+++ b/solution.py
@@ -208,9 +208,9 @@
             token = lax.broadcasted_iota(jnp.int32, feat.shape, 1)
             feat = jnp.where(token < KCONV - 1, 0.0, feat)
         before = raw[:, -2:]
-        high, low = halves(feat)
+        feat = feat.astype(bf16)
         v = wide_values(rows_of(data, c, AT_V, DV))
-        total = total + (mm(high, v, NT) + mm(low, v, NT))
+        total = total + mm(feat, v, NT)
     first, last = data[0, AT_P:ROWS], data[H - 1, AT_P:ROWS]
     begin = data[0, AT_V : AT_V + DV]
     extra = []
@@ -283,7 +283,7 @@
         grads = halves(wide)
         g_weights = mm(v, grads[0], TN) + mm(v, grads[1], TN)
         g_scores = jnp.where(causal, g_weights * near_one, 0.0).astype(bf16)
-        g_local = (mm(kh, g_scores, NN) + mm(kl, g_scores, NN)) * F**-0.5
+        g_local = mm(kh, g_scores, NN) * F**-0.5
         g_query = g_local + features_back(q, mm(held, grads[0], NN))
         if c == 0:
             extra = [g_query[:, 0:1], g_query[:, 1:2]]
@@ -291,8 +291,8 @@
                 column = wide[F * j : F * (j + 1), 0:1]
                 high = column.astype(bf16)
                 extra += [high, column - high.astype(f32)]
-        g_key = mm(qh, g_scores, NT) + mm(ql, g_scores, NT)
-        g_value = mm(grads[0][:DV], weights, NT) + mm(grads[1][:DV], weights, NT)
+        g_key = mm(qh, g_scores, NT)
+        g_value = mm(grads[0][:DV], weights, NT)
         part = mm(q_feat, grads[0], NT)
         whole = whole + part
         parts[c] = part.astype(bf16)

time: 136 us -> 135 us (level)
  no operation moved by 1% of the time
where the time goes in v11:
time: 135 us; the launch traced here: 134 us
  blocking collectives  78.7 us (58%)
  Pallas kernels  22.2 us (16%)
  starting transfers between devices  16.3 us (12%)
  waiting for transfers between devices  15.7 us (12%)
    all_to_all x5, blocking collectives, swap(): return near(lax.all_to_all(x, axis, 0, 0, tiled=True))  78.7 us
    pallas_call x11, Pallas kernels, call(): pl.pallas_call(kernel, name=name, out_shape=out_shape, in_specs=specs, ou...  22.2 us
    all_to_all x1, waiting for transfers between devices, body(): data = lax.all_to_all(packed, GROUP, 0, 0, tiled=True)  11.1 us
    all_to_all x1, starting transfers between devices, body(): data = lax.all_to_all(packed, GROUP, 0, 0, tiled=True)  7.15 us
    ppermute x1, starting transfers between devices, body(): theirs = lax.ppermute(mine, 'core', [(0, 1), (1, 0)])  5.14 us
    all_to_all x1, waiting for transfers between devices, body(): mine = lax.all_to_all(summed, ('h',) + OTHER, 0, 0, tiled=True)  4.59 us
    all_to_all x1, starting transfers between devices, body(): mine = lax.all_to_all(summed, ('h',) + OTHER, 0, 0, tiled=True)  4.05 us
  transfers between devices with their start and end apart: 3, of which 2 were waited for; matrix products, arithmetic and copies ran while one was open for 0% of the time, Pallas kernels for 4%

profile of v11, /device:TPU:1, one launch (start us, length us, event | category | flops | bytes accessed | tf_op | source)
XLA Modules:
  0.0 134.3 jit_solution(15224398381316682143)
XLA Ops:
  0.6 2.9 %pack.1 = bf16[8,416,128]{2,1,0:T(8,128)(2,1)} custom-call(bf16[128,2048]{1,0:T(8,128)(2,1)} %bitcast.16, bf16[2048,256]{1,0:T(8,128)(2,1)} %weight.3, bf16[128,512]{1,0:T(8,128)(2,1)} %bitcast.21, bf16[128,512]{1,0:T(8,128)(2,1)} %bitcast.17, bf16[128,512]{1,0:T(8,128)(2,1)} %bitcast.19), custom_call_target="tpu_custom_call" | custom-call | tf_op jit(solution)/shard_map/pack/pallas_call | solution.py:451
  3.5 7.2 %all-to-all-start = ((bf16[8,416,128]{2,1,0:T(8,128)(2,1)}), bf16[8,416,128]{2,1,0:T(8,128)(2,1)S(1)}, u32[]{:S(2)}, u32[]{:S(2)}) async-start(bf16[8,416,128]{2,1,0:T(8,128)(2,1)} %pack.1), calls=%async_computation | async-start | bytes 1703936 | tf_op jit(solution)/shard_map/all_to_all | solution.py:499
  10.7 0.7 pad_add_fusion.place
  11.3 11.1 %all-to-all-done.data.far = bf16[8,416,128]{2,1,0:T(8,128)(2,1)S(1)} async-done(((bf16[8,416,128]{2,1,0:T(8,128)(2,1)}), bf16[8,416,128]{2,1,0:T(8,128)(2,1)S(1)}, u32[]{:S(2)}, u32[]{:S(2)}) %all-to-all-start) | async-done | bytes 852000 | tf_op jit(solution)/shard_map/all_to_all | solution.py:499
  22.4 0.0 copy-start
  22.4 1.3 state.1
  23.7 23.3 %all_to_all.35.states = bf16[16,96,128]{2,1,0:T(8,128)(2,1)S(1)} all-to-all(bf16[16,96,128]{2,1,0:T(8,128)(2,1)S(1)} %state.1), channel_id=1, replica_groups=mesh['dp'=2,'y'=4,'z'=4,'h'=4,'core'=2] {'y','z'}, dimensions={0} | all-to-all | bytes 786432 | tf_op jit(solution)/shard_map/all_to_all | solution.py:471
  47.0 0.0 copy-done
  47.0 5.2 %main.1 = (bf16[8,64,128]{2,1,0:T(8,128)(2,1)}, f32[4,112,256]{2,1,0:T(8,128)}, bf16[4,160,128]{2,1,0:T(8,128)(2,1)}, f32[96,128]{1,0:T(8,128)}, bf16[16,96,128]{2,1,0:T(8,128)(2,1)S(1)}) custom-call(s32[2]{0:T(128)} %pad_add_fusion.place, bf16[8,416,128]{2,1,0:T(8,128)(2,1)S(1)} %all-to-all-done.data.far, bf16[16,96,128]{2,1,0:T(8,128)(2,1)S(1)} %all_to_all.35.states, ...), custom_call_target="tpu_custom_call" | custom-call | tf_op jit(solution)/shard_map/main/pallas_call | solution.py:451
  52.2 15.2 %all_to_all.36.states = bf16[16,96,128]{2,1,0:T(8,128)(2,1)S(1)} all-to-all(bf16[16,96,128]{2,1,0:T(8,128)(2,1)S(1)} %get-tuple-element.18), channel_id=1, replica_groups=mesh['dp'=2,'y'=4,'z'=4,'h'=4,'core'=2] {'y','z'}, dimensions={0} | all-to-all | bytes 786432 | tf_op jit(solution)/shard_map/all_to_all | solution.py:471
  67.3 2.5 %back.1 = bf16[8,384,128]{2,1,0:T(8,128)(2,1)S(1)} custom-call(s32[2]{0:T(128)} %pad_add_fusion.place, bf16[16,96,128]{2,1,0:T(8,128)(2,1)S(1)} %all_to_all.36.states, f32[3,256]{1,0:T(4,128)} %conv.5, bf16[8,64,128]{2,1,0:T(8,128)(2,1)} %get-tuple-element.19.far_done, f32[4,112,256]{2,1,0:T(8,128)} %get-tuple-element.20.far_saved, ...), custom_call_target="tpu_custom_call" | custom-call | tf_op jit(solution)/shard_map/back/pallas_call | solution.py:451
  69.8 22.1 %all_to_all.37.grads.data = bf16[8,384,128]{2,1,0:T(8,128)(2,1)S(1)} all-to-all(bf16[8,384,128]{2,1,0:T(8,128)(2,1)S(1)} %back.1), channel_id=1, replica_groups=mesh['dp'=2,'y'=4,'z'=4,'h'=4,'core'=2] {'h','core'}, dimensions={0} | all-to-all | bytes 1572864 | tf_op jit(solution)/shard_map/all_to_all | solution.py:471
  91.9 2.2 %weight.2 = (bf16[8,32,256]{2,1,0:T(8,128)(2,1)S(1)}, bf16[256,128]{1,0:T(8,128)(2,1)S(1)}) custom-call(s32[2]{0:T(128)} %pad_add_fusion.place, bf16[8,384,128]{2,1,0:T(8,128)(2,1)S(1)} %all_to_all.37.grads.data, bf16[8,416,128]{2,1,0:T(8,128)(2,1)} %copy-done), custom_call_target="tpu_custom_call" | custom-call | tf_op jit(solution)/shard_map/weight/pallas_call | solution.py:451
  94.1 7.8 %all_to_all.38.data = bf16[8,32,256]{2,1,0:T(8,128)(2,1)S(1)} all-to-all(bf16[8,32,256]{2,1,0:T(8,128)(2,1)S(1)} %get-tuple-element.23), channel_id=1, replica_groups=mesh['dp'=2,'y'=4,'z'=4,'h'=4,'core'=2] {'dp','y'}, dimensions={0} | all-to-all | bytes 262144 | tf_op jit(solution)/shard_map/all_to_all | solution.py:471
  101.9 10.3 %all_to_all.39.data = bf16[4,32,256]{2,1,0:T(8,128)(2,1)S(1)} all-to-all(bf16[4,32,256]{2,1,0:T(8,128)(2,1)S(1)} %sum_a.1), channel_id=1, replica_groups=mesh['dp'=2,'y'=4,'z'=4,'h'=4,'core'=2] {'z'}, dimensions={0} | all-to-all | bytes 131072 | tf_op jit(solution)/shard_map/all_to_all | solution.py:471
  112.3 0.9 sum_b.1
  113.1 4.1 %all-to-all-start.6 = ((bf16[32,32,256]{2,1,0:T(8,128)(2,1)}), bf16[32,32,256]{2,1,0:T(8,128)(2,1)S(1)}, u32[]{:S(2)}, u32[]{:S(2)}) async-start(bf16[32,32,256]{2,1,0:T(8,128)(2,1)} %sum_b.1), calls=%async_computation.6 | async-start | bytes 1048576 | tf_op jit(solution)/shard_map/all_to_all | solution.py:583
  117.2 2.5 %hidden.1 = bf16[128,2048]{1,0:T(8,128)(2,1)} custom-call(bf16[256,128]{1,0:T(8,128)(2,1)S(1)} %get-tuple-element.25.own, bf16[2048,256]{1,0:T(8,128)(2,1)} %weight.3), custom_call_target="tpu_custom_call" | custom-call | tf_op jit(solution)/shard_map/hidden/pallas_call | solution.py:451
  119.7 1.9 %unpack.1 = (bf16[128,512]{1,0:T(8,128)(2,1)}, bf16[128,512]{1,0:T(8,128)(2,1)}, bf16[128,512]{1,0:T(8,128)(2,1)}) custom-call(bf16[8,384,128]{2,1,0:T(8,128)(2,1)S(1)} %all_to_all.37.grads.data, bf16[128,512]{1,0:T(8,128)(2,1)} %bitcast.18, bf16[128,512]{1,0:T(8,128)(2,1)} %bitcast.20), custom_call_target="tpu_custom_call" | custom-call | tf_op jit(solution)/shard_map/unpack/pallas_call | solution.py:451
  121.5 4.6 %all-to-all-done.6 = bf16[32,32,256]{2,1,0:T(8,128)(2,1)S(1)} async-done(((bf16[32,32,256]{2,1,0:T(8,128)(2,1)}), bf16[32,32,256]{2,1,0:T(8,128)(2,1)S(1)}, u32[]{:S(2)}, u32[]{:S(2)}) %all-to-all-start.6) | async-done | bytes 524320 | tf_op jit(solution)/shard_map/all_to_all | solution.py:583
  126.1 5.1 %collective-permute-start = (bf16[4,256,256]{2,1,0:T(8,128)(2,1)S(1)}, bf16[4,256,256]{2,1,0:T(8,128)(2,1)S(1)}, u32[]{:S(2)}, u32[]{:S(2)}) collective-permute-start(bf16[4,256,256]{2,1,0:T(8,128)(2,1)S(1)} %bitcast.12), channel_id=1, source_target_pairs={{0,1},{1,0},{2,3},{3,2},{4,5},{5,4},{6,7},{7,6},{8,9},{9,8},{10,11... | collective-permute-start | bytes 1572872 | tf_op jit(solution)/shard_map/ppermute | solution.py:603
  131.3 1.5 %join_0.1.refs_0_ = bf16[8,256,256]{2,1,0:T(8,128)(2,1)} custom-call(s32[2]{0:T(128)} %pad_add_fusion.place, bf16[4,256,256]{2,1,0:T(8,128)(2,1)S(1)} %bitcast.13), custom_call_target="tpu_custom_call" | custom-call | tf_op jit(solution)/shard_map/join_0/pallas_call | solution.py:451
  132.8 0.0 collective-permute-done.part
  132.8 1.5 %join_1.1 = bf16[8,256,256]{2,1,0:T(8,128)(2,1)} custom-call(s32[2]{0:T(128)} %pad_add_fusion.place, bf16[4,256,256]{2,1,0:T(8,128)(2,1)S(1)} %collective-permute-done.part, bf16[8,256,256]{2,1,0:T(8,128)(2,1)} %join_0.1.refs_0_), custom_call_target="tpu_custom_call", output_to_operand_aliasing={{}: (2, {})} | custom-call | tf_op jit(solution)/shard_map/join_1/pallas_call | solution.py:451
  (1 shorter events, 0.0 us)
Async XLA Ops:
  3.5 18.9 %all-to-all-start = ((bf16[8,416,128]{2,1,0:T(8,128)(2,1)}), bf16[8,416,128]{2,1,0:T(8,128)(2,1)S(1)}, u32[]{:S(2)}, u32[]{:S(2)}) async-start(bf16[8,416,128]{2,1,0:T(8,128)(2,1)} %pack.1), calls=%async_computation | async-start | bytes 1703936 | tf_op jit(solution)/shard_map/all_to_all | solution.py:499
  22.4 24.6 %copy-start = (bf16[8,416,128]{2,1,0:T(8,128)(2,1)}, bf16[8,416,128]{2,1,0:T(8,128)(2,1)S(1)}, u32[]{:S(2)}) copy-start(bf16[8,416,128]{2,1,0:T(8,128)(2,1)S(1)} %all-to-all-done.data.far) | copy-start | bytes 2555908
  113.1 13.0 %all-to-all-start.6 = ((bf16[32,32,256]{2,1,0:T(8,128)(2,1)}), bf16[32,32,256]{2,1,0:T(8,128)(2,1)S(1)}, u32[]{:S(2)}, u32[]{:S(2)}) async-start(bf16[32,32,256]{2,1,0:T(8,128)(2,1)} %sum_b.1), calls=%async_computation.6 | async-start | bytes 1048576 | tf_op jit(solution)/shard_map/all_to_all | solution.py:583
  126.1 6.7 %collective-permute-start = (bf16[4,256,256]{2,1,0:T(8,128)(2,1)S(1)}, bf16[4,256,256]{2,1,0:T(8,128)(2,1)S(1)}, u32[]{:S(2)}, u32[]{:S(2)}) collective-permute-start(bf16[4,256,256]{2,1,0:T(8,128)(2,1)S(1)} %bitcast.12), channel_id=1, source_target_pairs={{0,1},{1,0},{2,3},{3,2},{4,5},{5,4},{6,7},{7,6},{8,9},{9,8},{10,11... | collective-permute-start | bytes 1572872 | tf_op jit(solution)/shard_map/ppermute | solution.py:603
